TPU v7x, 512 devices: a whole 4x8x8 slice. The times are simulated.
512 devices in a mesh: seq: 128 (over z_hi, y, x, core), chan: 4 (over z_lo).
Axes of the slice: x: 4, y: 8, z: 8 (z_hi: 2, z_lo: 4; z = z_hi * 4 + z_lo), core: 2. Of those that a mesh axis runs over, the one named last changes fastest.
Arguments:
- residual: bfloat16 [16384, 8192], P('seq', 'chan'), may hold values from -64 to 64
- query_in: bfloat16 [16384, 8192], P('seq', 'chan'), may hold values from -6 to 6
- key_in: bfloat16 [16384, 8192], P('seq', 'chan'), may hold values from -6 to 6
- value_in: bfloat16 [16384, 8192], P('seq', 'chan'), may hold values from -6 to 6
- short_filter: float32 [3, 3, 8192], P(None, None, 'chan'), may hold values from -3.5 to 3.5
- decay_rate: float32 [16, 8192], P(None, 'chan'), may hold values from 0 to 1
- residue: float32 [16, 8192], P(None, 'chan'), may hold values from -1.5 to 1.5
- skip_gain: float32 [8192], P('chan'), may hold values from -3 to 3
- norm_gain: float32 [8192], P('chan'), may hold values from 0.1 to 1.9
Outputs:
- residual_out: bfloat16 [16384, 8192], P('seq', 'chan')
- normed: bfloat16 [16384, 8192], P('seq', 'chan')
All inputs are finite; a program needn't handle non-finite values.
Results may differ from a plain program's by a relative error of at most 0.0055.
Values may be sent and summed in bfloat16 or wider, within the bound.
No kernel may reach another device: no remote copies, remote signals or barrier semaphores. Data moves between devices by JAX's collectives and lax.ppermute only.
A program may use at most 128 MiB of HBM per device.

v0:
```python
import jax
import jax.numpy as jnp
from jax import lax
from jax.sharding import PartitionSpec as P

D = 8192


sub_block = 16
epsilon = 1e-06
highest = lax.Precision.HIGHEST


def shifted(block, axis, distance):
    devices = range(lax.axis_size(axis))
    route = [(i - distance, i) for i in devices if i - distance in devices]
    return lax.ppermute(block, axis, route)


def short_features(inputs, before, tap_weights):
    lag_rows = before.shape[0]
    token_rows = inputs.shape[0]
    extended = jnp.concatenate([before, inputs], axis=0).astype(jnp.float32)
    result = tap_weights[0][None, :] * extended[lag_rows : lag_rows + token_rows]
    for offset in range(1, lag_rows + 1):
        result = (
            result
            + tap_weights[offset][None, :]
            * extended[lag_rows - offset : lag_rows - offset + token_rows]
        )
    return result


def link_states(earlier, later):
    return (earlier[0] * later[0], later[0] * earlier[1] + later[1])


def body(
    residual, query_in, key_in, value_in, short_filter, decay_rate, residue, skip_gain, norm_gain
):
    token_rows, chan_width = residual.shape
    lag_rows = short_filter.shape[1] - 1
    tail_rows = (
        query_in[token_rows - lag_rows :],
        key_in[token_rows - lag_rows :],
        value_in[token_rows - lag_rows :],
    )
    before = shifted((tail_rows[0], tail_rows[1], tail_rows[2]), "seq", 1)
    query_side = short_features(query_in, before[0], short_filter[0])
    key_side = short_features(key_in, before[1], short_filter[1])
    value_side = short_features(value_in, before[2], short_filter[2])
    mixed = key_side * value_side
    weights = residue * jnp.sqrt(2.0 * decay_rate)
    sub_count = token_rows // sub_block
    positions = jnp.arange(sub_block, dtype=jnp.float32)
    local_taps = jnp.sum(
        weights[None] * jnp.exp(-decay_rate[None] * positions[:, None, None]), axis=1
    )
    lag_table = positions[:, None] - positions[None, :]
    one_hot = (lag_table[:, :, None] == positions[None, None, :]).astype(jnp.float32)
    toeplitz = jnp.dot(
        one_hot.reshape(sub_block * sub_block, sub_block), local_taps, precision=highest
    ).reshape(sub_block, sub_block, chan_width)
    blocks = mixed.reshape(sub_count, sub_block, chan_width)
    inside = jnp.sum(toeplitz[None, :, :, :] * blocks[:, None, :, :], axis=2)
    tail_decay = jnp.exp(-decay_rate[None] * (sub_block - 1.0 - positions)[:, None, None])
    sub_states = jnp.sum(blocks[:, :, None, :] * tail_decay[None], axis=1)
    step_decay = jnp.broadcast_to(jnp.exp(-decay_rate * sub_block)[None], sub_states.shape)
    _, running = lax.associative_scan(link_states, (step_decay, sub_states), axis=0)
    block_state = running[sub_count - 1]
    entering = jnp.concatenate([jnp.zeros_like(running[:1]), running[:-1]], axis=0)
    position = lax.axis_index("seq")
    piece = lax.all_gather(
        block_state[None].astype(jnp.bfloat16), "seq", axis=0, tiled=True
    ).astype(jnp.float32)
    members = piece.shape[0]
    sources = jnp.arange(members, dtype=jnp.int32)
    distance = position - 1 - sources
    spans = (token_rows * jnp.maximum(distance, 0)).astype(jnp.float32)
    factors = jnp.exp(-decay_rate[None] * spans[:, None, None])
    masked = jnp.where((distance >= 0)[:, None, None], factors * piece, 0.0)
    carried = jnp.zeros_like(block_state) + jnp.sum(masked, axis=0)
    sub_starts = jnp.arange(sub_count, dtype=jnp.float32) * sub_block
    entering = entering + jnp.exp(-decay_rate[None] * sub_starts[:, None, None]) * carried[None]
    readout = weights[None] * jnp.exp(-decay_rate[None] * (positions + 1.0)[:, None, None])
    across = jnp.sum(readout[None, :, :, :] * entering[:, None, :, :], axis=2)
    convolved = (inside + across).reshape(token_rows, chan_width)
    gated = query_side * (convolved + skip_gain[None, :] * mixed)
    summed = (residual.astype(jnp.float32) + gated).astype(jnp.bfloat16)
    widened = lax.optimization_barrier(summed).astype(jnp.float32)
    row_squares = lax.psum(jnp.sum(widened * widened, axis=1), "chan")
    inverse_rms = lax.rsqrt(row_squares / D + epsilon)
    normed = (widened * inverse_rms[:, None] * norm_gain[None, :]).astype(jnp.bfloat16)
    return (summed, normed)


def solution(mesh):
    in_specs = (
        P("seq", "chan"),
        P("seq", "chan"),
        P("seq", "chan"),
        P("seq", "chan"),
        P(None, None, "chan"),
        P(None, "chan"),
        P(None, "chan"),
        P("chan"),
        P("chan"),
    )
    out_specs = (P("seq", "chan"), P("seq", "chan"))
    return jax.shard_map(body, mesh=mesh, in_specs=in_specs, out_specs=out_specs, check_vma=False)
```

profile of v0, /device:TPU:1, one launch (start us, length us, event | category | flops | bytes accessed | tf_op | source)
XLA Modules:
  0.0 228.4 jit_solution(10560586186307022351)
XLA Ops:
  7.2 0.0 all-gather.2.cloned.1.call-start
  7.2 0.8 slice.156
  8.0 4.5 %collective-permute-start.1 = (bf16[2,2048]{1,0:T(2,128)(2,1)S(1)}, bf16[2,2048]{1,0:T(2,128)(2,1)S(1)}, u32[]{:S(2)}, u32[]{:S(2)}) collective-permute-start(bf16[2,2048]{1,0:T(2,128)(2,1)S(1)} %slice.156), channel_id=1, source_target_pairs={{0,4},{4,8},{8,12},{12,16},{16,20},{20,24},{24,28},{28,32},{32,36}... | collective-permute-start | bytes 24584 | tf_op jit(solution)/shard_map/ppermute | solution.py:17
  12.5 0.8 slice.163
  13.3 1.9 collective-permute-start.2
  15.2 1.0 fusion.24
  16.2 1.0 fusion.21
  17.3 2.4 %exponential_multiply_fusion = (f32[16,16,2048]{2,1,0:T(8,128)}, f32[16,2048]{1,0:T(8,128)S(1)}, f32[16,16,2048]{2,1,0:T(8,128)S(1)}) fusion(f32[16]{0:T(128)S(1)} %get-tuple-element.25, f32[16,2048]{1,0:T(8,128)S(1)} %get-tuple-element.13, f32[16,2048]{1,0:T(8,128)S(1)} %get-tuple-element.14, f32[16]{0:T(128)S(1)} %get-tuple-element.24), kind=kLoop, calls=%fused_computation.5 | loop fusion | flops 3112960 | bytes 4587648 | tf_op jit(solution)/shard_map/mul | solution.py:85
  19.7 1.0 fusion.17
  20.7 0.0 collective-permute-done.1
  20.7 0.1 maximum_convert_fusion.1
  20.9 0.0 collective-permute-done.2
  20.9 0.1 maximum_convert_fusion.2
  21.1 0.7 fusion.4
  21.7 5.8 %multiply_reduce_fusion.1 = (f32[8,16,2048]{2,1,0:T(8,128)S(1)}, f32[8,16,2048]{2,1,0:T(8,128)}) fusion(f32[16,16,2048]{2,1,0:T(8,128)S(1)} %get-tuple-element.10, f32[8,16,2048]{2,1,0:T(8,128)S(1)} %bitcast.23, f32[16,16,2048]{2,1,0:T(8,128)S(1)} %fusion.17), kind=kLoop, calls=%fused_computation.2 | loop fusion | flops 16252928 | bytes 7340032 | tf_op jit(solution)/shard_map/reduce_sum | solution.py:67
  27.5 0.1 slice_add_fusion.1
  27.6 0.8 copy-done.6
  28.6 0.1 pad.23
  28.6 1.5 pad.22
  30.1 1.1 add.100
  31.2 2.3 %pad.62 = f32[7,16,2048]{2,1,0:T(8,128)} pad(f32[4,16,2048]{2,1,0:T(8,128)S(1)} %add.100, f32[]{:T(128)} %constant.13.clone.1), padding=0_0_1x0_0_0x0_0_0 | pad | bytes 1441796
  33.5 1.5 add_convert_fusion
  35.1 0.0 all-gather.2.cloned.1.call-update
  35.1 0.8 slice.149
  35.9 3.7 %collective-permute-start = (bf16[2,2048]{1,0:T(2,128)(2,1)S(1)}, bf16[2,2048]{1,0:T(2,128)(2,1)S(1)}, u32[]{:S(2)}, u32[]{:S(2)}) collective-permute-start(bf16[2,2048]{1,0:T(2,128)(2,1)S(1)} %slice.149), channel_id=1, source_target_pairs={{0,4},{4,8},{8,12},{12,16},{16,20},{20,24},{24,28},{28,32},{32,36}... | collective-permute-start | bytes 24584 | tf_op jit(solution)/shard_map/ppermute | solution.py:17
  39.6 1.1 fusion.13
  40.7 2.4 %pad.25 = f32[8,16,2048]{2,1,0:T(8,128)} pad(f32[4,16,2048]{2,1,0:T(8,128)S(1)} %add.100, f32[]{:T(128)} %constant.13.clone.1), padding=1_0_1x0_0_0x0_0_0 | pad | bytes 1572868 | tf_op jit(solution)/shard_map/pad | solution.py:69
  43.1 2.4 %pad.24 = f32[8,16,2048]{2,1,0:T(8,128)} pad(f32[4,16,2048]{2,1,0:T(8,128)S(1)} %pad_maximum_fusion, f32[]{:T(128)} %constant.13.clone.1), padding=0_1_1x0_0_0x0_0_0 | pad | bytes 1572868 | tf_op jit(solution)/shard_map/pad | solution.py:69
  45.5 0.0 collective-permute-done
  45.5 1.3 maximum_convert_fusion
  46.8 0.1 copy-done.4
  46.9 1.0 slice_add_fusion
  47.9 150.3 %all-gather.2.cloned.1.call-done = bf16[128,16,2048]{2,1,0:T(8,128)(2,1)} async-done(((bf16[1,16,2048]{2,1,0:T(8,128)(2,1)}), bf16[128,16,2048]{2,1,0:T(8,128)(2,1)}) %all-gather.2.cloned.1.call-update) | async-done | bytes 8388624 | tf_op jit(solution)/shard_map/all_gather | solution.py:73
  198.2 7.1 %select_reduce_fusion = f32[16,2048]{1,0:T(8,128)S(1)} fusion(bf16[128,16,2048]{2,1,0:T(8,128)(2,1)} %all-gather.2.cloned.1.call-done, f32[128]{0:T(128)S(1)} %multiply_convert_fusion, f32[16,2048]{1,0:T(8,128)S(1)} %get-tuple-element.13, pred[128]{0:T(512)(128)(4,1)S(1)} %fusion.20), kind=kLoop, calls=%fused_computation.1 | loop fusion | flops 20938752 | bytes 8651392 | tf_op jit(solution)/shard_map/reduce_sum | solution.py:82
  205.3 0.0 copy-done.5
  205.3 0.0 copy-start
  205.3 0.2 multiply_add_fusion
  205.6 1.3 copy-done
  206.9 4.2 %multiply_reduce_fusion = f32[8,16,2048]{2,1,0:T(8,128)S(1)} fusion(f32[8,16,2048]{2,1,0:T(8,128)S(1)} %multiply_add_fusion, f32[16,16,2048]{2,1,0:T(8,128)S(1)} %copy-done), kind=kLoop, calls=%fused_computation | loop fusion | flops 8126464 | bytes 4194304 | tf_op jit(solution)/shard_map/reduce_sum | solution.py:86
  211.1 0.0 copy-start.9
  211.2 0.0 copy-start.10
  211.2 0.1 add.104
  211.3 0.9 copy-done.9
  212.2 0.5 fusion.11
  212.7 0.0 copy-start.1
  212.7 0.2 fusion
  212.9 7.6 %psum.7 = f32[128]{0:T(128)S(1)} all-reduce(f32[128]{0:T(128)S(1)} %fusion), channel_id=1, replica_groups=mesh['seq'=128,'chan'=4] {'chan'}, use_global_device_ids=true, to_apply=%region_6.7 | all-reduce | flops 128 | bytes 1024 | tf_op jit(solution)/shard_map/psum | solution.py:91
  220.5 1.0 fusion.2
  (28 shorter events, 0.3 us)
Async XLA Ops:
  7.2 191.1 %all-gather.2.cloned.1.call-start = ((), (), s32[]{:S(2)}) async-start(), calls=%async_computation | async-start | bytes 8454144 | tf_op jit(solution)/shard_map/all_gather | solution.py:73
  8.0 12.7 %collective-permute-start.1 = (bf16[2,2048]{1,0:T(2,128)(2,1)S(1)}, bf16[2,2048]{1,0:T(2,128)(2,1)S(1)}, u32[]{:S(2)}, u32[]{:S(2)}) collective-permute-start(bf16[2,2048]{1,0:T(2,128)(2,1)S(1)} %slice.156), channel_id=1, source_target_pairs={{0,4},{4,8},{8,12},{12,16},{16,20},{20,24},{24,28},{28,32},{32,36}... | collective-permute-start | bytes 24584 | tf_op jit(solution)/shard_map/ppermute | solution.py:17
  13.3 7.6 %collective-permute-start.2 = (bf16[2,2048]{1,0:T(2,128)(2,1)S(1)}, bf16[2,2048]{1,0:T(2,128)(2,1)S(1)}, u32[]{:S(2)}, u32[]{:S(2)}) collective-permute-start(bf16[2,2048]{1,0:T(2,128)(2,1)S(1)} %slice.163), channel_id=1, source_target_pairs={{0,4},{4,8},{8,12},{12,16},{16,20},{20,24},{24,28},{28,32},{32,36}... | collective-permute-start | bytes 24584 | tf_op jit(solution)/shard_map/ppermute | solution.py:17
  19.7 1.0 copy-start.7
  19.7 1.2 copy-start.8
  27.5 0.9 copy-start.6
  35.9 9.7 %collective-permute-start = (bf16[2,2048]{1,0:T(2,128)(2,1)S(1)}, bf16[2,2048]{1,0:T(2,128)(2,1)S(1)}, u32[]{:S(2)}, u32[]{:S(2)}) collective-permute-start(bf16[2,2048]{1,0:T(2,128)(2,1)S(1)} %slice.149), channel_id=1, source_target_pairs={{0,4},{4,8},{8,12},{12,16},{16,20},{20,24},{24,28},{28,32},{32,36}... | collective-permute-start | bytes 24584 | tf_op jit(solution)/shard_map/ppermute | solution.py:17
  43.1 3.7 %copy-start.3 = (f32[8,16,2048]{2,1,0:T(8,128)S(1)}, f32[8,16,2048]{2,1,0:T(8,128)}, u32[]{:S(2)}) copy-start(f32[8,16,2048]{2,1,0:T(8,128)} %pad.25) | copy-start | bytes 3145732
  45.5 1.4 copy-start.4
  47.9 157.4 %copy-start.5 = (f32[7,16,2048]{2,1,0:T(8,128)S(1)}, f32[7,16,2048]{2,1,0:T(8,128)}, u32[]{:S(2)}) copy-start(f32[7,16,2048]{2,1,0:T(8,128)} %slice_add_fusion) | copy-start | bytes 2752516
  205.3 1.6 copy-start
  206.9 4.2 %copy-start.2 = (f32[8,16,2048]{2,1,0:T(8,128)S(1)}, f32[8,16,2048]{2,1,0:T(8,128)}, u32[]{:S(2)}) copy-start(f32[8,16,2048]{2,1,0:T(8,128)} %get-tuple-element.3) | copy-start | bytes 3145732
  211.1 1.0 copy-start.9
  211.2 1.0 copy-start.10
  212.2 8.3 %copy-start.11 = (f32[2048]{0:T(1024)S(1)}, f32[2048]{0:T(1024)}, u32[]{:S(2)}) copy-start(f32[2048]{0:T(1024)} %param.17) | copy-start | bytes 24580
  212.7 8.8 %copy-start.1 = (bf16[128,2048]{1,0:T(8,128)(2,1)}, bf16[128,2048]{1,0:T(8,128)(2,1)S(1)}, u32[]{:S(2)}) copy-start(bf16[128,2048]{1,0:T(8,128)(2,1)S(1)} %fusion.11) | copy-start | bytes 1572868
Sparse Core Ops, SparseCore 0:
  35.2 162.9 all-gather.1
where the time goes:
time: 230 us; the launch traced here: 228 us
  waiting for transfers between devices  150 us (65%)
  other arithmetic  29.9 us (13%)
  local copies, waits for them, and re-layouts  15.1 us (7%)
  between operations  14.3 us (6%)
  starting transfers between devices  10.1 us (4%)
  blocking collectives  7.59 us (3%)
    all_gather x1, waiting for transfers between devices, body(): lax.all_gather(block_state[None].astype(jnp.bfloat16), 'seq', axis=0, til...  150 us
    ppermute x3, starting transfers between devices, shifted(): return lax.ppermute(block, axis, route)  10.1 us
    psum x1, blocking collectives, body(): row_squares = lax.psum(jnp.sum(widened * widened, axis=1), 'chan')  7.59 us
    reduce_sum x1, other arithmetic, body(): carried = jnp.zeros_like(block_state) + jnp.sum(masked, axis=0)  7.07 us
    pad x4, local copies, waits for them, and re-layouts, body(): lax.associative_scan(link_states, (step_decay, sub_states), axis=0)  6.35 us
    reduce_sum x1, other arithmetic, body(): sub_states = jnp.sum(blocks[:, :, None, :] * tail_decay[None], axis=1)  5.81 us
    unnamed x25, local copies, waits for them, and re-layouts  5.43 us
  transfers between devices with their start and end apart: 4, of which 1 were waited for; matrix products, arithmetic and copies ran while one was open for 7% of the time, Pallas kernels for 0%

commit v1 on v0

v1 whole, which is shorter than its diff:
```python
import functools

import jax
import jax.numpy as jnp
from jax import lax
from jax.experimental import pallas as pl
from jax.experimental.pallas import tpu as pltpu
from jax.sharding import PartitionSpec as P

D = 8192
EPSILON = 1e-06
LANES = 128
SUBLANES = 8
MINOR = 8
MIDDLE = 8
MAJOR = 2
STEP = 6

f32 = jnp.float32
bf16 = jnp.bfloat16


def call(kernel, out_shape, name, scratch=(), **extra):
    return pl.pallas_call(
        kernel,
        out_shape=out_shape,
        scratch_shapes=scratch,
        compiler_params=pltpu.CompilerParams(vmem_limit_bytes=14 << 20),
        name=name,
        **extra,
    )


def spread(source, target, first=0):
    items, chans = source.shape
    groups = chans // LANES
    for j in range(groups):
        target[pl.ds(first * groups + j, items, stride=groups), :] = source[
            :, j * LANES : (j + 1) * LANES
        ].astype(f32)


def tile(ref, item, half, groups):
    start = item * groups + half * SUBLANES
    if not isinstance(start, int):
        start = pl.multiple_of(start, SUBLANES)
    return ref[pl.ds(start, SUBLANES), :]


def put(ref, item, half, groups, value):
    start = item * groups + half * SUBLANES
    if not isinstance(start, int):
        start = pl.multiple_of(start, SUBLANES)
    ref[pl.ds(start, SUBLANES), :] = value


def taps_of(taps_ref, which, half, groups):
    return [tile(taps_ref, which * 3 + lag, half, groups) for lag in range(3)]


def fir(taps, now, last, older):
    return taps[0] * now + taps[1] * last + taps[2] * older


def tails_kernel(query_in, key_in, value_in, tails):
    last = [x[...].astype(f32)[-2:] for x in (query_in, key_in, value_in)]
    tails[...] = jnp.concatenate(last, axis=0).astype(bf16)


def first_kernel(
    key_in, value_in, filters, decay_rate, mixed, heads, taps, rates, partial, keys, values
):
    tokens, chans = key_in.shape
    groups = chans // LANES
    poles = decay_rate.shape[0]
    spread(decay_rate, rates)
    for which in range(3):
        spread(filters.at[which], taps, 3 * which)
    spread(key_in, keys)
    spread(value_in, values)
    heads[: 2 * groups, :] = keys[: 2 * groups, :]
    heads[2 * groups :, :] = values[: 2 * groups, :]
    for half in range(groups // SUBLANES):
        key_taps = taps_of(taps, 1, half, groups)
        value_taps = taps_of(taps, 2, half, groups)
        factor = [jnp.exp(-tile(rates, n, half, groups)) for n in range(poles)]

        def turn(i, carry):
            k1, k2, v1, v2, *state = carry
            for u in range(STEP):
                t = 2 + i * STEP + u
                k0 = tile(keys, t, half, groups)
                v0 = tile(values, t, half, groups)
                m = fir(key_taps, k0, k1, k2) * fir(value_taps, v0, v1, v2)
                put(mixed, t, half, groups, m)
                state = [factor[n] * state[n] + m for n in range(poles)]
                k1, k2, v1, v2 = k0, k1, v0, v1
            return (k1, k2, v1, v2, *state)

        begin = (
            tile(keys, 1, half, groups),
            tile(keys, 0, half, groups),
            tile(values, 1, half, groups),
            tile(values, 0, half, groups),
        ) + (jnp.zeros((SUBLANES, LANES), f32),) * poles
        end = lax.fori_loop(0, (tokens - 2) // STEP, turn, begin)
        for n in range(poles):
            put(partial, n, half, groups, end[4 + n])
        for t in range(2):
            put(mixed, t, half, groups, jnp.zeros((SUBLANES, LANES), f32))


def state_kernel(tokens, tails, heads, taps, rates, partial, state, opening, before):
    groups = tails.shape[1] // LANES
    poles = rates.shape[0] // groups
    spread(tails, before)
    for half in range(groups // SUBLANES):
        m = []
        for t in range(2):
            pair = []
            for side in range(2):
                line = [tile(before, 2 * side + 2 + r, half, groups) for r in range(2)]
                line += [tile(heads, 2 * side + r, half, groups) for r in range(2)]
                tap = taps_of(taps, 1 + side, half, groups)
                pair.append(fir(tap, line[t + 2], line[t + 1], line[t]))
            m.append(pair[0] * pair[1])
            put(opening, t, half, groups, m[t])
        for n in range(poles):
            rate = tile(rates, n, half, groups)
            total = (
                tile(partial, n, half, groups)
                + jnp.exp(-rate * (tokens - 1.0)) * m[0]
                + jnp.exp(-rate * (tokens - 2.0)) * m[1]
            )
            put(before, n, half, groups, total)
    state[...] = before[...].astype(bf16)


def inner_kernel(
    query_in, tails, taps, rates, residue, skip, mixed, opening, base, query, lead, rows, weights
):
    tokens, chans = query_in.shape
    groups = chans // LANES
    poles = residue.shape[0]
    spread(residue, weights)
    spread(tails, rows)
    spread(query_in, rows, 2)
    for half in range(groups // SUBLANES):
        query_taps = taps_of(taps, 0, half, groups)
        factor, weight = [], []
        for n in range(poles):
            rate = tile(rates, n, half, groups)
            factor.append(jnp.exp(-rate))
            weight.append(tile(weights, n, half, groups) * jnp.sqrt(2.0 * rate))
            put(lead, n, half, groups, weight[n] * factor[n])
        direct = tile(skip, 0, half, groups)

        def follow(state, m):
            state = [factor[n] * state[n] + m for n in range(poles)]
            parts = [direct * m, weight[0] * state[0]]
            for n in range(1, poles):
                parts[n % 2] = parts[n % 2] + weight[n] * state[n]
            return state, parts[0] + parts[1]

        state = [jnp.zeros((SUBLANES, LANES), f32)] * poles
        for t in range(2):
            state, out = follow(state, tile(opening, t, half, groups))
            put(base, t, half, groups, out)

        def turn(i, state):
            for u in range(STEP):
                t = 2 + i * STEP + u
                state, out = follow(state, tile(mixed, t, half, groups))
                put(base, t, half, groups, out)
            return tuple(state)

        lax.fori_loop(0, (tokens - 2) // STEP, turn, tuple(state))

        def filtered(i, carry):
            q1, q2 = carry
            for u in range(8):
                t = i * 8 + u
                q0 = tile(rows, t + 2, half, groups)
                put(query, t, half, groups, fir(query_taps, q0, q1, q2))
                q1, q2 = q0, q1
            return q1, q2

        lax.fori_loop(
            0, tokens // 8, filtered, (tile(rows, 1, half, groups), tile(rows, 0, half, groups))
        )


def pair_rates(rates, place, rows):
    return rates[pl.ds(pl.multiple_of(place * rows, SUBLANES), rows), :]


def minor_kernel(block, place, arrived, rates, sums, prefix):
    rows = arrived.shape[0] // MINOR
    decay = jnp.exp(-pair_rates(rates, place[0] % MINOR, rows) * block)
    total = jnp.zeros((rows, LANES), f32)
    for b in range(MINOR):
        prefix[b * rows : (b + 1) * rows, :] = total
        total = decay * total + arrived[b * rows : (b + 1) * rows, :].astype(f32)
    total = total.astype(bf16)
    for other in range(MIDDLE):
        sums[other * rows : (other + 1) * rows, :] = total


def middle_kernel(block, place, arrived, rates, prefix, carries):
    rows = arrived.shape[0] // MIDDLE
    rate = pair_rates(rates, place[0] % MINOR, rows)
    mine = (place[0] // MINOR) % MIDDLE
    lower = place[0] < MINOR * MIDDLE
    decay = jnp.exp(-rate * block)
    line_decay = jnp.exp(-rate * (block * MINOR))
    before = jnp.zeros((rows, LANES), f32)
    whole = jnp.zeros((rows, LANES), f32)
    for other in range(MIDDLE):
        piece = arrived[other * rows : (other + 1) * rows, :].astype(f32)
        whole = line_decay * whole + piece
        before = jnp.where(other < mine, whole, before)
    onward = jnp.exp(-rate * (mine.astype(f32) * (block * MINOR))) * whole
    half_rows = MINOR * rows
    for b in range(MINOR):
        here = before + prefix[b * rows : (b + 1) * rows, :]
        carries[b * rows : (b + 1) * rows, :] = jnp.where(lower, here, 0.0).astype(bf16)
        carries[half_rows + b * rows : half_rows + (b + 1) * rows, :] = jnp.where(
            lower, onward, here
        ).astype(bf16)
        before = decay * before
        onward = decay * onward


def outer_kernel(carries, rates, lead, base, query, residual, summed, squares, gated):
    tokens, chans = residual.shape
    groups = chans // LANES
    poles = rates.shape[0] // groups
    for half in range(groups // SUBLANES):
        factor, state = [], []
        for n in range(poles):
            factor.append(jnp.exp(-tile(rates, n, half, groups)))
            start = n * groups + half * SUBLANES
            carried = carries[start : start + SUBLANES, :].astype(f32)
            start += poles * groups
            carried = carried + carries[start : start + SUBLANES, :].astype(f32)
            state.append(tile(lead, n, half, groups) * carried)

        def turn(i, state):
            for u in range(8):
                t = i * 8 + u
                parts = [tile(base, t, half, groups) + state[0], state[1]]
                for n in range(2, poles):
                    parts[n % 2] = parts[n % 2] + state[n]
                put(
                    gated, t, half, groups, tile(query, t, half, groups) * (parts[0] + parts[1])
                )
                state = [factor[n] * state[n] for n in range(poles)]
            return tuple(state)

        lax.fori_loop(0, tokens // 8, turn, tuple(state))
    total = jnp.zeros((tokens, LANES), f32)
    for j in range(groups):
        columns = slice(j * LANES, (j + 1) * LANES)
        value = residual[:, columns].astype(f32) + gated[pl.ds(j, tokens, stride=groups), :]
        value = value.astype(bf16)
        summed[:, columns] = value
        value = value.astype(f32)
        total = total + value * value
    squares[...] = jnp.broadcast_to(
        jnp.sum(total.T, axis=0, keepdims=True), squares.shape
    )


def norm_kernel(summed, squares, gain, normed):
    tokens, chans = summed.shape
    mean = jnp.sum(squares[...], axis=0, keepdims=True) / D
    inverse = jnp.broadcast_to(lax.rsqrt(mean + EPSILON), (LANES, tokens)).T
    for j in range(chans // LANES):
        columns = slice(j * LANES, (j + 1) * LANES)
        normed[:, columns] = (
            summed[:, columns].astype(f32) * inverse * gain[j : j + 1, :]
        ).astype(bf16)


def body(
    residual, query_in, key_in, value_in, short_filter, decay_rate, residue, skip_gain, norm_gain
):
    tokens, chans = residual.shape
    poles = decay_rate.shape[0]
    groups = chans // LANES
    count = MINOR * MIDDLE * MAJOR

    def rows(items, kind=f32):
        return jax.ShapeDtypeStruct((items * groups, LANES), kind)

    def hold(items):
        return pltpu.VMEM((items * groups, LANES), f32)

    tail_spec = pl.BlockSpec((16, chans), lambda i: (tokens // 16 - 1, 0))
    tails = call(
        tails_kernel,
        jax.ShapeDtypeStruct((6, chans), bf16),
        "tails",
        grid=(1,),
        in_specs=[tail_spec] * 3,
        out_specs=pl.BlockSpec((6, chans), lambda i: (0, 0)),
    )(query_in, key_in, value_in)
    tails = lax.ppermute(tails, "seq", [(i, i + 1) for i in range(count - 1)])

    mixed, heads, taps, rates, partial = call(
        first_kernel,
        (rows(tokens), rows(4), rows(9), rows(poles), rows(poles)),
        "first",
        scratch=[hold(tokens), hold(tokens)],
    )(key_in, value_in, short_filter, decay_rate)
    state, opening = call(
        functools.partial(state_kernel, float(tokens)),
        (rows(poles, bf16), rows(2)),
        "state",
        scratch=[hold(poles)],
    )(tails, heads, taps, rates, partial)

    place = lax.axis_index("seq").astype(jnp.int32).reshape(1)
    smem = pl.BlockSpec(memory_space=pltpu.SMEM)
    vmem = pl.BlockSpec(memory_space=pltpu.VMEM)
    lines = [[g * MINOR + j for j in range(MINOR)] for g in range(MIDDLE * MAJOR)]
    planes = [
        [(z * MIDDLE + y) * MINOR + j for y in range(MIDDLE)]
        for z in range(MAJOR)
        for j in range(MINOR)
    ]
    pairs = [
        [(z * MIDDLE + y) * MINOR + j for z in range(MAJOR) for j in range(MINOR)]
        for y in range(MIDDLE)
    ]

    def exchange(x, members):
        return lax.all_to_all(x, "seq", 0, 0, axis_index_groups=members, tiled=True)

    arrived = exchange(state, lines)
    base, query, lead = call(
        inner_kernel,
        (rows(tokens), rows(tokens), rows(poles)),
        "inner",
        scratch=[hold(tokens + 4), hold(poles)],
    )(
        query_in,
        tails,
        taps,
        rates,
        residue,
        skip_gain.reshape(groups, LANES),
        mixed,
        opening,
    )
    sums, prefix = call(
        functools.partial(minor_kernel, float(tokens)),
        (rows(poles, bf16), rows(poles)),
        "minor",
        in_specs=[smem, vmem, vmem],
    )(place, arrived, rates)
    arrived = exchange(sums, planes)
    carries = call(
        functools.partial(middle_kernel, float(tokens)),
        rows(MAJOR * poles, bf16),
        "middle",
        in_specs=[smem, vmem, vmem, vmem],
    )(place, arrived, rates, prefix)
    carries = exchange(carries, pairs)
    members = lax.axis_size("chan")
    summed, squares = call(
        outer_kernel,
        (
            jax.ShapeDtypeStruct((tokens, chans), bf16),
            jax.ShapeDtypeStruct((members, tokens), f32),
        ),
        "outer",
        scratch=[hold(tokens)],
    )(carries, rates, lead, base, query, residual)
    squares = lax.all_to_all(squares, "chan", 0, 0, tiled=True)
    normed = call(norm_kernel, jax.ShapeDtypeStruct((tokens, chans), bf16), "norm")(
        summed, squares, norm_gain.reshape(groups, LANES)
    )
    return (summed, normed)


def solution(mesh):
    whole = P("seq", "chan")
    in_specs = (whole, whole, whole, whole, P(None, None, "chan"))
    in_specs += (P(None, "chan"), P(None, "chan"), P("chan"), P("chan"))
    return jax.shard_map(
        body, mesh=mesh, in_specs=in_specs, out_specs=(whole, whole), check_vma=False
    )
```

time: 230 us -> 76.8 us (0.33)
  waiting for transfers between devices: 150 us -> 9.19 us
  other arithmetic: 29.9 us -> 0 us
  blocking collectives: 7.59 us -> 24.7 us
  between operations: 14.3 us -> 0.76 us
  starting transfers between devices: 10.1 us -> 21.4 us
  Pallas kernels: 0 us -> 11.2 us
  local copies, waits for them, and re-layouts: 15.1 us -> 8.87 us
    all_gather x1 -> x0, waiting for transfers between devices: 150 us -> none  [body(): lax.all_gather(block_state[None].astype(jnp.bfloat16), 'seq', axis=0, til...]
    all_to_all x0 -> x2, blocking collectives: none -> 24.7 us  [the longest x1 15.5 us: exchange(): return lax.all_to_all(x, 'seq', 0, 0, axis_index_groups=members, tiled=True)]
    reduce_sum x4 -> x0, other arithmetic: 17.3 us -> none  [the longest x1 7.07 us: body(): carried = jnp.zeros_like(block_state) + jnp.sum(masked, axis=0)]
    all_to_all x0 -> x2, starting transfers between devices: none -> 16.8 us  [exchange(): return lax.all_to_all(x, 'seq', 0, 0, axis_index_groups=members, tiled=True)]
    pallas_call x0 -> x8, Pallas kernels: none -> 11.2 us  [the longest x1 3.48 us: body(): call(inner_kernel, (rows(tokens), rows(tokens), rows(poles)), 'inner', sc...]
    all_to_all x0 -> x2, waiting for transfers between devices: none -> 8.69 us  [exchange(): return lax.all_to_all(x, 'seq', 0, 0, axis_index_groups=members, tiled=True)]
    psum x1 -> x0, blocking collectives: 7.59 us -> none  [body(): row_squares = lax.psum(jnp.sum(widened * widened, axis=1), 'chan')]
    pad x4 -> x0, local copies, waits for them, and re-layouts: 6.35 us -> none  [body(): lax.associative_scan(link_states, (step_decay, sub_states), axis=0)]
  transfers between devices with their start and end apart: 4 -> 3, of which waited for: 1 -> 3; matrix products, arithmetic and copies ran while one was open for 7% -> 0% of each run, Pallas kernels for 0% -> 8%
where the time goes in v1:
time: 76.8 us; the launch traced here: 76.1 us
  blocking collectives  24.7 us (32%)
  starting transfers between devices  21.4 us (28%)
  Pallas kernels  11.2 us (15%)
  waiting for transfers between devices  9.19 us (12%)
  local copies, waits for them, and re-layouts  8.87 us (12%)
    all_to_all x2, starting transfers between devices, exchange(): return lax.all_to_all(x, 'seq', 0, 0, axis_index_groups=members, tiled=True)  16.8 us
    all_to_all x1, blocking collectives, exchange(): return lax.all_to_all(x, 'seq', 0, 0, axis_index_groups=members, tiled=True)  15.5 us
    all_to_all x1, blocking collectives, body(): squares = lax.all_to_all(squares, 'chan', 0, 0, tiled=True)  9.15 us
    unnamed x34, local copies, waits for them, and re-layouts  8.87 us
    all_to_all x2, waiting for transfers between devices, exchange(): return lax.all_to_all(x, 'seq', 0, 0, axis_index_groups=members, tiled=True)  8.69 us
    ppermute x1, starting transfers between devices, body(): tails = lax.ppermute(tails, 'seq', [(i, i + 1) for i in range(count - 1)])  4.63 us
    pallas_call x1, Pallas kernels, body(): call(inner_kernel, (rows(tokens), rows(tokens), rows(poles)), 'inner', sc...  3.48 us
    pallas_call x1, Pallas kernels, body(): call(first_kernel, (rows(tokens), rows(4), rows(9), rows(poles), rows(pol...  2.75 us
  transfers between devices with their start and end apart: 3, of which 3 were waited for; matrix products, arithmetic and copies ran while one was open for 0% of the time, Pallas kernels for 8%

profile of v1, /device:TPU:1, one launch (start us, length us, event | category | flops | bytes accessed | tf_op | source)
XLA Modules:
  0.0 76.1 jit_solution(9592408782293327153)
XLA Ops:
  0.6 0.0 copy-start
  0.6 1.0 %copy-done = bf16[128,2048]{1,0:T(8,128)(2,1)S(1)} copy-done((bf16[128,2048]{1,0:T(8,128)(2,1)S(1)}, bf16[128,2048]{1,0:T(8,128)(2,1)}, u32[]{:S(2)}) %copy-start) | copy-done | bytes 524312
  1.7 0.0 copy-start.2
  1.7 1.0 %copy-done.2 = bf16[128,2048]{1,0:T(8,128)(2,1)S(1)} copy-done((bf16[128,2048]{1,0:T(8,128)(2,1)S(1)}, bf16[128,2048]{1,0:T(8,128)(2,1)}, u32[]{:S(2)}) %copy-start.2) | copy-done | bytes 524312
  2.7 0.0 copy-start.4
  2.7 1.0 %copy-done.4 = bf16[128,2048]{1,0:T(8,128)(2,1)S(1)} copy-done((bf16[128,2048]{1,0:T(8,128)(2,1)S(1)}, bf16[128,2048]{1,0:T(8,128)(2,1)}, u32[]{:S(2)}) %copy-start.4) | copy-done | bytes 524312
  3.8 0.0 copy-start.1
  3.8 0.0 copy-start.3
  3.8 0.0 copy-start.10
  3.8 0.0 copy-start.14
  3.8 4.6 %collective-permute-start = (bf16[6,2048]{1,0:T(8,128)(2,1)S(1)}, bf16[6,2048]{1,0:T(8,128)(2,1)S(1)}, u32[]{:S(2)}, u32[]{:S(2)}) collective-permute-start(bf16[6,2048]{1,0:T(8,128)(2,1)S(1)} %tails.1), channel_id=1, source_target_pairs={{0,4},{4,8},{8,12},{12,16},{16,20},{20,24},{24,28},{28,32},{32,36}... | collective-permute-start | bytes 73736 | tf_op jit(solution)/shard_map/ppermute | solution.py:308
  8.4 0.0 copy-done.1
  8.4 0.0 copy-done.3
  8.5 0.0 copy-done.10
  8.5 0.0 copy-done.14
  8.5 2.8 %first.1 = (f32[2048,128]{1,0:T(8,128)S(1)}, f32[64,128]{1,0:T(8,128)S(1)}, f32[144,128]{1,0:T(8,128)S(1)}, f32[256,128]{1,0:T(8,128)S(1)}, f32[256,128]{1,0:T(8,128)S(1)}) custom-call(bf16[128,2048]{1,0:T(8,128)(2,1)S(1)} %copy-done.1, bf16[128,2048]{1,0:T(8,128)(2,1)S(1)} %copy-done.3, f32[3,3,2048]{2,1,0:T(4,128)S(1)} %copy-done.14, f32[16,2048]{1,0:T(8,128)S(1)} %copy-done.10), custom_call_target="tpu_custom_call" | custom-call | tf_op jit(solution)/shard_map/first/pallas_call | solution.py:310
  11.2 0.0 copy-start.6
  11.2 1.0 %copy-done.6 = f32[2048,128]{1,0:T(8,128)} copy-done((f32[2048,128]{1,0:T(8,128)}, f32[2048,128]{1,0:T(8,128)S(1)}, u32[]{:S(2)}) %copy-start.6) | copy-done | bytes 1048600
  12.3 0.5 collective-permute-done.tails
  12.7 0.7 state.1
  13.5 6.4 %all-to-all-start = ((bf16[8,32,128]{2,1,0:T(8,128)(2,1)}), bf16[8,32,128]{2,1,0:T(8,128)(2,1)S(1)}, u32[]{:S(2)}, u32[]{:S(2)}) async-start(bf16[8,32,128]{2,1,0:T(8,128)(2,1)} %bitcast.1), calls=%async_computation | async-start | bytes 131072 | tf_op jit(solution)/shard_map/all_to_all | solution.py:338
  19.8 4.9 %all-to-all-done = bf16[8,32,128]{2,1,0:T(8,128)(2,1)S(1)} async-done(((bf16[8,32,128]{2,1,0:T(8,128)(2,1)}), bf16[8,32,128]{2,1,0:T(8,128)(2,1)S(1)}, u32[]{:S(2)}, u32[]{:S(2)}) %all-to-all-start) | async-done | bytes 65568 | tf_op jit(solution)/shard_map/all_to_all | solution.py:338
  24.7 0.0 copy-start.5
  24.8 15.5 %all_to_all.44 = bf16[8,32,128]{2,1,0:T(8,128)(2,1)S(1)} all-to-all(bf16[8,32,128]{2,1,0:T(8,128)(2,1)S(1)} %bitcast.16), channel_id=1, replica_groups={{0,32,64,96,128,160,192,224},{4,36,68,100,132,164,196,228},{8,40,72,104..., dimensions={0} | all-to-all | bytes 131072 | tf_op jit(solution)/shard_map/all_to_all | solution.py:338
  40.3 0.7 middle.1
  41.0 0.0 copy-start.15
  41.0 10.4 %all-to-all-start.2 = ((bf16[16,32,128]{2,1,0:T(8,128)(2,1)}), bf16[16,32,128]{2,1,0:T(8,128)(2,1)S(1)}, u32[]{:S(2)}, u32[]{:S(2)}) async-start(bf16[16,32,128]{2,1,0:T(8,128)(2,1)} %bitcast.5), calls=%async_computation.2 | async-start | bytes 262144 | tf_op jit(solution)/shard_map/all_to_all | solution.py:338
  51.4 0.0 copy-done.5
  51.4 0.0 copy-done.15
  51.4 0.0 copy-start.7
  51.4 1.2 %copy-done.7 = f32[2048,128]{1,0:T(8,128)S(1)} copy-done((f32[2048,128]{1,0:T(8,128)S(1)}, f32[2048,128]{1,0:T(8,128)}, u32[]{:S(2)}) %copy-start.7) | copy-done | bytes 1048600
  52.6 0.0 copy-start.13
  52.6 0.9 %copy-done.13 = f32[16,2048]{1,0:T(8,128)S(1)} copy-done((f32[16,2048]{1,0:T(8,128)S(1)}, f32[16,2048]{1,0:T(8,128)}, u32[]{:S(2)}) %copy-start.13) | copy-done | bytes 131096
  53.5 0.0 copy-start.9
  53.5 3.5 %inner.1 = (f32[2048,128]{1,0:T(8,128)S(1)}, f32[2048,128]{1,0:T(8,128)S(1)}, f32[256,128]{1,0:T(8,128)S(1)}) custom-call(bf16[128,2048]{1,0:T(8,128)(2,1)S(1)} %copy-done.5, bf16[6,2048]{1,0:T(8,128)(2,1)S(1)} %collective-permute-done.tails, f32[144,128]{1,0:T(8,128)S(1)} %get-tuple-element.17.taps, f32[256,128]{1,0:T(8,128)S(1)} %get-tuple-element.18.rates, ...), custom_call_target="tpu_custom_call" | custom-call | tf_op jit(solution)/shard_map/inner/pallas_call | solution.py:341
  57.0 0.0 copy-start.11
  57.0 0.6 copy-done.11
  57.7 3.8 %all-to-all-done.2 = bf16[16,32,128]{2,1,0:T(8,128)(2,1)S(1)} async-done(((bf16[16,32,128]{2,1,0:T(8,128)(2,1)}), bf16[16,32,128]{2,1,0:T(8,128)(2,1)S(1)}, u32[]{:S(2)}, u32[]{:S(2)}) %all-to-all-start.2) | async-done | bytes 131104 | tf_op jit(solution)/shard_map/all_to_all | solution.py:338
  61.5 0.0 copy-done.9
  61.5 0.0 copy-start.12
  61.5 0.9 %copy-done.12 = f32[256,128]{1,0:T(8,128)S(1)} copy-done((f32[256,128]{1,0:T(8,128)S(1)}, f32[256,128]{1,0:T(8,128)}, u32[]{:S(2)}) %copy-start.12) | copy-done | bytes 131096
  62.4 2.5 %outer.1 = (bf16[128,2048]{1,0:T(8,128)(2,1)}, f32[4,128]{1,0:T(4,128)S(1)}) custom-call(bf16[512,128]{1,0:T(8,128)(2,1)S(1)} %bitcast.13, f32[256,128]{1,0:T(8,128)S(1)} %get-tuple-element.18.rates, f32[256,128]{1,0:T(8,128)S(1)} %copy-done.12, f32[2048,128]{1,0:T(8,128)S(1)} %get-tuple-element.26.base, f32[2048,128]{1,0:T(8,128)S(1)} %get-tuple-element.27.query, ...), custom_call_target="tpu_custom_call" | custom-call | tf_op jit(solution)/shard_map/outer/pallas_call | solution.py:371
  64.9 0.0 copy-start.16
  64.9 9.2 %all_to_all.45 = f32[4,1,128]{2,1,0:T(1,128)S(1)} all-to-all(f32[4,1,128]{2,1,0:T(1,128)S(1)} %bitcast.20), channel_id=1, replica_groups=mesh['seq'=128,'chan'=4] {'chan'}, dimensions={0} | all-to-all | bytes 4096 | tf_op jit(solution)/shard_map/all_to_all | solution.py:380
  74.0 0.0 copy-done.16
  74.0 0.0 copy-start.8
  74.1 1.0 %copy-done.8 = bf16[128,2048]{1,0:T(8,128)(2,1)S(1)} copy-done((bf16[128,2048]{1,0:T(8,128)(2,1)S(1)}, bf16[128,2048]{1,0:T(8,128)(2,1)}, u32[]{:S(2)}) %copy-start.8) | copy-done | bytes 524312
  75.1 1.0 %norm.1 = bf16[128,2048]{1,0:T(8,128)(2,1)} custom-call(bf16[128,2048]{1,0:T(8,128)(2,1)S(1)} %copy-done.8, f32[4,128]{1,0:T(4,128)S(1)} %bitcast.19, f32[16,128]{1,0:T(8,128)S(1)} %bitcast.18), custom_call_target="tpu_custom_call" | custom-call | tf_op jit(solution)/shard_map/norm/pallas_call | solution.py:381
  (2 shorter events, 0.1 us)
Async XLA Ops:
  0.6 1.0 %copy-start = (bf16[128,2048]{1,0:T(8,128)(2,1)S(1)}, bf16[128,2048]{1,0:T(8,128)(2,1)}, u32[]{:S(2)}) copy-start(bf16[128,2048]{1,0:T(8,128)(2,1)} %key_in.3) | copy-start | bytes 1572868
  1.7 1.0 %copy-start.2 = (bf16[128,2048]{1,0:T(8,128)(2,1)S(1)}, bf16[128,2048]{1,0:T(8,128)(2,1)}, u32[]{:S(2)}) copy-start(bf16[128,2048]{1,0:T(8,128)(2,1)} %value_in.3) | copy-start | bytes 1572868
  2.7 1.0 %copy-start.4 = (bf16[128,2048]{1,0:T(8,128)(2,1)S(1)}, bf16[128,2048]{1,0:T(8,128)(2,1)}, u32[]{:S(2)}) copy-start(bf16[128,2048]{1,0:T(8,128)(2,1)} %query_in.3) | copy-start | bytes 1572868
  3.8 4.7 %copy-start.1 = (bf16[128,2048]{1,0:T(8,128)(2,1)S(1)}, bf16[128,2048]{1,0:T(8,128)(2,1)}, u32[]{:S(2)}) copy-start(bf16[128,2048]{1,0:T(8,128)(2,1)} %key_in.3) | copy-start | bytes 1572868
  3.8 4.7 %copy-start.3 = (bf16[128,2048]{1,0:T(8,128)(2,1)S(1)}, bf16[128,2048]{1,0:T(8,128)(2,1)}, u32[]{:S(2)}) copy-start(bf16[128,2048]{1,0:T(8,128)(2,1)} %value_in.3) | copy-start | bytes 1572868
  3.8 4.7 %copy-start.10 = (f32[16,2048]{1,0:T(8,128)S(1)}, f32[16,2048]{1,0:T(8,128)}, u32[]{:S(2)}) copy-start(f32[16,2048]{1,0:T(8,128)} %decay_rate.1) | copy-start | bytes 393220
  3.8 4.7 %copy-start.14 = (f32[3,3,2048]{2,1,0:T(4,128)S(1)}, f32[3,3,2048]{2,1,0:T(4,128)}, u32[]{:S(2)}) copy-start(f32[3,3,2048]{2,1,0:T(4,128)} %filters.1) | copy-start | bytes 221188
  3.8 8.9 %collective-permute-start = (bf16[6,2048]{1,0:T(8,128)(2,1)S(1)}, bf16[6,2048]{1,0:T(8,128)(2,1)S(1)}, u32[]{:S(2)}, u32[]{:S(2)}) collective-permute-start(bf16[6,2048]{1,0:T(8,128)(2,1)S(1)} %tails.1), channel_id=1, source_target_pairs={{0,4},{4,8},{8,12},{12,16},{16,20},{20,24},{24,28},{28,32},{32,36}... | collective-permute-start | bytes 73736 | tf_op jit(solution)/shard_map/ppermute | solution.py:308
  11.2 1.0 %copy-start.6 = (f32[2048,128]{1,0:T(8,128)}, f32[2048,128]{1,0:T(8,128)S(1)}, u32[]{:S(2)}) copy-start(f32[2048,128]{1,0:T(8,128)S(1)} %get-tuple-element.23.mixed) | copy-start | bytes 3145732
  13.5 11.3 %all-to-all-start = ((bf16[8,32,128]{2,1,0:T(8,128)(2,1)}), bf16[8,32,128]{2,1,0:T(8,128)(2,1)S(1)}, u32[]{:S(2)}, u32[]{:S(2)}) async-start(bf16[8,32,128]{2,1,0:T(8,128)(2,1)} %bitcast.1), calls=%async_computation | async-start | bytes 131072 | tf_op jit(solution)/shard_map/all_to_all | solution.py:338
  24.7 26.7 %copy-start.5 = (bf16[128,2048]{1,0:T(8,128)(2,1)S(1)}, bf16[128,2048]{1,0:T(8,128)(2,1)}, u32[]{:S(2)}) copy-start(bf16[128,2048]{1,0:T(8,128)(2,1)} %query_in.3) | copy-start | bytes 1572868
  41.0 10.4 %copy-start.15 = (f32[2048]{0:T(1024)S(1)}, f32[2048]{0:T(1024)}, u32[]{:S(2)}) copy-start(f32[2048]{0:T(1024)} %param.16) | copy-start | bytes 24580
  41.0 20.5 %all-to-all-start.2 = ((bf16[16,32,128]{2,1,0:T(8,128)(2,1)}), bf16[16,32,128]{2,1,0:T(8,128)(2,1)S(1)}, u32[]{:S(2)}, u32[]{:S(2)}) async-start(bf16[16,32,128]{2,1,0:T(8,128)(2,1)} %bitcast.5), calls=%async_computation.2 | async-start | bytes 262144 | tf_op jit(solution)/shard_map/all_to_all | solution.py:338
  51.4 1.2 %copy-start.7 = (f32[2048,128]{1,0:T(8,128)S(1)}, f32[2048,128]{1,0:T(8,128)}, u32[]{:S(2)}) copy-start(f32[2048,128]{1,0:T(8,128)} %copy-done.6) | copy-start | bytes 3145732
  52.6 0.9 %copy-start.13 = (f32[16,2048]{1,0:T(8,128)S(1)}, f32[16,2048]{1,0:T(8,128)}, u32[]{:S(2)}) copy-start(f32[16,2048]{1,0:T(8,128)} %residue.1) | copy-start | bytes 393220
  53.5 8.0 %copy-start.9 = (bf16[128,2048]{1,0:T(8,128)(2,1)S(1)}, bf16[128,2048]{1,0:T(8,128)(2,1)}, u32[]{:S(2)}) copy-start(bf16[128,2048]{1,0:T(8,128)(2,1)} %residual.1) | copy-start | bytes 1572868
  57.0 0.7 copy-start.11
  61.5 0.9 %copy-start.12 = (f32[256,128]{1,0:T(8,128)S(1)}, f32[256,128]{1,0:T(8,128)}, u32[]{:S(2)}) copy-start(f32[256,128]{1,0:T(8,128)} %copy-done.11) | copy-start | bytes 393220
  64.9 9.2 %copy-start.16 = (f32[2048]{0:T(1024)S(1)}, f32[2048]{0:T(1024)}, u32[]{:S(2)}) copy-start(f32[2048]{0:T(1024)} %param.17) | copy-start | bytes 24580
  74.0 1.0 %copy-start.8 = (bf16[128,2048]{1,0:T(8,128)(2,1)S(1)}, bf16[128,2048]{1,0:T(8,128)(2,1)}, u32[]{:S(2)}) copy-start(bf16[128,2048]{1,0:T(8,128)(2,1)} %get-tuple-element.14.summed) | copy-start | bytes 1572868

commit v2 on v0

v2 whole, which is shorter than its diff:
```python
import functools

import jax
import jax.numpy as jnp
from jax import lax
from jax.experimental import pallas as pl
from jax.experimental.pallas import tpu as pltpu
from jax.sharding import PartitionSpec as P


D = 8192
EPSILON = 1e-06
LANES = 128
SUBLANES = 8
MINOR = 8
MIDDLE = 8
MAJOR = 2
STEP = 6
HALO = 2
RAW = 8

f32 = jnp.float32
bf16 = jnp.bfloat16

POLES = 16


def call(kernel, out_shape, scratch=(), room=50, **extra):
    limit = int((64 - room) * 1024) << 10
    return pl.pallas_call(
        kernel,
        out_shape=out_shape,
        scratch_shapes=scratch,
        compiler_params=pltpu.CompilerParams(vmem_limit_bytes=limit),
        **extra,
    )


def spread(source, target, first, columns, groups):
    items = source.shape[0]
    for g in columns:
        target[pl.ds(first * groups + g, items, stride=groups), :] = source[
            :, g * LANES : (g + 1) * LANES
        ].astype(f32)


def start_of(item, half, groups):
    start = item * groups + half * SUBLANES
    return start if isinstance(start, int) else pl.multiple_of(start, SUBLANES)


def tile(ref, item, half, groups):
    return ref[pl.ds(start_of(item, half, groups), SUBLANES), :]


def put(ref, item, half, groups, value):
    ref[pl.ds(start_of(item, half, groups), SUBLANES), :] = value


def poled(item, half, stride=POLES):
    return pl.ds(half * SUBLANES * stride + item, SUBLANES, stride=stride)


def halves_of(tables):
    rows = tables.shape[0] // 2
    return tables.at[:rows], tables.at[rows:]


def taps_of(taps, which, half):
    return [taps[poled(which * 3 + lag, half), :] for lag in range(3)]


def fir(taps, now, last, older):
    return taps[0] * now + taps[1] * last + taps[2] * older


def first_kernel(
    query_in, key_in, value_in, filters_in, decay_in, parcel, tails, tables,
    key, value, query, filters, decay, keys, values, states, sem,
):
    tokens, chans = key.shape
    groups = chans // LANES
    halves = groups // SUBLANES
    width = SUBLANES * LANES

    def part(source, target, half, slot):
        columns = slice(half * width, (half + 1) * width)
        return pltpu.make_async_copy(source.at[:, columns], target.at[:, columns], sem.at[slot])

    small = [
        pltpu.make_async_copy(decay_in, decay, sem.at[0]),
        pltpu.make_async_copy(filters_in, filters, sem.at[1]),
        pltpu.make_async_copy(query_in.at[tokens - 8 : tokens, :], query, sem.at[2]),
    ]
    large = [
        (part(key_in, key, h, 3 + 2 * h), part(value_in, value, h, 4 + 2 * h))
        for h in range(halves)
    ]
    small[0].start()
    small[1].start()
    for pair in large:
        pair[0].start()
        pair[1].start()
    small[2].start()
    small[0].wait()
    small[1].wait()
    rates, taps = halves_of(tables)
    for g in range(groups):
        columns = slice(g * LANES, (g + 1) * LANES)
        rates[g * POLES : (g + 1) * POLES, :] = decay[:, columns]
        for which in range(3):
            start = g * POLES + 3 * which
            taps[start : start + 3, :] = filters[which, :, columns]
        taps[g * POLES + 9 : (g + 1) * POLES, :] = jnp.zeros((POLES - 9, LANES), f32)
    for half in range(halves):
        factor = [jnp.exp(-rates[poled(n, half), :]) for n in range(POLES)]
        key_taps = taps_of(taps, 1, half)
        value_taps = taps_of(taps, 2, half)
        for copy in large[half]:
            copy.wait()
        columns = range(half * SUBLANES, (half + 1) * SUBLANES)
        spread(key, keys, 0, columns, groups)
        spread(value, values, 0, columns, groups)

        def turn(i, carry):
            k1, k2, v1, v2, *state = carry
            for u in range(STEP):
                t = HALO + i * STEP + u
                k0 = tile(keys, t, half, groups)
                v0 = tile(values, t, half, groups)
                m = fir(key_taps, k0, k1, k2) * fir(value_taps, v0, v1, v2)
                state = [factor[n] * state[n] + m for n in range(POLES)]
                k1, k2, v1, v2 = k0, k1, v0, v1
            return (k1, k2, v1, v2, *state)

        begin = tuple(tile(x, t, half, groups) for x in (keys, values) for t in (1, 0))
        begin += (jnp.zeros((SUBLANES, LANES), f32),) * POLES
        end = lax.fori_loop(0, (tokens - HALO) // STEP, turn, begin)
        for n in range(POLES):
            states[poled(n, half), :] = end[4 + n]
    small[2].wait()
    ends = [(x[:16, :].astype(f32)[:2], x[tokens - 16 :, :].astype(f32)[-2:]) for x in (key, value)]
    raw = jnp.concatenate([*ends[0], *ends[1]], axis=0)
    tails[...] = jnp.concatenate(
        [query[...].astype(f32)[-2:], ends[0][1], ends[1][1]], axis=0
    ).astype(bf16)
    each = groups // MINOR
    rows = each * (POLES + RAW)
    for j in range(MINOR):
        pieces = [raw[:, g * LANES : (g + 1) * LANES] for g in range(each * j, each * (j + 1))]
        parcel[j * rows : j * rows + each * POLES, :] = states[
            each * POLES * j : each * POLES * (j + 1), :
        ].astype(bf16)
        parcel[j * rows + each * POLES : (j + 1) * rows, :] = jnp.concatenate(
            pieces, axis=0
        ).astype(bf16)


def opening_of(tap, head, tail):
    result = [[], []]
    for g in range(head.shape[0] // RAW):
        pair = [[], []]
        for side in range(2):
            weight = [
                tap[g * POLES + 3 + 3 * side + lag : g * POLES + 4 + 3 * side + lag, :]
                for lag in range(3)
            ]
            at = g * RAW + 4 * side
            line = [tail[at + 2 + r : at + 3 + r, :] for r in range(2)]
            line += [head[at + r : at + 1 + r, :] for r in range(2)]
            for t in range(2):
                pair[t].append(fir(weight, line[t + 2], line[t + 1], line[t]))
        for t in range(2):
            m = pair[t][0] * pair[t][1]
            result[t].append(jnp.broadcast_to(m, (POLES, LANES)))
    return [jnp.concatenate(x, axis=0) for x in result]


def piece_of(ref, place, rows):
    return ref[pl.ds(pl.multiple_of((place[0] % MINOR) * rows, SUBLANES), rows), :]


def is_head(shape):
    return (lax.broadcasted_iota(jnp.int32, shape, 0) & 2) == 0


def minor_kernel(block, place, arrived, tables, sums, prefix):
    rates, taps = halves_of(tables)
    size = arrived.shape[0] // MINOR
    rows = rates.shape[0] // MINOR
    rate = piece_of(rates, place, rows)
    tap = piece_of(taps, place, rows)
    decay = jnp.exp(-rate * block)
    late = [jnp.exp(-rate * (block - 1.0)), jnp.exp(-rate * (block - 2.0))]
    total = jnp.zeros((rows, LANES), f32)
    raw = []
    for b in range(MINOR):
        prefix[b * rows : (b + 1) * rows, :] = total
        total = decay * total + arrived[b * size : b * size + rows, :].astype(f32)
        raw.append(arrived[b * size + rows : (b + 1) * size, :].astype(f32))
        if b:
            m = opening_of(tap, raw[b], raw[b - 1])
            total = total + (late[0] * m[0] + late[1] * m[1])
    ends = jnp.where(is_head(raw[0].shape), raw[0], raw[-1]).astype(bf16)
    total = total.astype(bf16)
    for other in range(MIDDLE):
        sums[other * size : other * size + rows, :] = total
        sums[other * size + rows : (other + 1) * size, :] = ends


def middle_kernel(block, place, arrived, tables, prefix, carries):
    rates, taps = halves_of(tables)
    size = arrived.shape[0] // MIDDLE
    rows = rates.shape[0] // MINOR
    rate = piece_of(rates, place, rows)
    tap = piece_of(taps, place, rows)
    mine = (place[0] // MINOR) % MIDDLE
    lower = place[0] < MINOR * MIDDLE
    decay = jnp.exp(-rate * block)
    line_decay = jnp.exp(-rate * (block * MINOR))
    rest_decay = jnp.exp(-rate * (block * (MINOR - 1)))
    late = [jnp.exp(-rate * (block - 1.0)), jnp.exp(-rate * (block - 2.0))]
    before = jnp.zeros((rows, LANES), f32)
    whole = jnp.zeros((rows, LANES), f32)
    own = jnp.zeros((rows, LANES), f32)
    raw = []
    for other in range(MIDDLE):
        raw.append(arrived[other * size + rows : (other + 1) * size, :].astype(f32))
        last = raw[other - 1] if other else jnp.zeros_like(raw[0])
        m = opening_of(tap, raw[other], last)
        opening = late[0] * m[0] + late[1] * m[1]
        if not other:
            opening = jnp.where(lower, opening, 0.0)
        piece = arrived[other * size : other * size + rows, :].astype(f32)
        whole = line_decay * whole + (piece + rest_decay * opening)
        before = jnp.where(other < mine, whole, before)
        own = jnp.where(other == mine, opening, own)
    onward = jnp.exp(-rate * (mine.astype(f32) * (block * MINOR))) * whole
    head = is_head(raw[0].shape)
    ends = jnp.where(
        lower, jnp.where(head, 0.0, raw[-1]), jnp.where(head, raw[0], 0.0)
    )
    half = MINOR * size
    for b in range(MINOR):
        here = before + prefix[b * rows : (b + 1) * rows, :]
        if b:
            here = here + own
            own = decay * own
        send = jnp.where(mine + b > 0, ends, 0.0)
        at = b * size
        carries[at : at + rows, :] = jnp.where(lower, here, 0.0).astype(bf16)
        carries[at + rows : at + size, :] = jnp.zeros((size - rows, LANES), bf16)
        at += half
        carries[at : at + rows, :] = jnp.where(lower, onward, here).astype(bf16)
        carries[at + rows : at + size, :] = send.astype(bf16)
        before = decay * before
        onward = decay * onward


def inner_kernel(
    query_hbm, key_hbm, value_hbm, residual_hbm, residue_hbm, tails, tables, skip,
    base, query, lead, query_in, key_in, value_in, residual, residue,
    queries, keys, values, streams, weights, sem,
):
    tokens, chans = query_in.shape
    groups = chans // LANES
    every = range(groups)
    rates, taps = halves_of(tables)
    sources = (query_hbm, key_hbm, value_hbm, residual_hbm, residue_hbm)
    targets = (query_in, key_in, value_in, residual, residue)
    copies = [
        pltpu.make_async_copy(source, target, sem.at[i])
        for i, (source, target) in enumerate(zip(sources, targets, strict=True))
    ]
    for copy in copies:
        copy.start()
    for copy in copies:
        copy.wait()
    ends = tails[...].astype(f32)
    for which, (source, target) in enumerate(
        ((query_in, queries), (key_in, keys), (value_in, values))
    ):
        spread(ends[2 * which : 2 * which + 2], target, 0, every, groups)
        spread(source, target, HALO, every, groups)
    spread(residual, streams, 0, every, groups)
    for g in every:
        weights[g * POLES : (g + 1) * POLES, :] = residue[:, g * LANES : (g + 1) * LANES]
    for half in range(groups // SUBLANES):
        taps_here = [taps_of(taps, which, half) for which in range(3)]
        sources = (queries, keys, values)

        def filtered(i, carry):
            carry = list(carry)
            for u in range(4):
                t = i * 4 + u
                now = [tile(x, t + HALO, half, groups) for x in sources]
                out = [fir(taps_here[w], now[w], carry[2 * w], carry[2 * w + 1]) for w in range(3)]
                put(query, t, half, groups, out[0])
                put(keys, t, half, groups, out[1] * out[2])
                for w in range(3):
                    carry[2 * w + 1], carry[2 * w] = carry[2 * w], now[w]
            return tuple(carry)

        begin = tuple(tile(x, t, half, groups) for x in sources for t in (1, 0))
        lax.fori_loop(0, tokens // 4, filtered, begin)

        factor, weight = [], []
        for n in range(POLES):
            rate = rates[poled(n, half), :]
            factor.append(jnp.exp(-rate))
            weight.append(weights[poled(n, half), :] * jnp.sqrt(2.0 * rate))
            put(lead, n, half, groups, weight[n] * factor[n])
        direct = tile(skip, 0, half, groups)

        def turn(i, state):
            for u in range(8):
                t = i * 8 + u
                m = tile(keys, t, half, groups)
                state = [factor[n] * state[n] + m for n in range(POLES)]
                parts = [direct * m, weight[0] * state[0]]
                for n in range(1, POLES):
                    parts[n % 2] = parts[n % 2] + weight[n] * state[n]
                gated = tile(query, t, half, groups) * (parts[0] + parts[1])
                put(base, t, half, groups, tile(streams, t, half, groups) + gated)
            return tuple(state)

        lax.fori_loop(0, tokens // 8, turn, (jnp.zeros((SUBLANES, LANES), f32),) * POLES)


def outer_kernel(
    block, place, carries, tables, lead, query_hbm, base_hbm, summed, squares,
    carried, raw, query, gated, sem,
):
    tokens, chans = summed.shape
    groups = chans // LANES
    each = groups // MINOR
    size = each * (POLES + RAW)
    rows = each * POLES
    rates, taps = halves_of(tables)
    parts = sem.shape[0] // 2
    span = tokens // parts
    copies = []
    for p in range(parts):
        part = slice(p * span * groups, (p + 1) * span * groups)
        for i, (source, target) in enumerate(((query_hbm, query), (base_hbm, gated))):
            copies.append(
                pltpu.make_async_copy(source.at[part, :], target.at[part, :], sem.at[2 * p + i])
            )
            copies[-1].start()
    for j in range(MINOR):
        at, more = j * size, (MINOR + j) * size
        both = carries[at : at + size, :].astype(f32) + carries[more : more + size, :].astype(f32)
        carried[j * rows : (j + 1) * rows, :] = both[:rows]
        raw[j * each * RAW : (j + 1) * each * RAW, :] = both[rows:]
    away = (place[0] % (MINOR * MIDDLE)).astype(f32) * block - 2.0
    for half in range(groups // SUBLANES):
        pair = [[], []]
        for side in range(2):
            weight = taps_of(taps, 1 + side, half)
            line = [raw[poled(4 * side + r, half, RAW), :] for r in (2, 3, 0, 1)]
            for t in range(2):
                pair[t].append(fir(weight, line[t + 2], line[t + 1], line[t]))
        opening = [p[0] * p[1] for p in pair]
        factor, state = [], []
        for n in range(POLES):
            rate = rates[poled(n, half), :]
            factor.append(jnp.exp(-rate))
            entering = carried[poled(n, half), :] + jnp.exp(-rate * away) * (
                factor[n] * opening[0] + opening[1]
            )
            state.append(tile(lead, n, half, groups) * entering)

        def turn(i, state):
            for u in range(8):
                t = i * 8 + u
                sums = [state[0], state[1]]
                for n in range(2, POLES):
                    sums[n % 2] = sums[n % 2] + state[n]
                added = tile(query, t, half, groups) * (sums[0] + sums[1])
                put(gated, t, half, groups, tile(gated, t, half, groups) + added)
                state = [factor[n] * state[n] for n in range(POLES)]
            return tuple(state)

        state = tuple(state)
        for p in range(parts):
            if half == 0:
                copies[2 * p].wait()
                copies[2 * p + 1].wait()
            state = lax.fori_loop(p * span // 8, (p + 1) * span // 8, turn, state)
    total = jnp.zeros((tokens, LANES), f32)
    for g in range(groups):
        value = gated[pl.ds(g, tokens, stride=groups), :].astype(bf16)
        summed[:, g * LANES : (g + 1) * LANES] = value
        value = value.astype(f32)
        total = total + value * value
    squares[...] = jnp.broadcast_to(jnp.sum(total.T, axis=0, keepdims=True), squares.shape)


def norm_kernel(summed, squares, gain, stream_out, normed_out, normed, sem):
    tokens, chans = summed.shape
    parts = 4
    width = chans // parts
    stream = pltpu.make_async_copy(summed, stream_out, sem.at[parts])
    stream.start()
    mean = jnp.sum(squares[...], axis=0, keepdims=True) / D
    inverse = jnp.broadcast_to(lax.rsqrt(mean + EPSILON), (LANES, tokens)).T
    copies = []
    for part in range(parts):
        for g in range(part * width // LANES, (part + 1) * width // LANES):
            columns = slice(g * LANES, (g + 1) * LANES)
            normed[:, columns] = (
                summed[:, columns].astype(f32) * inverse * gain[g : g + 1, :]
            ).astype(bf16)
        columns = slice(part * width, (part + 1) * width)
        copies.append(
            pltpu.make_async_copy(normed.at[:, columns], normed_out.at[:, columns], sem.at[part])
        )
        copies[part].start()
    for copy in copies:
        copy.wait()
    stream.wait()


def layer(
    residual, query_in, key_in, value_in, short_filter, decay_rate, residue, skip_gain, norm_gain
):
    tokens, chans = residual.shape
    groups = chans // LANES
    count = MINOR * MIDDLE * MAJOR
    block = float(tokens)

    def shape(rows, kind=f32):
        return jax.ShapeDtypeStruct((rows, LANES), kind)

    def hold(rows):
        return pltpu.VMEM((rows, LANES), f32)

    smem = pl.BlockSpec(memory_space=pltpu.SMEM)
    vmem = pl.BlockSpec(memory_space=pltpu.VMEM)
    hbm = pl.BlockSpec(memory_space=pltpu.HBM)
    wide = pltpu.VMEM((tokens, chans), bf16)
    poled_rows = POLES * groups
    parcel_rows = (POLES + RAW) * groups

    parcel, tails, tables = call(
        first_kernel,
        (
            shape(parcel_rows, bf16),
            jax.ShapeDtypeStruct((6, chans), bf16),
            shape(2 * poled_rows),
        ),
        room=10.25,
        in_specs=[hbm] * 5,
        scratch=[
            wide,
            wide,
            pltpu.VMEM((8, chans), bf16),
            pltpu.VMEM(short_filter.shape, f32),
            pltpu.VMEM(decay_rate.shape, f32),
            hold(tokens * groups),
            hold(tokens * groups),
            hold(poled_rows),
            pltpu.SemaphoreType.DMA((3 + 2 * (groups // SUBLANES),)),
        ],
    )(query_in, key_in, value_in, short_filter, decay_rate)

    place = lax.axis_index("seq").astype(jnp.int32).reshape(1)
    lines = [[g * MINOR + j for j in range(MINOR)] for g in range(MIDDLE * MAJOR)]
    planes = [
        [(z * MIDDLE + y) * MINOR + j for y in range(MIDDLE)]
        for z in range(MAJOR)
        for j in range(MINOR)
    ]
    pairs = [
        [(z * MIDDLE + y) * MINOR + j for z in range(MAJOR) for j in range(MINOR)]
        for y in range(MIDDLE)
    ]

    def exchange(x, members):
        return lax.all_to_all(x, "seq", 0, 0, axis_index_groups=members, tiled=True)

    arrived = exchange(parcel, lines)
    tails = lax.ppermute(tails, "seq", [(i, i + 1) for i in range(count - 1)])
    sums, prefix = call(
        functools.partial(minor_kernel, block),
        (shape(parcel_rows, bf16), shape(poled_rows)),
        in_specs=[smem, vmem, vmem],
    )(place, arrived, tables)
    arrived = exchange(sums, planes)
    carries = call(
        functools.partial(middle_kernel, block),
        shape(MAJOR * parcel_rows, bf16),
        in_specs=[smem, vmem, vmem, vmem],
    )(place, arrived, tables, prefix)
    base, query, lead = call(
        inner_kernel,
        (shape(tokens * groups),) * 2 + (shape(poled_rows),),
        room=11.5,
        in_specs=[hbm] * 5 + [vmem] * 3,
        scratch=[
            wide,
            wide,
            wide,
            wide,
            pltpu.VMEM(residue.shape, f32),
            hold((tokens + HALO) * groups),
            hold((tokens + HALO) * groups),
            hold((tokens + HALO) * groups),
            hold(tokens * groups),
            hold(poled_rows),
            pltpu.SemaphoreType.DMA((5,)),
        ],
    )(
        query_in,
        key_in,
        value_in,
        residual,
        residue,
        tails,
        tables,
        skip_gain.reshape(groups, LANES),
    )
    carries = exchange(carries, pairs)
    members = lax.axis_size("chan")
    summed, squares = call(
        functools.partial(outer_kernel, block),
        (
            jax.ShapeDtypeStruct((tokens, chans), bf16),
            jax.ShapeDtypeStruct((members, tokens), f32),
        ),
        room=11.5,
        in_specs=[smem] + [vmem] * 3 + [hbm] * 2,
        scratch=[
            hold(poled_rows),
            hold(RAW * groups),
            hold(tokens * groups),
            hold(tokens * groups),
            pltpu.SemaphoreType.DMA((8,)),
        ],
    )(place, carries, tables, lead, query, base)
    squares = lax.all_to_all(squares, "chan", 0, 0, tiled=True)
    whole = jax.ShapeDtypeStruct((tokens, chans), bf16)
    return call(
        norm_kernel,
        (whole, whole),
        in_specs=[vmem] * 3,
        out_specs=(hbm, hbm),
        scratch=[wide, pltpu.SemaphoreType.DMA((5,))],
    )(summed, squares, norm_gain.reshape(groups, LANES))


def solution(mesh):
    whole = P("seq", "chan")
    in_specs = (whole, whole, whole, whole, P(None, None, "chan"))
    in_specs += (P(None, "chan"), P(None, "chan"), P("chan"), P("chan"))
    return jax.shard_map(
        layer, mesh=mesh, in_specs=in_specs, out_specs=(whole, whole), check_vma=False
    )
```

time: 230 us -> 77.2 us (0.34)
  the two profiles are of different devices: /device:TPU:1 before, /device:TPU:256 now
where the time goes in v2:
time: 77.2 us; the launch traced here: 76.7 us
  blocking collectives  25.2 us (33%)
  Pallas kernels  18 us (23%)
  waiting for transfers between devices  17.5 us (23%)
  starting transfers between devices  14.3 us (19%)
  local copies, waits for them, and re-layouts  0.97 us (1%)
    all_to_all x1, blocking collectives, exchange(): return lax.all_to_all(x, 'seq', 0, 0, axis_index_groups=members, tiled=True)  15.6 us
    all_to_all x2, starting transfers between devices, exchange(): return lax.all_to_all(x, 'seq', 0, 0, axis_index_groups=members, tiled=True)  12.3 us
    ppermute x1, waiting for transfers between devices, layer(): tails = lax.ppermute(tails, 'seq', [(i, i + 1) for i in range(count - 1)])  11.7 us
    all_to_all x1, blocking collectives, layer(): squares = lax.all_to_all(squares, 'chan', 0, 0, tiled=True)  9.61 us
    pallas_call x1, Pallas kernels, layer(): call(inner_kernel, (shape(tokens * groups),) * 2 + (shape(poled_rows),),...  8.41 us
    all_to_all x2, waiting for transfers between devices, exchange(): return lax.all_to_all(x, 'seq', 0, 0, axis_index_groups=members, tiled=True)  5.8 us
    pallas_call x1, Pallas kernels, layer(): call(first_kernel, (shape(parcel_rows, bf16), jax.ShapeDtypeStruct((6, ch...  4.71 us
    pallas_call x1, Pallas kernels, layer(): call(functools.partial(outer_kernel, block), (jax.ShapeDtypeStruct((token...  2.9 us
  transfers between devices with their start and end apart: 3, of which 2 were waited for; matrix products, arithmetic and copies ran while one was open for 0% of the time, Pallas kernels for 11%

profile of v2, /device:TPU:256, one launch (start us, length us, event | category | flops | bytes accessed | tf_op | source)
XLA Modules:
  0.0 76.7 jit_solution(15861990002274201609)
XLA Ops:
  0.6 4.7 %shard_map.104 = (bf16[384,128]{1,0:T(8,128)(2,1)}, bf16[6,2048]{1,0:T(8,128)(2,1)S(1)}, f32[512,128]{1,0:T(8,128)}) custom-call(bf16[128,2048]{1,0:T(8,128)(2,1)} %query_hbm.1, bf16[128,2048]{1,0:T(8,128)(2,1)} %key_hbm.1, bf16[128,2048]{1,0:T(8,128)(2,1)} %value_hbm.1, f32[3,3,2048]{2,1,0:T(4,128)} %filters_in.1, f32[16,2048]{1,0:T(8,128)} %decay_in.1), custom_call_target="tpu_custom_call" | custom-call | tf_op jit(solution)/shard_map/pallas_call | solution.py:445
  5.3 4.3 %all-to-all-start = ((bf16[8,48,128]{2,1,0:T(8,128)(2,1)}), bf16[8,48,128]{2,1,0:T(8,128)(2,1)S(1)}, u32[]{:S(2)}, u32[]{:S(2)}) async-start(bf16[8,48,128]{2,1,0:T(8,128)(2,1)} %bitcast.1), calls=%async_computation | async-start | bytes 196608 | tf_op jit(solution)/shard_map/all_to_all | solution.py:480
  9.7 5.8 %all-to-all-done = bf16[8,48,128]{2,1,0:T(8,128)(2,1)S(1)} async-done(((bf16[8,48,128]{2,1,0:T(8,128)(2,1)}), bf16[8,48,128]{2,1,0:T(8,128)(2,1)S(1)}, u32[]{:S(2)}, u32[]{:S(2)}) %all-to-all-start) | async-done | bytes 98336 | tf_op jit(solution)/shard_map/all_to_all | solution.py:480
  15.5 0.0 copy-start
  15.5 0.9 %copy-done = f32[512,128]{1,0:T(8,128)S(1)} copy-done((f32[512,128]{1,0:T(8,128)S(1)}, f32[512,128]{1,0:T(8,128)}, u32[]{:S(2)}) %copy-start) | copy-done | bytes 262168
  16.4 0.1 shard_map.105
  16.5 15.6 %all_to_all.44 = bf16[8,48,128]{2,1,0:T(8,128)(2,1)S(1)} all-to-all(bf16[8,48,128]{2,1,0:T(8,128)(2,1)S(1)} %bitcast.16), channel_id=1, replica_groups={{0,32,64,96,128,160,192,224},{4,36,68,100,132,164,196,228},{8,40,72,104..., dimensions={0} | all-to-all | bytes 196608 | tf_op jit(solution)/shard_map/all_to_all | solution.py:480
  32.2 0.0 copy-start.2
  32.2 0.0 copy-start.4
  32.2 0.9 %shard_map.106 = bf16[768,128]{1,0:T(8,128)(2,1)} custom-call(s32[1]{0:T(128)} %bitcast.place, bf16[384,128]{1,0:T(8,128)(2,1)S(1)} %bitcast.14, f32[512,128]{1,0:T(8,128)S(1)} %copy-done, f32[256,128]{1,0:T(8,128)S(1)} %get-tuple-element.15.prefix), custom_call_target="tpu_custom_call" | custom-call | tf_op jit(solution)/shard_map/pallas_call | solution.py:490
  33.0 0.0 copy-start.1
  33.0 0.0 copy-start.3
  33.0 8.0 %all-to-all-start.2 = ((bf16[16,48,128]{2,1,0:T(8,128)(2,1)}), bf16[16,48,128]{2,1,0:T(8,128)(2,1)S(1)}, u32[]{:S(2)}, u32[]{:S(2)}) async-start(bf16[16,48,128]{2,1,0:T(8,128)(2,1)} %bitcast.5), calls=%async_computation.2 | async-start | bytes 393216 | tf_op jit(solution)/shard_map/all_to_all | solution.py:480
  41.0 2.0 %collective-permute-start = (bf16[6,2048]{1,0:T(8,128)(2,1)S(1)}, bf16[6,2048]{1,0:T(8,128)(2,1)S(1)}, u32[]{:S(2)}, u32[]{:S(2)}) collective-permute-start(bf16[6,2048]{1,0:T(8,128)(2,1)S(1)} %get-tuple-element.16), channel_id=1, source_target_pairs={{0,4},{4,8},{8,12},{12,16},{16,20},{20,24},{24,28},{28,32},{32,36}... | collective-permute-start | bytes 73736 | tf_op jit(solution)/shard_map/ppermute | solution.py:483
  43.0 11.7 %collective-permute-done.tails = bf16[6,2048]{1,0:T(8,128)(2,1)S(1)} collective-permute-done((bf16[6,2048]{1,0:T(8,128)(2,1)S(1)}, bf16[6,2048]{1,0:T(8,128)(2,1)S(1)}, u32[]{:S(2)}, u32[]{:S(2)}) %collective-permute-start) | collective-permute-done | bytes 24608 | tf_op jit(solution)/shard_map/ppermute | solution.py:483
  54.6 0.0 copy-done.2
  54.7 0.0 copy-done.4
  54.7 0.0 copy-done.1
  54.7 0.0 copy-done.3
  54.7 8.4 %shard_map.107 = (f32[2048,128]{1,0:T(8,128)}, f32[2048,128]{1,0:T(8,128)}, f32[256,128]{1,0:T(8,128)S(1)}) custom-call(bf16[128,2048]{1,0:T(8,128)(2,1)S(1)} %copy-done.2, bf16[128,2048]{1,0:T(8,128)(2,1)} %key_hbm.1, bf16[128,2048]{1,0:T(8,128)(2,1)} %value_hbm.1, bf16[128,2048]{1,0:T(8,128)(2,1)} %residual_hbm.1, f32[16,2048]{1,0:T(8,128)S(1)} %copy-done.3, ...), custom_call_target="tpu_custom_call" | custom-call | tf_op jit(solution)/shard_map/pallas_call | solution.py:495
  63.1 0.0 all-to-all-done.2
  63.1 2.9 %shard_map.108 = (bf16[128,2048]{1,0:T(8,128)(2,1)S(1)}, f32[4,128]{1,0:T(4,128)S(1)}) custom-call(s32[1]{0:T(128)} %bitcast.place, bf16[768,128]{1,0:T(8,128)(2,1)S(1)} %bitcast.13, f32[512,128]{1,0:T(8,128)S(1)} %copy-done.1, f32[256,128]{1,0:T(8,128)S(1)} %get-tuple-element.17.lead, f32[2048,128]{1,0:T(8,128)} %get-tuple-element.18.query_hbm, ...), custom_call_target="tpu_custom_call" | custom-call | tf_op jit(solution)/shard_map/pallas_call | solution.py:525
  66.0 0.0 copy-start.5
  66.0 9.6 %all_to_all.45 = f32[4,1,128]{2,1,0:T(1,128)S(1)} all-to-all(f32[4,1,128]{2,1,0:T(1,128)S(1)} %bitcast.20), channel_id=1, replica_groups=mesh['seq'=128,'chan'=4] {'chan'}, dimensions={0} | all-to-all | bytes 4096 | tf_op jit(solution)/shard_map/all_to_all | solution.py:541
  75.6 0.0 copy-done.5
  75.6 1.0 %shard_map.109 = (bf16[128,2048]{1,0:T(8,128)(2,1)}, bf16[128,2048]{1,0:T(8,128)(2,1)}) custom-call(bf16[128,2048]{1,0:T(8,128)(2,1)S(1)} %get-tuple-element.20.summed, f32[4,128]{1,0:T(4,128)S(1)} %bitcast.19, f32[16,128]{1,0:T(8,128)S(1)} %bitcast.18), custom_call_target="tpu_custom_call" | custom-call | tf_op jit(solution)/shard_map/pallas_call | solution.py:543
Async XLA Ops:
  5.3 10.1 %all-to-all-start = ((bf16[8,48,128]{2,1,0:T(8,128)(2,1)}), bf16[8,48,128]{2,1,0:T(8,128)(2,1)S(1)}, u32[]{:S(2)}, u32[]{:S(2)}) async-start(bf16[8,48,128]{2,1,0:T(8,128)(2,1)} %bitcast.1), calls=%async_computation | async-start | bytes 196608 | tf_op jit(solution)/shard_map/all_to_all | solution.py:480
  15.5 1.0 %copy-start = (f32[512,128]{1,0:T(8,128)S(1)}, f32[512,128]{1,0:T(8,128)}, u32[]{:S(2)}) copy-start(f32[512,128]{1,0:T(8,128)} %get-tuple-element.13.tables) | copy-start | bytes 786436
  32.2 22.5 %copy-start.2 = (bf16[128,2048]{1,0:T(8,128)(2,1)S(1)}, bf16[128,2048]{1,0:T(8,128)(2,1)}, u32[]{:S(2)}) copy-start(bf16[128,2048]{1,0:T(8,128)(2,1)} %query_hbm.1) | copy-start | bytes 1572868
  32.2 22.5 %copy-start.4 = (f32[2048]{0:T(1024)S(1)}, f32[2048]{0:T(1024)}, u32[]{:S(2)}) copy-start(f32[2048]{0:T(1024)} %param.16) | copy-start | bytes 24580
  33.0 21.6 %copy-start.1 = (f32[512,128]{1,0:T(8,128)S(1)}, f32[512,128]{1,0:T(8,128)}, u32[]{:S(2)}) copy-start(f32[512,128]{1,0:T(8,128)} %get-tuple-element.13.tables) | copy-start | bytes 786436
  33.0 21.7 %copy-start.3 = (f32[16,2048]{1,0:T(8,128)S(1)}, f32[16,2048]{1,0:T(8,128)}, u32[]{:S(2)}) copy-start(f32[16,2048]{1,0:T(8,128)} %residue_hbm.1) | copy-start | bytes 393220
  33.0 30.1 %all-to-all-start.2 = ((bf16[16,48,128]{2,1,0:T(8,128)(2,1)}), bf16[16,48,128]{2,1,0:T(8,128)(2,1)S(1)}, u32[]{:S(2)}, u32[]{:S(2)}) async-start(bf16[16,48,128]{2,1,0:T(8,128)(2,1)} %bitcast.5), calls=%async_computation.2 | async-start | bytes 393216 | tf_op jit(solution)/shard_map/all_to_all | solution.py:480
  41.0 13.7 %collective-permute-start = (bf16[6,2048]{1,0:T(8,128)(2,1)S(1)}, bf16[6,2048]{1,0:T(8,128)(2,1)S(1)}, u32[]{:S(2)}, u32[]{:S(2)}) collective-permute-start(bf16[6,2048]{1,0:T(8,128)(2,1)S(1)} %get-tuple-element.16), channel_id=1, source_target_pairs={{0,4},{4,8},{8,12},{12,16},{16,20},{20,24},{24,28},{28,32},{32,36}... | collective-permute-start | bytes 73736 | tf_op jit(solution)/shard_map/ppermute | solution.py:483
  66.0 9.6 %copy-start.5 = (f32[2048]{0:T(1024)S(1)}, f32[2048]{0:T(1024)}, u32[]{:S(2)}) copy-start(f32[2048]{0:T(1024)} %param.17) | copy-start | bytes 24580

commit v3 on v2

--- a/solution.py
+++ b/solution.py
@@ -74,9 +74,20 @@
     return taps[0] * now + taps[1] * last + taps[2] * older
 
 
+def fill_tables(filters, decay, rates, taps):
+    groups = decay.shape[1] // LANES
+    for g in range(groups):
+        columns = slice(g * LANES, (g + 1) * LANES)
+        rates[g * POLES : (g + 1) * POLES, :] = decay[:, columns]
+        for which in range(3):
+            start = g * POLES + 3 * which
+            taps[start : start + 3, :] = filters[which, :, columns]
+        taps[g * POLES + 9 : (g + 1) * POLES, :] = jnp.zeros((POLES - 9, LANES), f32)
+
+
 def first_kernel(
-    query_in, key_in, value_in, filters_in, decay_in, parcel, tails, tables,
-    key, value, query, filters, decay, keys, values, states, sem,
+    query_in, key_in, value_in, filters_in, decay_in, parcel, tails,
+    key, value, query, filters, decay, keys, values, states, rates, taps, sem,
 ):
     tokens, chans = key.shape
     groups = chans // LANES
@@ -104,14 +115,7 @@
     small[2].start()
     small[0].wait()
     small[1].wait()
-    rates, taps = halves_of(tables)
-    for g in range(groups):
-        columns = slice(g * LANES, (g + 1) * LANES)
-        rates[g * POLES : (g + 1) * POLES, :] = decay[:, columns]
-        for which in range(3):
-            start = g * POLES + 3 * which
-            taps[start : start + 3, :] = filters[which, :, columns]
-        taps[g * POLES + 9 : (g + 1) * POLES, :] = jnp.zeros((POLES - 9, LANES), f32)
+    fill_tables(filters, decay, rates, taps)
     for half in range(halves):
         factor = [jnp.exp(-rates[poled(n, half), :]) for n in range(POLES)]
         key_taps = taps_of(taps, 1, half)
@@ -257,53 +261,85 @@
         onward = decay * onward
 
 
-def inner_kernel(
-    query_hbm, key_hbm, value_hbm, residual_hbm, residue_hbm, tails, tables, skip,
-    base, query, lead, query_in, key_in, value_in, residual, residue,
-    queries, keys, values, streams, weights, sem,
+def features_kernel(
+    query_hbm, key_hbm, value_hbm, tails, tables, query, mixed,
+    query_in, key_in, value_in, queries, keys, values, sem,
 ):
     tokens, chans = query_in.shape
     groups = chans // LANES
-    every = range(groups)
-    rates, taps = halves_of(tables)
-    sources = (query_hbm, key_hbm, value_hbm, residual_hbm, residue_hbm)
-    targets = (query_in, key_in, value_in, residual, residue)
-    copies = [
-        pltpu.make_async_copy(source, target, sem.at[i])
-        for i, (source, target) in enumerate(zip(sources, targets, strict=True))
-    ]
-    for copy in copies:
-        copy.start()
-    for copy in copies:
-        copy.wait()
+    _, taps = halves_of(tables)
+    halves = groups // SUBLANES
+    width = SUBLANES * LANES
+    lanes = (
+        (query_hbm, query_in, queries),
+        (key_hbm, key_in, keys),
+        (value_hbm, value_in, values),
+    )
+    copies = []
+    for half in range(halves):
+        columns = slice(half * width, (half + 1) * width)
+        for i, (source, target, _) in enumerate(lanes):
+            copies.append(
+                pltpu.make_async_copy(
+                    source.at[:, columns], target.at[:, columns], sem.at[3 * half + i]
+                )
+            )
+            copies[-1].start()
     ends = tails[...].astype(f32)
-    for which, (source, target) in enumerate(
-        ((query_in, queries), (key_in, keys), (value_in, values))
-    ):
-        spread(ends[2 * which : 2 * which + 2], target, 0, every, groups)
-        spread(source, target, HALO, every, groups)
-    spread(residual, streams, 0, every, groups)
-    for g in every:
-        weights[g * POLES : (g + 1) * POLES, :] = residue[:, g * LANES : (g + 1) * LANES]
-    for half in range(groups // SUBLANES):
+    for half in range(halves):
+        columns = range(half * SUBLANES, (half + 1) * SUBLANES)
+        for i, (_, source, target) in enumerate(lanes):
+            spread(ends[2 * i : 2 * i + 2], target, 0, columns, groups)
+            copies[3 * half + i].wait()
+            spread(source, target, HALO, columns, groups)
         taps_here = [taps_of(taps, which, half) for which in range(3)]
         sources = (queries, keys, values)
 
-        def filtered(i, carry):
+        def turn(i, carry):
             carry = list(carry)
             for u in range(4):
                 t = i * 4 + u
                 now = [tile(x, t + HALO, half, groups) for x in sources]
                 out = [fir(taps_here[w], now[w], carry[2 * w], carry[2 * w + 1]) for w in range(3)]
                 put(query, t, half, groups, out[0])
-                put(keys, t, half, groups, out[1] * out[2])
+                put(mixed, t, half, groups, out[1] * out[2])
                 for w in range(3):
                     carry[2 * w + 1], carry[2 * w] = carry[2 * w], now[w]
             return tuple(carry)
 
         begin = tuple(tile(x, t, half, groups) for x in sources for t in (1, 0))
-        lax.fori_loop(0, tokens // 4, filtered, begin)
-
+        lax.fori_loop(0, tokens // 4, turn, begin)
+
+
+def inner_kernel(
+    query_hbm, mixed_hbm, residual_hbm, residue_hbm, tables, skip, base, lead,
+    query, mixed, residual, residue, streams, weights, sem,
+):
+    tokens, chans = residual.shape
+    groups = chans // LANES
+    rates, _ = halves_of(tables)
+    parts = (sem.shape[0] - 2) // 2
+    span = tokens // parts
+    small = [
+        pltpu.make_async_copy(residue_hbm, residue, sem.at[0]),
+        pltpu.make_async_copy(residual_hbm, residual, sem.at[1]),
+    ]
+    for copy in small:
+        copy.start()
+    copies = []
+    for p in range(parts):
+        part = slice(p * span * groups, (p + 1) * span * groups)
+        for i, (source, target) in enumerate(((query_hbm, query), (mixed_hbm, mixed))):
+            copies.append(
+                pltpu.make_async_copy(source.at[part, :], target.at[part, :], sem.at[2 + 2 * p + i])
+            )
+            copies[-1].start()
+    for copy in small:
+        copy.wait()
+    for g in range(groups):
+        weights[g * POLES : (g + 1) * POLES, :] = residue[:, g * LANES : (g + 1) * LANES]
+    spread(residual, streams, 0, range(groups), groups)
+    for half in range(groups // SUBLANES):
         factor, weight = [], []
         for n in range(POLES):
             rate = rates[poled(n, half), :]
@@ -315,16 +351,26 @@
         def turn(i, state):
             for u in range(8):
                 t = i * 8 + u
-                m = tile(keys, t, half, groups)
+                m = tile(mixed, t, half, groups)
                 state = [factor[n] * state[n] + m for n in range(POLES)]
-                parts = [direct * m, weight[0] * state[0]]
+                sums = [direct * m, weight[0] * state[0]]
                 for n in range(1, POLES):
-                    parts[n % 2] = parts[n % 2] + weight[n] * state[n]
-                gated = tile(query, t, half, groups) * (parts[0] + parts[1])
+                    sums[n % 2] = sums[n % 2] + weight[n] * state[n]
+                gated = tile(query, t, half, groups) * (sums[0] + sums[1])
                 put(base, t, half, groups, tile(streams, t, half, groups) + gated)
             return tuple(state)
 
-        lax.fori_loop(0, tokens // 8, turn, (jnp.zeros((SUBLANES, LANES), f32),) * POLES)
+        state = (jnp.zeros((SUBLANES, LANES), f32),) * POLES
+        for p in range(parts):
+            if half == 0:
+                copies[2 * p].wait()
+                copies[2 * p + 1].wait()
+            state = lax.fori_loop(p * span // 8, (p + 1) * span // 8, turn, state)
+
+
+def tables_kernel(filters, decay, tables):
+    rates, taps = halves_of(tables)
+    fill_tables(filters, decay, rates, taps)
 
 
 def outer_kernel(
@@ -442,12 +488,11 @@
     poled_rows = POLES * groups
     parcel_rows = (POLES + RAW) * groups
 
-    parcel, tails, tables = call(
+    parcel, tails = call(
         first_kernel,
         (
             shape(parcel_rows, bf16),
             jax.ShapeDtypeStruct((6, chans), bf16),
-            shape(2 * poled_rows),
         ),
         room=10.25,
         in_specs=[hbm] * 5,
@@ -460,6 +505,8 @@
             hold(tokens * groups),
             hold(tokens * groups),
             hold(poled_rows),
+            hold(poled_rows),
+            hold(poled_rows),
             pltpu.SemaphoreType.DMA((3 + 2 * (groups // SUBLANES),)),
         ],
     )(query_in, key_in, value_in, short_filter, decay_rate)
@@ -481,45 +528,48 @@
 
     arrived = exchange(parcel, lines)
     tails = lax.ppermute(tails, "seq", [(i, i + 1) for i in range(count - 1)])
+    tables = call(tables_kernel, shape(2 * poled_rows))(short_filter, decay_rate)
     sums, prefix = call(
         functools.partial(minor_kernel, block),
         (shape(parcel_rows, bf16), shape(poled_rows)),
         in_specs=[smem, vmem, vmem],
     )(place, arrived, tables)
     arrived = exchange(sums, planes)
+    query, mixed = call(
+        features_kernel,
+        (shape(tokens * groups),) * 2,
+        room=11.5,
+        in_specs=[hbm] * 3 + [vmem] * 2,
+        scratch=[
+            wide,
+            wide,
+            wide,
+            hold((tokens + HALO) * groups),
+            hold((tokens + HALO) * groups),
+            hold((tokens + HALO) * groups),
+            pltpu.SemaphoreType.DMA((3 * (groups // SUBLANES),)),
+        ],
+    )(query_in, key_in, value_in, tails, tables)
     carries = call(
         functools.partial(middle_kernel, block),
         shape(MAJOR * parcel_rows, bf16),
         in_specs=[smem, vmem, vmem, vmem],
     )(place, arrived, tables, prefix)
-    base, query, lead = call(
+    base, lead = call(
         inner_kernel,
-        (shape(tokens * groups),) * 2 + (shape(poled_rows),),
+        (shape(tokens * groups), shape(poled_rows)),
         room=11.5,
-        in_specs=[hbm] * 5 + [vmem] * 3,
+        in_specs=[hbm] * 4 + [vmem] * 2,
         scratch=[
-            wide,
-            wide,
-            wide,
+            hold(tokens * groups),
+            hold(tokens * groups),
             wide,
             pltpu.VMEM(residue.shape, f32),
-            hold((tokens + HALO) * groups),
-            hold((tokens + HALO) * groups),
-            hold((tokens + HALO) * groups),
             hold(tokens * groups),
             hold(poled_rows),
-            pltpu.SemaphoreType.DMA((5,)),
+            pltpu.SemaphoreType.DMA((10,)),
         ],
-    )(
-        query_in,
-        key_in,
-        value_in,
-        residual,
-        residue,
-        tails,
-        tables,
-        skip_gain.reshape(groups, LANES),
-    )
+    )(query, mixed, residual, residue, tables, skip_gain.reshape(groups, LANES))
     carries = exchange(carries, pairs)
     members = lax.axis_size("chan")
     summed, squares = call(

time: 77.2 us -> 77.1 us (level)
  local copies, waits for them, and re-layouts: 0.97 us -> 0.04 us
    unnamed x12 -> x16, local copies, waits for them, and re-layouts: 0.97 us -> 0.04 us
    pallas_call x1 -> x3, Pallas kernels: 8.41 us -> 9.14 us  [the longest x1 4.87 us: layer(): call(inner_kernel, (shape(tokens * groups), shape(poled_rows)), room=11.5...]
  transfers between devices with their start and end apart: 3 -> 3, of which waited for: 2 -> 2; matrix products, arithmetic and copies ran while one was open for 0% -> 0% of each run, Pallas kernels for 11% -> 12%
where the time goes in v3:
time: 77.1 us; the launch traced here: 76.6 us
  blocking collectives  25.2 us (33%)
  Pallas kernels  18.7 us (24%)
  waiting for transfers between devices  17.4 us (23%)
  starting transfers between devices  14.4 us (19%)
    all_to_all x1, blocking collectives, exchange(): return lax.all_to_all(x, 'seq', 0, 0, axis_index_groups=members, tiled=True)  15.6 us
    all_to_all x2, starting transfers between devices, exchange(): return lax.all_to_all(x, 'seq', 0, 0, axis_index_groups=members, tiled=True)  12.3 us
    ppermute x1, waiting for transfers between devices, layer(): tails = lax.ppermute(tails, 'seq', [(i, i + 1) for i in range(count - 1)])  11.7 us
    all_to_all x1, blocking collectives, layer(): squares = lax.all_to_all(squares, 'chan', 0, 0, tiled=True)  9.61 us
    all_to_all x2, waiting for transfers between devices, exchange(): return lax.all_to_all(x, 'seq', 0, 0, axis_index_groups=members, tiled=True)  5.74 us
    pallas_call x1, Pallas kernels, layer(): call(inner_kernel, (shape(tokens * groups), shape(poled_rows)), room=11.5...  4.87 us
    pallas_call x1, Pallas kernels, layer(): call(first_kernel, (shape(parcel_rows, bf16), jax.ShapeDtypeStruct((6, ch...  4.67 us
    pallas_call x1, Pallas kernels, layer(): call(features_kernel, (shape(tokens * groups),) * 2, room=11.5, in_specs=...  4.24 us
  transfers between devices with their start and end apart: 3, of which 2 were waited for; matrix products, arithmetic and copies ran while one was open for 0% of the time, Pallas kernels for 12%

profile of v3, /device:TPU:256, one launch (start us, length us, event | category | flops | bytes accessed | tf_op | source)
XLA Modules:
  0.0 76.6 jit_solution(6221963329391149871)
XLA Ops:
  0.6 0.0 copy-start.4
  0.6 4.7 %shard_map.104 = (bf16[384,128]{1,0:T(8,128)(2,1)}, bf16[6,2048]{1,0:T(8,128)(2,1)S(1)}) custom-call(bf16[128,2048]{1,0:T(8,128)(2,1)} %query_hbm.1, bf16[128,2048]{1,0:T(8,128)(2,1)} %key_hbm.1, bf16[128,2048]{1,0:T(8,128)(2,1)} %value_hbm.1, f32[3,3,2048]{2,1,0:T(4,128)} %filters.1, f32[16,2048]{1,0:T(8,128)} %decay.1), custom_call_target="tpu_custom_call" | custom-call | tf_op jit(solution)/shard_map/pallas_call | solution.py:491
  5.3 0.0 copy-start.2
  5.3 4.4 %all-to-all-start = ((bf16[8,48,128]{2,1,0:T(8,128)(2,1)}), bf16[8,48,128]{2,1,0:T(8,128)(2,1)S(1)}, u32[]{:S(2)}, u32[]{:S(2)}) async-start(bf16[8,48,128]{2,1,0:T(8,128)(2,1)} %bitcast.1), calls=%async_computation | async-start | bytes 196608 | tf_op jit(solution)/shard_map/all_to_all | solution.py:527
  9.8 0.0 copy-done.4
  9.8 0.0 copy-done.2
  9.8 5.7 %all-to-all-done = bf16[8,48,128]{2,1,0:T(8,128)(2,1)S(1)} async-done(((bf16[8,48,128]{2,1,0:T(8,128)(2,1)}), bf16[8,48,128]{2,1,0:T(8,128)(2,1)S(1)}, u32[]{:S(2)}, u32[]{:S(2)}) %all-to-all-start) | async-done | bytes 98336 | tf_op jit(solution)/shard_map/all_to_all | solution.py:527
  15.6 0.1 shard_map.106
  15.7 15.6 %all_to_all.44 = bf16[8,48,128]{2,1,0:T(8,128)(2,1)S(1)} all-to-all(bf16[8,48,128]{2,1,0:T(8,128)(2,1)S(1)} %bitcast.16), channel_id=1, replica_groups={{0,32,64,96,128,160,192,224},{4,36,68,100,132,164,196,228},{8,40,72,104..., dimensions={0} | all-to-all | bytes 196608 | tf_op jit(solution)/shard_map/all_to_all | solution.py:527
  31.3 0.0 copy-start
  31.3 0.0 copy-start.1
  31.3 0.9 %shard_map.107 = bf16[768,128]{1,0:T(8,128)(2,1)} custom-call(s32[1]{0:T(128)} %bitcast.place, bf16[384,128]{1,0:T(8,128)(2,1)S(1)} %bitcast.14, f32[512,128]{1,0:T(8,128)S(1)} %shard_map.105.tables, f32[256,128]{1,0:T(8,128)S(1)} %get-tuple-element.14.prefix), custom_call_target="tpu_custom_call" | custom-call | tf_op jit(solution)/shard_map/pallas_call | solution.py:553
  32.2 7.8 %all-to-all-start.2 = ((bf16[16,48,128]{2,1,0:T(8,128)(2,1)}), bf16[16,48,128]{2,1,0:T(8,128)(2,1)S(1)}, u32[]{:S(2)}, u32[]{:S(2)}) async-start(bf16[16,48,128]{2,1,0:T(8,128)(2,1)} %bitcast.5), calls=%async_computation.2 | async-start | bytes 393216 | tf_op jit(solution)/shard_map/all_to_all | solution.py:527
  40.0 0.0 copy-start.3
  40.0 0.0 copy-start.5
  40.0 2.2 %collective-permute-start = (bf16[6,2048]{1,0:T(8,128)(2,1)S(1)}, bf16[6,2048]{1,0:T(8,128)(2,1)S(1)}, u32[]{:S(2)}, u32[]{:S(2)}) collective-permute-start(bf16[6,2048]{1,0:T(8,128)(2,1)S(1)} %get-tuple-element.15), channel_id=1, source_target_pairs={{0,4},{4,8},{8,12},{12,16},{16,20},{20,24},{24,28},{28,32},{32,36}... | collective-permute-start | bytes 73736 | tf_op jit(solution)/shard_map/ppermute | solution.py:530
  42.2 11.7 %collective-permute-done.tails = bf16[6,2048]{1,0:T(8,128)(2,1)S(1)} collective-permute-done((bf16[6,2048]{1,0:T(8,128)(2,1)S(1)}, bf16[6,2048]{1,0:T(8,128)(2,1)S(1)}, u32[]{:S(2)}, u32[]{:S(2)}) %collective-permute-start) | collective-permute-done | bytes 24608 | tf_op jit(solution)/shard_map/ppermute | solution.py:530
  53.8 0.0 copy-done
  53.8 0.0 copy-done.1
  53.8 0.0 copy-start.6
  53.8 4.2 %shard_map.108 = (f32[2048,128]{1,0:T(8,128)}, f32[2048,128]{1,0:T(8,128)}) custom-call(bf16[128,2048]{1,0:T(8,128)(2,1)S(1)} %copy-done, bf16[128,2048]{1,0:T(8,128)(2,1)S(1)} %copy-done.1, bf16[128,2048]{1,0:T(8,128)(2,1)} %value_hbm.1, bf16[6,2048]{1,0:T(8,128)(2,1)S(1)} %collective-permute-done.tails, f32[512,128]{1,0:T(8,128)S(1)} %shard_map.105.tables), custom_call_target="tpu_custom_call" | custom-call | tf_op jit(solution)/shard_map/pallas_call | solution.py:538
  58.1 0.0 copy-done.3
  58.1 0.0 copy-done.5
  58.1 0.0 copy-done.6
  58.1 4.9 %shard_map.109 = (f32[2048,128]{1,0:T(8,128)}, f32[256,128]{1,0:T(8,128)S(1)}) custom-call(f32[2048,128]{1,0:T(8,128)} %get-tuple-element.16.query_hbm, f32[2048,128]{1,0:T(8,128)} %get-tuple-element.17.mixed_hbm, bf16[128,2048]{1,0:T(8,128)(2,1)S(1)} %copy-done.3, f32[16,2048]{1,0:T(8,128)S(1)} %copy-done.5, f32[512,128]{1,0:T(8,128)S(1)} %shard_map.105.tables, ...), custom_call_target="tpu_custom_call" | custom-call | tf_op jit(solution)/shard_map/pallas_call | solution.py:558
  63.0 0.0 all-to-all-done.2
  63.0 2.9 %shard_map.110 = (bf16[128,2048]{1,0:T(8,128)(2,1)S(1)}, f32[4,128]{1,0:T(4,128)S(1)}) custom-call(s32[1]{0:T(128)} %bitcast.place, bf16[768,128]{1,0:T(8,128)(2,1)S(1)} %bitcast.13, f32[512,128]{1,0:T(8,128)S(1)} %shard_map.105.tables, f32[256,128]{1,0:T(8,128)S(1)} %get-tuple-element.18.lead, f32[2048,128]{1,0:T(8,128)} %get-tuple-element.16.query_hbm, ...), custom_call_target="tpu_custom_call" | custom-call | tf_op jit(solution)/shard_map/pallas_call | solution.py:575
  65.9 0.0 copy-start.7
  65.9 9.6 %all_to_all.45 = f32[4,1,128]{2,1,0:T(1,128)S(1)} all-to-all(f32[4,1,128]{2,1,0:T(1,128)S(1)} %bitcast.20), channel_id=1, replica_groups=mesh['seq'=128,'chan'=4] {'chan'}, dimensions={0} | all-to-all | bytes 4096 | tf_op jit(solution)/shard_map/all_to_all | solution.py:591
  75.5 0.0 copy-done.7
  75.5 1.0 %shard_map.111 = (bf16[128,2048]{1,0:T(8,128)(2,1)}, bf16[128,2048]{1,0:T(8,128)(2,1)}) custom-call(bf16[128,2048]{1,0:T(8,128)(2,1)S(1)} %get-tuple-element.20.summed, f32[4,128]{1,0:T(4,128)S(1)} %bitcast.19, f32[16,128]{1,0:T(8,128)S(1)} %bitcast.18), custom_call_target="tpu_custom_call" | custom-call | tf_op jit(solution)/shard_map/pallas_call | solution.py:593
  (1 shorter events, 0.0 us)
Async XLA Ops:
  0.6 9.2 %copy-start.4 = (f32[3,3,2048]{2,1,0:T(4,128)S(1)}, f32[3,3,2048]{2,1,0:T(4,128)}, u32[]{:S(2)}) copy-start(f32[3,3,2048]{2,1,0:T(4,128)} %filters.1) | copy-start | bytes 221188
  5.3 4.5 %copy-start.2 = (f32[16,2048]{1,0:T(8,128)S(1)}, f32[16,2048]{1,0:T(8,128)}, u32[]{:S(2)}) copy-start(f32[16,2048]{1,0:T(8,128)} %decay.1) | copy-start | bytes 393220
  5.3 10.2 %all-to-all-start = ((bf16[8,48,128]{2,1,0:T(8,128)(2,1)}), bf16[8,48,128]{2,1,0:T(8,128)(2,1)S(1)}, u32[]{:S(2)}, u32[]{:S(2)}) async-start(bf16[8,48,128]{2,1,0:T(8,128)(2,1)} %bitcast.1), calls=%async_computation | async-start | bytes 196608 | tf_op jit(solution)/shard_map/all_to_all | solution.py:527
  31.3 22.5 %copy-start = (bf16[128,2048]{1,0:T(8,128)(2,1)S(1)}, bf16[128,2048]{1,0:T(8,128)(2,1)}, u32[]{:S(2)}) copy-start(bf16[128,2048]{1,0:T(8,128)(2,1)} %query_hbm.1) | copy-start | bytes 1572868
  31.3 22.5 %copy-start.1 = (bf16[128,2048]{1,0:T(8,128)(2,1)S(1)}, bf16[128,2048]{1,0:T(8,128)(2,1)}, u32[]{:S(2)}) copy-start(bf16[128,2048]{1,0:T(8,128)(2,1)} %key_hbm.1) | copy-start | bytes 1572868
  32.2 30.8 %all-to-all-start.2 = ((bf16[16,48,128]{2,1,0:T(8,128)(2,1)}), bf16[16,48,128]{2,1,0:T(8,128)(2,1)S(1)}, u32[]{:S(2)}, u32[]{:S(2)}) async-start(bf16[16,48,128]{2,1,0:T(8,128)(2,1)} %bitcast.5), calls=%async_computation.2 | async-start | bytes 393216 | tf_op jit(solution)/shard_map/all_to_all | solution.py:527
  40.0 18.1 %copy-start.3 = (bf16[128,2048]{1,0:T(8,128)(2,1)S(1)}, bf16[128,2048]{1,0:T(8,128)(2,1)}, u32[]{:S(2)}) copy-start(bf16[128,2048]{1,0:T(8,128)(2,1)} %residual_hbm.1) | copy-start | bytes 1572868
  40.0 18.1 %copy-start.5 = (f32[16,2048]{1,0:T(8,128)S(1)}, f32[16,2048]{1,0:T(8,128)}, u32[]{:S(2)}) copy-start(f32[16,2048]{1,0:T(8,128)} %residue_hbm.1) | copy-start | bytes 393220
  40.0 13.8 %collective-permute-start = (bf16[6,2048]{1,0:T(8,128)(2,1)S(1)}, bf16[6,2048]{1,0:T(8,128)(2,1)S(1)}, u32[]{:S(2)}, u32[]{:S(2)}) collective-permute-start(bf16[6,2048]{1,0:T(8,128)(2,1)S(1)} %get-tuple-element.15), channel_id=1, source_target_pairs={{0,4},{4,8},{8,12},{12,16},{16,20},{20,24},{24,28},{28,32},{32,36}... | collective-permute-start | bytes 73736 | tf_op jit(solution)/shard_map/ppermute | solution.py:530
  53.8 4.3 %copy-start.6 = (f32[2048]{0:T(1024)S(1)}, f32[2048]{0:T(1024)}, u32[]{:S(2)}) copy-start(f32[2048]{0:T(1024)} %param.16) | copy-start | bytes 24580
  65.9 9.6 %copy-start.7 = (f32[2048]{0:T(1024)S(1)}, f32[2048]{0:T(1024)}, u32[]{:S(2)}) copy-start(f32[2048]{0:T(1024)} %param.17) | copy-start | bytes 24580

commit v4 on v3

--- a/solution.py
+++ b/solution.py
@@ -180,20 +180,26 @@
     return [jnp.concatenate(x, axis=0) for x in result]
 
 
-def piece_of(ref, place, rows):
-    return ref[pl.ds(pl.multiple_of((place[0] % MINOR) * rows, SUBLANES), rows), :]
+def piece_of(place, filters, decay):
+    chans = decay.shape[1] // MINOR
+    start = pl.multiple_of((place[0] % MINOR) * chans, LANES)
+    rates = decay[:, pl.ds(start, chans)]
+    taps = jnp.concatenate([filters[which, :, pl.ds(start, chans)] for which in range(3)], axis=0)
+    taps = jnp.concatenate([taps, jnp.zeros((POLES - 9, chans), f32)], axis=0)
+    return [
+        jnp.concatenate([x[:, g : g + LANES] for g in range(0, chans, LANES)], axis=0)
+        for x in (rates, taps)
+    ]
 
 
 def is_head(shape):
     return (lax.broadcasted_iota(jnp.int32, shape, 0) & 2) == 0
 
 
-def minor_kernel(block, place, arrived, tables, sums, prefix):
-    rates, taps = halves_of(tables)
+def minor_kernel(block, place, arrived, filters, decay_rate, sums, prefix):
+    rate, tap = piece_of(place, filters, decay_rate)
     size = arrived.shape[0] // MINOR
-    rows = rates.shape[0] // MINOR
-    rate = piece_of(rates, place, rows)
-    tap = piece_of(taps, place, rows)
+    rows = rate.shape[0]
     decay = jnp.exp(-rate * block)
     late = [jnp.exp(-rate * (block - 1.0)), jnp.exp(-rate * (block - 2.0))]
     total = jnp.zeros((rows, LANES), f32)
@@ -212,62 +218,60 @@
         sums[other * size + rows : (other + 1) * size, :] = ends
 
 
-def middle_kernel(block, place, arrived, tables, prefix, carries):
-    rates, taps = halves_of(tables)
+def lines_of(block, rate, tap, arrived, state, tail):
     size = arrived.shape[0] // MIDDLE
-    rows = rates.shape[0] // MINOR
-    rate = piece_of(rates, place, rows)
-    tap = piece_of(taps, place, rows)
-    mine = (place[0] // MINOR) % MIDDLE
-    lower = place[0] < MINOR * MIDDLE
-    decay = jnp.exp(-rate * block)
+    rows = rate.shape[0]
     line_decay = jnp.exp(-rate * (block * MINOR))
     rest_decay = jnp.exp(-rate * (block * (MINOR - 1)))
     late = [jnp.exp(-rate * (block - 1.0)), jnp.exp(-rate * (block - 2.0))]
-    before = jnp.zeros((rows, LANES), f32)
-    whole = jnp.zeros((rows, LANES), f32)
-    own = jnp.zeros((rows, LANES), f32)
-    raw = []
-    for other in range(MIDDLE):
-        raw.append(arrived[other * size + rows : (other + 1) * size, :].astype(f32))
-        last = raw[other - 1] if other else jnp.zeros_like(raw[0])
-        m = opening_of(tap, raw[other], last)
-        opening = late[0] * m[0] + late[1] * m[1]
-        if not other:
-            opening = jnp.where(lower, opening, 0.0)
-        piece = arrived[other * size : other * size + rows, :].astype(f32)
-        whole = line_decay * whole + (piece + rest_decay * opening)
-        before = jnp.where(other < mine, whole, before)
-        own = jnp.where(other == mine, opening, own)
-    onward = jnp.exp(-rate * (mine.astype(f32) * (block * MINOR))) * whole
-    head = is_head(raw[0].shape)
-    ends = jnp.where(
-        lower, jnp.where(head, 0.0, raw[-1]), jnp.where(head, raw[0], 0.0)
-    )
-    half = MINOR * size
+    entering, openings = [], []
+    for line in range(MIDDLE):
+        raw = arrived[line * size + rows : (line + 1) * size, :].astype(f32)
+        m = opening_of(tap, raw, tail)
+        openings.append(late[0] * m[0] + late[1] * m[1])
+        entering.append(state)
+        piece = arrived[line * size : line * size + rows, :].astype(f32)
+        state = line_decay * state + (piece + rest_decay * openings[-1])
+        tail = raw
+    return entering, openings, state, tail
+
+
+def ahead_kernel(block, place, arrived, filters, decay_rate, ahead):
+    rate, tap = piece_of(place, filters, decay_rate)
+    rows = rate.shape[0]
+    begin = jnp.zeros((rows, LANES), f32), jnp.zeros((ahead.shape[0] - rows, LANES), f32)
+    _, _, state, tail = lines_of(block, rate, tap, arrived, *begin)
+    ahead[:rows, :] = state.astype(bf16)
+    ahead[rows:, :] = tail.astype(bf16)
+
+
+def middle_kernel(block, place, arrived, ahead, prefix, filters, decay_rate, carries):
+    rate, tap = piece_of(place, filters, decay_rate)
+    rows = rate.shape[0]
+    mine = (place[0] // MINOR) % MIDDLE
+    begin = ahead[:rows, :].astype(f32), ahead[rows:, :].astype(f32)
+    entering, openings, _, _ = lines_of(block, rate, tap, arrived, *begin)
+    before, own = entering[0], openings[0]
+    for line in range(1, MIDDLE):
+        before = jnp.where(mine == line, entering[line], before)
+        own = jnp.where(mine == line, openings[line], own)
+    decay = jnp.exp(-rate * block)
     for b in range(MINOR):
         here = before + prefix[b * rows : (b + 1) * rows, :]
         if b:
             here = here + own
             own = decay * own
-        send = jnp.where(mine + b > 0, ends, 0.0)
-        at = b * size
-        carries[at : at + rows, :] = jnp.where(lower, here, 0.0).astype(bf16)
-        carries[at + rows : at + size, :] = jnp.zeros((size - rows, LANES), bf16)
-        at += half
-        carries[at : at + rows, :] = jnp.where(lower, onward, here).astype(bf16)
-        carries[at + rows : at + size, :] = send.astype(bf16)
+        carries[b * rows : (b + 1) * rows, :] = here.astype(bf16)
         before = decay * before
-        onward = decay * onward
 
 
 def features_kernel(
-    query_hbm, key_hbm, value_hbm, tails, tables, query, mixed,
+    query_hbm, key_hbm, value_hbm, filters, decay, query, mixed, tables,
     query_in, key_in, value_in, queries, keys, values, sem,
 ):
     tokens, chans = query_in.shape
     groups = chans // LANES
-    _, taps = halves_of(tables)
+    rates, taps = halves_of(tables)
     halves = groups // SUBLANES
     width = SUBLANES * LANES
     lanes = (
@@ -285,13 +289,12 @@
                 )
             )
             copies[-1].start()
-    ends = tails[...].astype(f32)
+    fill_tables(filters, decay, rates, taps)
     for half in range(halves):
         columns = range(half * SUBLANES, (half + 1) * SUBLANES)
         for i, (_, source, target) in enumerate(lanes):
-            spread(ends[2 * i : 2 * i + 2], target, 0, columns, groups)
             copies[3 * half + i].wait()
-            spread(source, target, HALO, columns, groups)
+            spread(source, target, 0, columns, groups)
         taps_here = [taps_of(taps, which, half) for which in range(3)]
         sources = (queries, keys, values)
 
@@ -299,7 +302,7 @@
             carry = list(carry)
             for u in range(4):
                 t = i * 4 + u
-                now = [tile(x, t + HALO, half, groups) for x in sources]
+                now = [tile(x, t, half, groups) for x in sources]
                 out = [fir(taps_here[w], now[w], carry[2 * w], carry[2 * w + 1]) for w in range(3)]
                 put(query, t, half, groups, out[0])
                 put(mixed, t, half, groups, out[1] * out[2])
@@ -307,23 +310,32 @@
                     carry[2 * w + 1], carry[2 * w] = carry[2 * w], now[w]
             return tuple(carry)
 
-        begin = tuple(tile(x, t, half, groups) for x in sources for t in (1, 0))
+        begin = (jnp.zeros((SUBLANES, LANES), f32),) * 6
         lax.fori_loop(0, tokens // 4, turn, begin)
 
 
 def inner_kernel(
-    query_hbm, mixed_hbm, residual_hbm, residue_hbm, tables, skip, base, lead,
-    query, mixed, residual, residue, streams, weights, sem,
+    query_hbm, mixed_hbm, residual_hbm, residue_hbm, query_in, key_in, value_in, tails, tables, skip,
+    base, lead, opening, query, mixed, residual, residue, heads, edges, streams, weights, sem,
 ):
     tokens, chans = residual.shape
     groups = chans // LANES
-    rates, _ = halves_of(tables)
-    parts = (sem.shape[0] - 2) // 2
+    rates, taps = halves_of(tables)
+    parts = (sem.shape[0] - 5) // 2
     span = tokens // parts
     small = [
         pltpu.make_async_copy(residue_hbm, residue, sem.at[0]),
         pltpu.make_async_copy(residual_hbm, residual, sem.at[1]),
     ]
+    first_rows = heads.shape[0] // 3
+    for i, source in enumerate((query_in, key_in, value_in)):
+        small.append(
+            pltpu.make_async_copy(
+                source.at[:first_rows, :],
+                heads.at[first_rows * i : first_rows * (i + 1), :],
+                sem.at[2 + i],
+            )
+        )
     for copy in small:
         copy.start()
     copies = []
@@ -331,7 +343,7 @@
         part = slice(p * span * groups, (p + 1) * span * groups)
         for i, (source, target) in enumerate(((query_hbm, query), (mixed_hbm, mixed))):
             copies.append(
-                pltpu.make_async_copy(source.at[part, :], target.at[part, :], sem.at[2 + 2 * p + i])
+                pltpu.make_async_copy(source.at[part, :], target.at[part, :], sem.at[5 + 2 * p + i])
             )
             copies[-1].start()
     for copy in small:
@@ -339,6 +351,11 @@
     for g in range(groups):
         weights[g * POLES : (g + 1) * POLES, :] = residue[:, g * LANES : (g + 1) * LANES]
     spread(residual, streams, 0, range(groups), groups)
+    ends = tails[...].astype(f32)
+    begins = heads[...].astype(f32)
+    for i in range(3):
+        spread(ends[2 * i : 2 * i + 2], edges, 4 * i, range(groups), groups)
+        spread(begins[first_rows * i : first_rows * i + 2], edges, 4 * i + 2, range(groups), groups)
     for half in range(groups // SUBLANES):
         factor, weight = [], []
         for n in range(POLES):
@@ -365,24 +382,25 @@
             if half == 0:
                 copies[2 * p].wait()
                 copies[2 * p + 1].wait()
+            if p == 0:
+                for t in range(HALO):
+                    out = []
+                    for i in range(3):
+                        now = [tile(edges, 4 * i + 2 + t - lag, half, groups) for lag in range(3)]
+                        out.append(fir(taps_of(taps, i, half), *now))
+                    put(query, t, half, groups, out[0])
+                    put(opening, t, half, groups, out[0])
+                    put(mixed, t, half, groups, out[1] * out[2])
             state = lax.fori_loop(p * span // 8, (p + 1) * span // 8, turn, state)
 
 
-def tables_kernel(filters, decay, tables):
-    rates, taps = halves_of(tables)
-    fill_tables(filters, decay, rates, taps)
-
-
 def outer_kernel(
-    block, place, carries, tables, lead, query_hbm, base_hbm, summed, squares,
-    carried, raw, query, gated, sem,
+    carries, tables, lead, opening, query_hbm, base_hbm, summed, squares,
+    carried, query, gated, sem,
 ):
     tokens, chans = summed.shape
     groups = chans // LANES
-    each = groups // MINOR
-    size = each * (POLES + RAW)
-    rows = each * POLES
-    rates, taps = halves_of(tables)
+    rates, _ = halves_of(tables)
     parts = sem.shape[0] // 2
     span = tokens // parts
     copies = []
@@ -393,27 +411,12 @@
                 pltpu.make_async_copy(source.at[part, :], target.at[part, :], sem.at[2 * p + i])
             )
             copies[-1].start()
-    for j in range(MINOR):
-        at, more = j * size, (MINOR + j) * size
-        both = carries[at : at + size, :].astype(f32) + carries[more : more + size, :].astype(f32)
-        carried[j * rows : (j + 1) * rows, :] = both[:rows]
-        raw[j * each * RAW : (j + 1) * each * RAW, :] = both[rows:]
-    away = (place[0] % (MINOR * MIDDLE)).astype(f32) * block - 2.0
+    carried[...] = carries[...].astype(f32)
     for half in range(groups // SUBLANES):
-        pair = [[], []]
-        for side in range(2):
-            weight = taps_of(taps, 1 + side, half)
-            line = [raw[poled(4 * side + r, half, RAW), :] for r in (2, 3, 0, 1)]
-            for t in range(2):
-                pair[t].append(fir(weight, line[t + 2], line[t + 1], line[t]))
-        opening = [p[0] * p[1] for p in pair]
         factor, state = [], []
         for n in range(POLES):
-            rate = rates[poled(n, half), :]
-            factor.append(jnp.exp(-rate))
-            entering = carried[poled(n, half), :] + jnp.exp(-rate * away) * (
-                factor[n] * opening[0] + opening[1]
-            )
+            factor.append(jnp.exp(-rates[poled(n, half), :]))
+            entering = carried[poled(n, half), :]
             state.append(tile(lead, n, half, groups) * entering)
 
         def turn(i, state):
@@ -432,6 +435,9 @@
             if half == 0:
                 copies[2 * p].wait()
                 copies[2 * p + 1].wait()
+            if p == 0:
+                for t in range(HALO):
+                    put(query, t, half, groups, tile(opening, t, half, groups))
             state = lax.fori_loop(p * span // 8, (p + 1) * span // 8, turn, state)
     total = jnp.zeros((tokens, LANES), f32)
     for g in range(groups):
@@ -518,76 +524,91 @@
         for z in range(MAJOR)
         for j in range(MINOR)
     ]
-    pairs = [
-        [(z * MIDDLE + y) * MINOR + j for z in range(MAJOR) for j in range(MINOR)]
-        for y in range(MIDDLE)
-    ]
 
     def exchange(x, members):
         return lax.all_to_all(x, "seq", 0, 0, axis_index_groups=members, tiled=True)
 
+    tables_in = (short_filter, decay_rate)
+    parcel, place = lax.optimization_barrier((parcel, place))
     arrived = exchange(parcel, lines)
-    tails = lax.ppermute(tails, "seq", [(i, i + 1) for i in range(count - 1)])
-    tables = call(tables_kernel, shape(2 * poled_rows))(short_filter, decay_rate)
     sums, prefix = call(
         functools.partial(minor_kernel, block),
         (shape(parcel_rows, bf16), shape(poled_rows)),
-        in_specs=[smem, vmem, vmem],
-    )(place, arrived, tables)
+        in_specs=[smem, vmem, vmem, vmem],
+    )(place, arrived, *tables_in)
     arrived = exchange(sums, planes)
-    query, mixed = call(
+    tails = lax.ppermute(tails, "seq", [(i, i + 1) for i in range(count - 1)])
+    query, mixed, tables = call(
         features_kernel,
-        (shape(tokens * groups),) * 2,
+        (shape(tokens * groups),) * 2 + (shape(2 * poled_rows),),
         room=11.5,
         in_specs=[hbm] * 3 + [vmem] * 2,
         scratch=[
             wide,
             wide,
             wide,
-            hold((tokens + HALO) * groups),
-            hold((tokens + HALO) * groups),
-            hold((tokens + HALO) * groups),
+            hold(tokens * groups),
+            hold(tokens * groups),
+            hold(tokens * groups),
             pltpu.SemaphoreType.DMA((3 * (groups // SUBLANES),)),
         ],
-    )(query_in, key_in, value_in, tails, tables)
+    )(query_in, key_in, value_in, *tables_in)
+    ahead = call(
+        functools.partial(ahead_kernel, block),
+        shape(parcel_rows // MINOR, bf16),
+        in_specs=[smem, vmem, vmem, vmem],
+    )(place, arrived, *tables_in)
+    ahead = lax.ppermute(ahead, "seq", [(i, i + count // 2) for i in range(count // 2)])
+    base, lead, opening = call(
+        inner_kernel,
+        (shape(tokens * groups), shape(poled_rows), shape(HALO * groups)),
+        room=11.5,
+        in_specs=[hbm] * 7 + [vmem] * 3,
+        scratch=[
+            hold(tokens * groups),
+            hold(tokens * groups),
+            wide,
+            pltpu.VMEM(residue.shape, f32),
+            pltpu.VMEM((48, chans), bf16),
+            hold(12 * groups),
+            hold(tokens * groups),
+            hold(poled_rows),
+            pltpu.SemaphoreType.DMA((13,)),
+        ],
+    )(
+        query,
+        mixed,
+        residual,
+        residue,
+        query_in,
+        key_in,
+        value_in,
+        tails,
+        tables,
+        skip_gain.reshape(groups, LANES),
+    )
     carries = call(
         functools.partial(middle_kernel, block),
-        shape(MAJOR * parcel_rows, bf16),
-        in_specs=[smem, vmem, vmem, vmem],
-    )(place, arrived, tables, prefix)
-    base, lead = call(
-        inner_kernel,
-        (shape(tokens * groups), shape(poled_rows)),
-        room=11.5,
-        in_specs=[hbm] * 4 + [vmem] * 2,
-        scratch=[
-            hold(tokens * groups),
-            hold(tokens * groups),
-            wide,
-            pltpu.VMEM(residue.shape, f32),
-            hold(tokens * groups),
-            hold(poled_rows),
-            pltpu.SemaphoreType.DMA((10,)),
-        ],
-    )(query, mixed, residual, residue, tables, skip_gain.reshape(groups, LANES))
-    carries = exchange(carries, pairs)
+        shape(poled_rows, bf16),
+        in_specs=[smem] + [vmem] * 5,
+    )(place, arrived, ahead, prefix, *tables_in)
+    carries = exchange(carries, lines)
     members = lax.axis_size("chan")
     summed, squares = call(
-        functools.partial(outer_kernel, block),
+        outer_kernel,
         (
             jax.ShapeDtypeStruct((tokens, chans), bf16),
             jax.ShapeDtypeStruct((members, tokens), f32),
         ),
         room=11.5,
-        in_specs=[smem] + [vmem] * 3 + [hbm] * 2,
+        in_specs=[vmem] * 4 + [hbm] * 2,
         scratch=[
             hold(poled_rows),
-            hold(RAW * groups),
             hold(tokens * groups),
             hold(tokens * groups),
             pltpu.SemaphoreType.DMA((8,)),
         ],
-    )(place, carries, tables, lead, query, base)
+    )(carries, tables, lead, opening, query, base)
     squares = lax.all_to_all(squares, "chan", 0, 0, tiled=True)
     whole = jax.ShapeDtypeStruct((tokens, chans), bf16)
     return call(

time: 77.1 us -> 77.7 us (level)
  the two profiles are of different devices: /device:TPU:256 before, /device:TPU:63 now
where the time goes in v4:
time: 77.7 us; the launch traced here: 77.3 us
  starting transfers between devices  29.2 us (38%)
  blocking collectives  27.6 us (36%)
  Pallas kernels  18.9 us (24%)
  waiting for transfers between devices  0.82 us (1%)
    all_to_all x2, blocking collectives, exchange(): return lax.all_to_all(x, 'seq', 0, 0, axis_index_groups=members, tiled=True)  19.1 us
    ppermute x1, starting transfers between devices, layer(): lax.ppermute(ahead, 'seq', [(i, i + count // 2) for i in range(count // 2)])  10.8 us
    ppermute x1, starting transfers between devices, layer(): tails = lax.ppermute(tails, 'seq', [(i, i + 1) for i in range(count - 1)])  10.4 us
    all_to_all x1, blocking collectives, layer(): squares = lax.all_to_all(squares, 'chan', 0, 0, tiled=True)  8.5 us
    all_to_all x1, starting transfers between devices, exchange(): return lax.all_to_all(x, 'seq', 0, 0, axis_index_groups=members, tiled=True)  8.05 us
    pallas_call x1, Pallas kernels, layer(): call(inner_kernel, (shape(tokens * groups), shape(poled_rows), shape(HALO...  5.42 us
    pallas_call x1, Pallas kernels, layer(): call(features_kernel, (shape(tokens * groups),) * 2 + (shape(2 * poled_ro...  4.47 us
    pallas_call x1, Pallas kernels, layer(): call(first_kernel, (shape(parcel_rows, bf16), jax.ShapeDtypeStruct((6, ch...  4.05 us
  transfers between devices with their start and end apart: 3, of which 1 were waited for; matrix products, arithmetic and copies ran while one was open for 0% of the time, Pallas kernels for 13%

profile of v4, /device:TPU:63, one launch (start us, length us, event | category | flops | bytes accessed | tf_op | source)
XLA Modules:
  0.0 77.3 jit_solution(10233475050331502712)
XLA Ops:
  0.6 0.0 copy-start.2
  0.6 4.0 %shard_map.104 = (bf16[384,128]{1,0:T(8,128)(2,1)S(1)}, bf16[6,2048]{1,0:T(8,128)(2,1)S(1)}) custom-call(bf16[128,2048]{1,0:T(8,128)(2,1)} %query_in.3, bf16[128,2048]{1,0:T(8,128)(2,1)} %key_in.3, bf16[128,2048]{1,0:T(8,128)(2,1)} %value_in.3, f32[3,3,2048]{2,1,0:T(4,128)} %filters.7, f32[16,2048]{1,0:T(8,128)} %decay.1), custom_call_target="tpu_custom_call" | custom-call | tf_op jit(solution)/shard_map/pallas_call | solution.py:497
  4.7 0.0 copy-start.1
  4.7 8.3 %all_to_all.44 = bf16[8,48,128]{2,1,0:T(8,128)(2,1)S(1)} all-to-all(bf16[8,48,128]{2,1,0:T(8,128)(2,1)S(1)} %bitcast.18), channel_id=1, replica_groups={{0,4,8,12,16,20,24,28},{32,36,40,44,48,52,56,60},{64,68,72,76,80,84,88,..., dimensions={0} | all-to-all | bytes 196608 | tf_op jit(solution)/shard_map/all_to_all | solution.py:529
  13.0 0.0 copy-done.2
  13.0 0.0 copy-done.1
  13.0 0.1 shard_map.105
  13.1 10.8 %all_to_all.45 = bf16[8,48,128]{2,1,0:T(8,128)(2,1)S(1)} all-to-all(bf16[8,48,128]{2,1,0:T(8,128)(2,1)S(1)} %bitcast.17), channel_id=1, replica_groups={{0,32,64,96,128,160,192,224},{4,36,68,100,132,164,196,228},{8,40,72,104..., dimensions={0} | all-to-all | bytes 196608 | tf_op jit(solution)/shard_map/all_to_all | solution.py:529
  23.9 0.0 copy-start
  23.9 0.1 shard_map.106
  24.0 10.8 %collective-permute-start = (bf16[48,128]{1,0:T(8,128)(2,1)S(1)}, bf16[48,128]{1,0:T(8,128)(2,1)S(1)}, u32[]{:S(2)}, u32[]{:S(2)}) collective-permute-start(bf16[48,128]{1,0:T(8,128)(2,1)S(1)} %shard_map.106), channel_id=1, source_target_pairs={{0,256},{4,260},{8,264},{12,268},{16,272},{20,276},{24,280},{28,28... | collective-permute-start | bytes 36872 | tf_op jit(solution)/shard_map/ppermute | solution.py:561
  34.8 0.8 %collective-permute-done.ahead = bf16[48,128]{1,0:T(8,128)(2,1)S(1)} collective-permute-done((bf16[48,128]{1,0:T(8,128)(2,1)S(1)}, bf16[48,128]{1,0:T(8,128)(2,1)S(1)}, u32[]{:S(2)}, u32[]{:S(2)}) %collective-permute-start) | collective-permute-done | bytes 12320 | tf_op jit(solution)/shard_map/ppermute | solution.py:561
  35.6 0.8 %shard_map.107 = bf16[256,128]{1,0:T(8,128)(2,1)} custom-call(s32[1]{0:T(128)} %bitcast.place, bf16[384,128]{1,0:T(8,128)(2,1)S(1)} %bitcast.14, bf16[48,128]{1,0:T(8,128)(2,1)S(1)} %collective-permute-done.ahead, f32[256,128]{1,0:T(8,128)S(1)} %get-tuple-element.20.prefix, f32[3,3,2048]{2,1,0:T(4,128)S(1)} %copy-done.2, f32[16,2048]{1,0:T(8,128)S(1)} %copy-done.1), custom_call_target="tpu_custom_call" | custom-call | tf_op jit(solution)/shard_map/pallas_call | solution.py:590
  36.4 8.0 %all-to-all-start.2 = ((bf16[8,32,128]{2,1,0:T(8,128)(2,1)}), bf16[8,32,128]{2,1,0:T(8,128)(2,1)S(1)}, u32[]{:S(2)}, u32[]{:S(2)}) async-start(bf16[8,32,128]{2,1,0:T(8,128)(2,1)} %bitcast.5), calls=%async_computation.2 | async-start | bytes 131072 | tf_op jit(solution)/shard_map/all_to_all | solution.py:529
  44.5 0.0 copy-start.3
  44.5 0.0 copy-start.4
  44.5 10.4 %collective-permute-start.1 = (bf16[6,2048]{1,0:T(8,128)(2,1)S(1)}, bf16[6,2048]{1,0:T(8,128)(2,1)S(1)}, u32[]{:S(2)}, u32[]{:S(2)}) collective-permute-start(bf16[6,2048]{1,0:T(8,128)(2,1)S(1)} %get-tuple-element.24), channel_id=1, source_target_pairs={{0,4},{4,8},{8,12},{12,16},{16,20},{20,24},{24,28},{28,32},{32,36}... | collective-permute-start | bytes 73736 | tf_op jit(solution)/shard_map/ppermute | solution.py:540
  54.9 0.0 copy-done
  54.9 0.0 copy-start.5
  54.9 4.5 %shard_map.108 = (f32[2048,128]{1,0:T(8,128)}, f32[2048,128]{1,0:T(8,128)}, f32[512,128]{1,0:T(8,128)S(1)}) custom-call(bf16[128,2048]{1,0:T(8,128)(2,1)S(1)} %copy-done, bf16[128,2048]{1,0:T(8,128)(2,1)} %key_in.3, bf16[128,2048]{1,0:T(8,128)(2,1)} %value_in.3, f32[3,3,2048]{2,1,0:T(4,128)S(1)} %copy-done.2, f32[16,2048]{1,0:T(8,128)S(1)} %copy-done.1), custom_call_target="tpu_custom_call" | custom-call | tf_op jit(solution)/shard_map/pallas_call | solution.py:541
  59.4 0.0 collective-permute-done.1.tails
  59.4 0.0 copy-done.3
  59.4 0.0 copy-done.4
  59.4 0.0 copy-done.5
  59.4 5.4 %shard_map.109 = (f32[2048,128]{1,0:T(8,128)}, f32[256,128]{1,0:T(8,128)S(1)}, f32[32,128]{1,0:T(8,128)S(1)}) custom-call(f32[2048,128]{1,0:T(8,128)} %get-tuple-element.22.query_hbm, f32[2048,128]{1,0:T(8,128)} %get-tuple-element.23.mixed_hbm, bf16[128,2048]{1,0:T(8,128)(2,1)S(1)} %copy-done.3, f32[16,2048]{1,0:T(8,128)S(1)} %copy-done.4, ...), custom_call_target="tpu_custom_call" | custom-call | tf_op jit(solution)/shard_map/pallas_call | solution.py:562
  64.9 0.0 all-to-all-done.2
  64.9 2.9 %shard_map.110 = (bf16[128,2048]{1,0:T(8,128)(2,1)S(1)}, f32[4,128]{1,0:T(4,128)S(1)}) custom-call(bf16[256,128]{1,0:T(8,128)(2,1)S(1)} %bitcast.16, f32[512,128]{1,0:T(8,128)S(1)} %get-tuple-element.21.tables, f32[256,128]{1,0:T(8,128)S(1)} %get-tuple-element.25.lead, f32[32,128]{1,0:T(8,128)S(1)} %get-tuple-element.26.opening, ...), custom_call_target="tpu_custom_call" | custom-call | tf_op jit(solution)/shard_map/pallas_call | solution.py:597
  67.8 0.0 copy-start.6
  67.8 8.5 %all_to_all.46 = f32[4,1,128]{2,1,0:T(1,128)S(1)} all-to-all(f32[4,1,128]{2,1,0:T(1,128)S(1)} %bitcast.22), channel_id=1, replica_groups=mesh['seq'=128,'chan'=4] {'chan'}, dimensions={0} | all-to-all | bytes 4096 | tf_op jit(solution)/shard_map/all_to_all | solution.py:612
  76.3 0.0 copy-done.6
  76.3 1.0 %shard_map.111 = (bf16[128,2048]{1,0:T(8,128)(2,1)}, bf16[128,2048]{1,0:T(8,128)(2,1)}) custom-call(bf16[128,2048]{1,0:T(8,128)(2,1)S(1)} %get-tuple-element.28.summed, f32[4,128]{1,0:T(4,128)S(1)} %bitcast.21, f32[16,128]{1,0:T(8,128)S(1)} %bitcast.20), custom_call_target="tpu_custom_call" | custom-call | tf_op jit(solution)/shard_map/pallas_call | solution.py:614
Async XLA Ops:
  0.6 12.4 %copy-start.2 = (f32[3,3,2048]{2,1,0:T(4,128)S(1)}, f32[3,3,2048]{2,1,0:T(4,128)}, u32[]{:S(2)}) copy-start(f32[3,3,2048]{2,1,0:T(4,128)} %filters.7) | copy-start | bytes 221188
  4.7 8.3 %copy-start.1 = (f32[16,2048]{1,0:T(8,128)S(1)}, f32[16,2048]{1,0:T(8,128)}, u32[]{:S(2)}) copy-start(f32[16,2048]{1,0:T(8,128)} %decay.1) | copy-start | bytes 393220
  23.9 31.0 %copy-start = (bf16[128,2048]{1,0:T(8,128)(2,1)S(1)}, bf16[128,2048]{1,0:T(8,128)(2,1)}, u32[]{:S(2)}) copy-start(bf16[128,2048]{1,0:T(8,128)(2,1)} %query_in.3) | copy-start | bytes 1572868
  24.0 11.6 %collective-permute-start = (bf16[48,128]{1,0:T(8,128)(2,1)S(1)}, bf16[48,128]{1,0:T(8,128)(2,1)S(1)}, u32[]{:S(2)}, u32[]{:S(2)}) collective-permute-start(bf16[48,128]{1,0:T(8,128)(2,1)S(1)} %shard_map.106), channel_id=1, source_target_pairs={{0,256},{4,260},{8,264},{12,268},{16,272},{20,276},{24,280},{28,28... | collective-permute-start | bytes 36872 | tf_op jit(solution)/shard_map/ppermute | solution.py:561
  36.4 28.4 %all-to-all-start.2 = ((bf16[8,32,128]{2,1,0:T(8,128)(2,1)}), bf16[8,32,128]{2,1,0:T(8,128)(2,1)S(1)}, u32[]{:S(2)}, u32[]{:S(2)}) async-start(bf16[8,32,128]{2,1,0:T(8,128)(2,1)} %bitcast.5), calls=%async_computation.2 | async-start | bytes 131072 | tf_op jit(solution)/shard_map/all_to_all | solution.py:529
  44.5 14.9 %copy-start.3 = (bf16[128,2048]{1,0:T(8,128)(2,1)S(1)}, bf16[128,2048]{1,0:T(8,128)(2,1)}, u32[]{:S(2)}) copy-start(bf16[128,2048]{1,0:T(8,128)(2,1)} %residual_hbm.1) | copy-start | bytes 1572868
  44.5 14.9 %copy-start.4 = (f32[16,2048]{1,0:T(8,128)S(1)}, f32[16,2048]{1,0:T(8,128)}, u32[]{:S(2)}) copy-start(f32[16,2048]{1,0:T(8,128)} %residue_hbm.1) | copy-start | bytes 393220
  44.5 14.9 %collective-permute-start.1 = (bf16[6,2048]{1,0:T(8,128)(2,1)S(1)}, bf16[6,2048]{1,0:T(8,128)(2,1)S(1)}, u32[]{:S(2)}, u32[]{:S(2)}) collective-permute-start(bf16[6,2048]{1,0:T(8,128)(2,1)S(1)} %get-tuple-element.24), channel_id=1, source_target_pairs={{0,4},{4,8},{8,12},{12,16},{16,20},{20,24},{24,28},{28,32},{32,36}... | collective-permute-start | bytes 73736 | tf_op jit(solution)/shard_map/ppermute | solution.py:540
  54.9 4.5 %copy-start.5 = (f32[2048]{0:T(1024)S(1)}, f32[2048]{0:T(1024)}, u32[]{:S(2)}) copy-start(f32[2048]{0:T(1024)} %param.16) | copy-start | bytes 24580
  67.8 8.5 %copy-start.6 = (f32[2048]{0:T(1024)S(1)}, f32[2048]{0:T(1024)}, u32[]{:S(2)}) copy-start(f32[2048]{0:T(1024)} %param.17) | copy-start | bytes 24580

commit v5 on v4

v5 whole, which is shorter than its diff:
```python
import functools

import jax
import jax.numpy as jnp
from jax import lax
from jax.experimental import pallas as pl
from jax.experimental.pallas import tpu as pltpu
from jax.sharding import PartitionSpec as P


D = 8192
EPSILON = 1e-06
LANES = 128
SUBLANES = 8
MINOR = 8
MIDDLE = 8
MAJOR = 2
STEP = 6
HALO = 2
RAW = 8
EXTRA = 8

f32 = jnp.float32
bf16 = jnp.bfloat16

POLES = 16


def call(kernel, out_shape, scratch=(), room=50, **extra):
    limit = int((64 - room) * 1024) << 10
    return pl.pallas_call(
        kernel,
        out_shape=out_shape,
        scratch_shapes=scratch,
        compiler_params=pltpu.CompilerParams(vmem_limit_bytes=limit),
        **extra,
    )


def spread(source, target, first, columns, groups):
    items = source.shape[0]
    for g in columns:
        target[pl.ds(first * groups + g, items, stride=groups), :] = source[
            :, g * LANES : (g + 1) * LANES
        ].astype(f32)


def start_of(item, half, groups):
    start = item * groups + half * SUBLANES
    return start if isinstance(start, int) else pl.multiple_of(start, SUBLANES)


def tile(ref, item, half, groups):
    return ref[pl.ds(start_of(item, half, groups), SUBLANES), :]


def put(ref, item, half, groups, value):
    ref[pl.ds(start_of(item, half, groups), SUBLANES), :] = value


def poled(item, half, stride=POLES):
    return pl.ds(half * SUBLANES * stride + item, SUBLANES, stride=stride)


def taps_of(taps, which, half):
    return [taps[poled(which * 3 + lag, half), :] for lag in range(3)]


def fir(taps, now, last, older):
    return taps[0] * now + taps[1] * last + taps[2] * older


def fill_tables(filters, decay, rates, taps):
    groups = decay.shape[1] // LANES
    for g in range(groups):
        columns = slice(g * LANES, (g + 1) * LANES)
        rates[g * POLES : (g + 1) * POLES, :] = decay[:, columns]
        for which in range(3):
            start = g * POLES + 3 * which
            taps[start : start + 3, :] = filters[which, :, columns]
        taps[g * POLES + 9 : (g + 1) * POLES, :] = jnp.zeros((POLES - 9, LANES), f32)


def first_kernel(
    query_in, key_in, value_in, filters_in, decay_in, parcel,
    key, value, query, filters, decay, keys, values, states, rates, taps, sem,
):
    tokens, chans = key.shape
    groups = chans // LANES
    halves = groups // SUBLANES
    width = SUBLANES * LANES

    def part(source, target, half, slot):
        columns = slice(half * width, (half + 1) * width)
        return pltpu.make_async_copy(source.at[:, columns], target.at[:, columns], sem.at[slot])

    small = [
        pltpu.make_async_copy(decay_in, decay, sem.at[0]),
        pltpu.make_async_copy(filters_in, filters, sem.at[1]),
        pltpu.make_async_copy(query_in.at[tokens - 8 : tokens, :], query, sem.at[2]),
    ]
    large = [
        (part(key_in, key, h, 3 + 2 * h), part(value_in, value, h, 4 + 2 * h))
        for h in range(halves)
    ]
    small[0].start()
    small[1].start()
    for pair in large:
        pair[0].start()
        pair[1].start()
    small[2].start()
    small[0].wait()
    small[1].wait()
    fill_tables(filters, decay, rates, taps)
    for half in range(halves):
        factor = [jnp.exp(-rates[poled(n, half), :]) for n in range(POLES)]
        key_taps = taps_of(taps, 1, half)
        value_taps = taps_of(taps, 2, half)
        for copy in large[half]:
            copy.wait()
        columns = range(half * SUBLANES, (half + 1) * SUBLANES)
        spread(key, keys, 0, columns, groups)
        spread(value, values, 0, columns, groups)

        def turn(i, carry):
            k1, k2, v1, v2, *state = carry
            for u in range(STEP):
                t = HALO + i * STEP + u
                k0 = tile(keys, t, half, groups)
                v0 = tile(values, t, half, groups)
                m = fir(key_taps, k0, k1, k2) * fir(value_taps, v0, v1, v2)
                state = [factor[n] * state[n] + m for n in range(POLES)]
                k1, k2, v1, v2 = k0, k1, v0, v1
            return (k1, k2, v1, v2, *state)

        begin = tuple(tile(x, t, half, groups) for x in (keys, values) for t in (1, 0))
        begin += (jnp.zeros((SUBLANES, LANES), f32),) * POLES
        end = lax.fori_loop(0, (tokens - HALO) // STEP, turn, begin)
        for n in range(POLES):
            states[poled(n, half), :] = end[4 + n]
    small[2].wait()
    ends = [(x[:16, :].astype(f32)[:2], x[tokens - 16 :, :].astype(f32)[-2:]) for x in (key, value)]
    raw = jnp.concatenate([*ends[0], *ends[1]], axis=0)
    last = query[...].astype(f32)[-2:]
    each = groups // MINOR
    rows = each * POLES
    size = rows + each * RAW + EXTRA
    for j in range(MINOR):
        lanes = [slice(g * LANES, (g + 1) * LANES) for g in range(each * j, each * (j + 1))]
        parcel[j * size : j * size + rows, :] = states[rows * j : rows * (j + 1), :].astype(bf16)
        pieces = [raw[:, x] for x in lanes] + [last[:, x] for x in lanes]
        pieces.append(jnp.zeros((EXTRA - 2 * each, LANES), f32))
        parcel[j * size + rows : (j + 1) * size, :] = jnp.concatenate(pieces, axis=0).astype(bf16)


def opening_of(tap, head, tail):
    result = [[], []]
    for g in range(head.shape[0] // RAW):
        pair = [[], []]
        for side in range(2):
            weight = [
                tap[g * POLES + 3 + 3 * side + lag : g * POLES + 4 + 3 * side + lag, :]
                for lag in range(3)
            ]
            at = g * RAW + 4 * side
            line = [tail[at + 2 + r : at + 3 + r, :] for r in range(2)]
            line += [head[at + r : at + 1 + r, :] for r in range(2)]
            for t in range(2):
                pair[t].append(fir(weight, line[t + 2], line[t + 1], line[t]))
        for t in range(2):
            m = pair[t][0] * pair[t][1]
            result[t].append(jnp.broadcast_to(m, (POLES, LANES)))
    return [jnp.concatenate(x, axis=0) for x in result]


def piece_of(place, filters, decay):
    chans = decay.shape[1] // MINOR
    start = pl.multiple_of((place[0] % MINOR) * chans, LANES)
    rates = decay[:, pl.ds(start, chans)]
    taps = jnp.concatenate([filters[which, :, pl.ds(start, chans)] for which in range(3)], axis=0)
    taps = jnp.concatenate([taps, jnp.zeros((POLES - 9, chans), f32)], axis=0)
    return [
        jnp.concatenate([x[:, g : g + LANES] for g in range(0, chans, LANES)], axis=0)
        for x in (rates, taps)
    ]


def is_head(shape):
    return (lax.broadcasted_iota(jnp.int32, shape, 0) & 2) == 0


def not_extra(shape):
    return lax.broadcasted_iota(jnp.int32, shape, 0) < shape[0] - EXTRA


def minor_kernel(block, place, arrived, filters, decay_rate, sums, prefix):
    rate, tap = piece_of(place, filters, decay_rate)
    size = arrived.shape[0] // MINOR
    rows = rate.shape[0]
    decay = jnp.exp(-rate * block)
    late = [jnp.exp(-rate * (block - 1.0)), jnp.exp(-rate * (block - 2.0))]
    total = jnp.zeros((rows, LANES), f32)
    raw = []
    for b in range(MINOR):
        prefix[b * rows : (b + 1) * rows, :] = total
        total = decay * total + arrived[b * size : b * size + rows, :].astype(f32)
        raw.append(arrived[b * size + rows : (b + 1) * size, :].astype(f32))
        if b:
            m = opening_of(tap, raw[b][:-EXTRA], raw[b - 1])
            total = total + (late[0] * m[0] + late[1] * m[1])
    head = is_head(raw[0].shape) & not_extra(raw[0].shape)
    ends = jnp.where(head, raw[0], raw[-1]).astype(bf16)
    total = total.astype(bf16)
    for other in range(MIDDLE):
        sums[other * size : other * size + rows, :] = total
        sums[other * size + rows : (other + 1) * size, :] = ends


def lines_of(block, rate, tap, arrived, state, tail):
    size = arrived.shape[0] // MIDDLE
    rows = rate.shape[0]
    line_decay = jnp.exp(-rate * (block * MINOR))
    rest_decay = jnp.exp(-rate * (block * (MINOR - 1)))
    late = [jnp.exp(-rate * (block - 1.0)), jnp.exp(-rate * (block - 2.0))]
    entering, openings, tails = [], [], []
    for line in range(MIDDLE):
        raw = arrived[line * size + rows : (line + 1) * size, :].astype(f32)
        m = opening_of(tap, raw[:-EXTRA], tail)
        tails.append(tail)
        openings.append(late[0] * m[0] + late[1] * m[1])
        entering.append(state)
        piece = arrived[line * size : line * size + rows, :].astype(f32)
        state = line_decay * state + (piece + rest_decay * openings[-1])
        tail = raw
    return entering, openings, tails, state, tail


def ahead_kernel(block, place, arrived, filters, decay_rate, ahead):
    rate, tap = piece_of(place, filters, decay_rate)
    rows = rate.shape[0]
    begin = jnp.zeros((rows, LANES), f32), jnp.zeros((ahead.shape[0] - rows, LANES), f32)
    *_, state, tail = lines_of(block, rate, tap, arrived, *begin)
    ahead[:rows, :] = state.astype(bf16)
    ahead[rows:, :] = tail.astype(bf16)


def tail_rows(raw):
    at = raw.shape[0] - EXTRA
    rows = []
    for g in range(at // RAW):
        rows += [raw[g * RAW + 2 : g * RAW + 4], raw[g * RAW + 6 : g * RAW + 8]]
        rows += [raw[at + 2 * g : at + 2 * g + 2], jnp.zeros((2, LANES), f32)]
    return jnp.concatenate(rows, axis=0)


def middle_kernel(block, place, line, arrived, ahead, prefix, filters, decay_rate, carries):
    rate, tap = piece_of(place, filters, decay_rate)
    rows = rate.shape[0]
    mine = (place[0] // MINOR) % MIDDLE
    begin = ahead[:rows, :].astype(f32), ahead[rows:, :].astype(f32)
    entering, openings, tails, *_ = lines_of(block, rate, tap, arrived, *begin)
    before, own, tail = entering[0], openings[0], tails[0]
    for other in range(1, MIDDLE):
        before = jnp.where(mine == other, entering[other], before)
        own = jnp.where(mine == other, openings[other], own)
        tail = jnp.where(mine == other, tails[other], tail)
    decay = jnp.exp(-rate * block)
    size = line.shape[0] // MINOR
    out = carries.shape[0] // MINOR
    for b in range(MINOR):
        here = before + prefix[b * rows : (b + 1) * rows, :]
        if b:
            here = here + own
            own = decay * own
            tail = line[(b - 1) * size + rows : b * size, :].astype(f32)
        carries[b * out : b * out + rows, :] = here.astype(bf16)
        carries[b * out + rows : (b + 1) * out, :] = tail_rows(tail).astype(bf16)
        before = decay * before


def inner_kernel(
    upper, place, query_hbm, key_hbm, value_hbm, residual_hbm, residue_hbm, filters, decay, skip,
    base_hbm, feature_hbm, lead, heads,
    query_in, key_in, value_in, residual, residue, queries, keys, values, streams, feature,
    weights, rates, taps, sem, out_sem,
):
    tokens, chans = query_in.shape
    groups = chans // LANES
    halves = groups // SUBLANES
    width = SUBLANES * LANES
    lanes = (
        (query_hbm, query_in, queries),
        (key_hbm, key_in, keys),
        (value_hbm, value_in, values),
        (residual_hbm, residual, streams),
    )
    parts = out_sem.shape[0] // 2
    span = tokens * groups // parts

    @pl.when((place[0] >= MINOR * MIDDLE) == upper)
    def _():
        small = pltpu.make_async_copy(residue_hbm, residue, sem.at[0])
        small.start()
        copies = []
        for half in range(halves):
            columns = slice(half * width, (half + 1) * width)
            for i, (source, target, _) in enumerate(lanes):
                copies.append(
                    pltpu.make_async_copy(
                        source.at[:, columns], target.at[:, columns], sem.at[1 + 4 * half + i]
                    )
                )
                copies[-1].start()
        fill_tables(filters, decay, rates, taps)
        small.wait()
        for g in range(groups):
            weights[g * POLES : (g + 1) * POLES, :] = residue[:, g * LANES : (g + 1) * LANES]
        outward = []
        for half in range(halves):
            for i, (_, source, target) in enumerate(lanes):
                copies[4 * half + i].wait()
                columns = range(half * SUBLANES, (half + 1) * SUBLANES)
                spread(source, target, 0, columns, groups)
            for i in range(3):
                for t in range(HALO):
                    put(heads, HALO * i + t, half, groups, tile(lanes[i][2], t, half, groups))
            taps_here = [taps_of(taps, which, half) for which in range(3)]

            def filtered(i, carry):
                carry = list(carry)
                for u in range(STEP):
                    t = HALO + i * STEP + u
                    now = [tile(lanes[w][2], t, half, groups) for w in range(3)]
                    out = [
                        fir(taps_here[w], now[w], carry[2 * w], carry[2 * w + 1]) for w in range(3)
                    ]
                    put(feature, t, half, groups, out[0])
                    put(keys, t, half, groups, out[1] * out[2])
                    for w in range(3):
                        carry[2 * w + 1], carry[2 * w] = carry[2 * w], now[w]
                return tuple(carry)

            begin = tuple(tile(lanes[w][2], t, half, groups) for w in range(3) for t in (1, 0))
            lax.fori_loop(0, (tokens - HALO) // STEP, filtered, begin)
            for t in range(HALO):
                put(feature, t, half, groups, jnp.zeros((SUBLANES, LANES), f32))

            factor, weight = [], []
            for n in range(POLES):
                rate = rates[poled(n, half), :]
                factor.append(jnp.exp(-rate))
                weight.append(weights[poled(n, half), :] * jnp.sqrt(2.0 * rate))
                put(lead, n, half, groups, weight[n])
            direct = tile(skip, 0, half, groups)

            def turn(i, state):
                for u in range(STEP):
                    t = HALO + i * STEP + u
                    m = tile(keys, t, half, groups)
                    state = [factor[n] * state[n] + m for n in range(POLES)]
                    sums = [direct * m, weight[0] * state[0]]
                    for n in range(1, POLES):
                        sums[n % 2] = sums[n % 2] + weight[n] * state[n]
                    gated = tile(feature, t, half, groups) * (sums[0] + sums[1])
                    put(streams, t, half, groups, tile(streams, t, half, groups) + gated)
                return tuple(state)

            state = (jnp.zeros((SUBLANES, LANES), f32),) * POLES
            turns = (tokens - HALO) // STEP
            done = 0
            for p in range(parts):
                last = min(turns, -((HALO - (p + 1) * tokens // parts) // STEP))
                state = lax.fori_loop(done, last, turn, state)
                done = last
                if half == halves - 1:
                    rows = slice(span * p, span * (p + 1))
                    for i, (source, target) in enumerate(
                        ((streams, base_hbm), (feature, feature_hbm))
                    ):
                        outward.append(
                            pltpu.make_async_copy(
                                source.at[rows, :], target.at[rows, :], out_sem.at[2 * p + i]
                            )
                        )
                        outward[-1].start()
        for copy in outward:
            copy.wait()


def outer_kernel(
    place, carries, filters, decay, skip, lead_low, heads_low, lead_high, heads_high,
    base_low, feature_low, base_high, feature_high, summed, squares,
    carried, before, rates, taps, query, gated, sem,
):
    tokens, chans = summed.shape
    groups = chans // LANES
    lower = place[0] < MINOR * MIDDLE
    parts = sem.shape[0] // 2
    span = tokens // parts

    def copies_from(feature, base):
        copies = []
        for p in range(parts):
            part = slice(p * span * groups, (p + 1) * span * groups)
            for i, (source, target) in enumerate(((feature, query), (base, gated))):
                copies.append(
                    pltpu.make_async_copy(
                        source.at[part, :], target.at[part, :], sem.at[2 * p + i]
                    )
                )
        return copies

    copies = copies_from(feature_low, base_low)

    @pl.when(lower)
    def _():
        for copy in copies:
            copy.start()

    @pl.when(jnp.logical_not(lower))
    def _():
        for copy in copies_from(feature_high, base_high):
            copy.start()

    fill_tables(filters, decay, rates, taps)
    size = carries.shape[0] // MINOR
    rows = groups // MINOR * POLES
    for j in range(MINOR):
        piece = carries[j * size : (j + 1) * size, :].astype(f32)
        carried[j * rows : (j + 1) * rows, :] = piece[:rows]
        before[j * (size - rows) : (j + 1) * (size - rows), :] = piece[rows:]

    def chosen(low, high, item, half):
        return jnp.where(lower, tile(low, item, half, groups), tile(high, item, half, groups))

    for half in range(groups // SUBLANES):
        opening = []
        for i, at in enumerate((4, 0, 2)):
            line = [before[poled(at + r, half, RAW), :] for r in range(2)]
            line += [chosen(heads_low, heads_high, HALO * i + r, half) for r in range(2)]
            weight = taps_of(taps, i, half)
            opening.append([fir(weight, line[t + 2], line[t + 1], line[t]) for t in range(2)])
        mixed = [opening[1][t] * opening[2][t] for t in range(2)]
        factor, state, weight = [], [], []
        for n in range(POLES):
            factor.append(jnp.exp(-rates[poled(n, half), :]))
            weight.append(chosen(lead_low, lead_high, n, half))
            state.append(weight[n] * (factor[n] * carried[poled(n, half), :] + mixed[0]))
        direct = tile(skip, 0, half, groups)

        def total_of(state, first):
            sums = [state[0] if first is None else first + state[0], state[1]]
            for n in range(2, POLES):
                sums[n % 2] = sums[n % 2] + state[n]
            return sums[0] + sums[1]

        start = []
        for t in range(HALO):
            if t:
                state = [factor[n] * state[n] + weight[n] * mixed[t] for n in range(POLES)]
            start.append(opening[0][t] * total_of(state, direct * mixed[t]))
        state = tuple(factor[n] * state[n] for n in range(POLES))

        def turn(i, state):
            for u in range(STEP):
                t = HALO + i * STEP + u
                added = tile(query, t, half, groups) * total_of(state, None)
                put(gated, t, half, groups, tile(gated, t, half, groups) + added)
                state = tuple(factor[n] * state[n] for n in range(POLES))
            return state

        turns = (tokens - HALO) // STEP
        done = 0
        for p in range(parts):
            if half == 0:
                copies[2 * p].wait()
                copies[2 * p + 1].wait()
            if p == 0:
                for t in range(HALO):
                    put(gated, t, half, groups, tile(gated, t, half, groups) + start[t])
            last = turns if p == parts - 1 else ((p + 1) * span - HALO) // STEP
            state = lax.fori_loop(done, last, turn, state)
            done = last
    total = jnp.zeros((tokens, LANES), f32)
    for g in range(groups):
        value = gated[pl.ds(g, tokens, stride=groups), :].astype(bf16)
        summed[:, g * LANES : (g + 1) * LANES] = value
        value = value.astype(f32)
        total = total + value * value
    squares[...] = jnp.broadcast_to(jnp.sum(total.T, axis=0, keepdims=True), squares.shape)


def norm_kernel(summed, squares, gain, stream_out, normed_out, normed, sem):
    tokens, chans = summed.shape
    parts = 4
    width = chans // parts
    stream = pltpu.make_async_copy(summed, stream_out, sem.at[parts])
    stream.start()
    mean = jnp.sum(squares[...], axis=0, keepdims=True) / D
    inverse = jnp.broadcast_to(lax.rsqrt(mean + EPSILON), (LANES, tokens)).T
    copies = []
    for part in range(parts):
        for g in range(part * width // LANES, (part + 1) * width // LANES):
            columns = slice(g * LANES, (g + 1) * LANES)
            normed[:, columns] = (
                summed[:, columns].astype(f32) * inverse * gain[g : g + 1, :]
            ).astype(bf16)
        columns = slice(part * width, (part + 1) * width)
        copies.append(
            pltpu.make_async_copy(normed.at[:, columns], normed_out.at[:, columns], sem.at[part])
        )
        copies[part].start()
    for copy in copies:
        copy.wait()
    stream.wait()


def layer(
    residual, query_in, key_in, value_in, short_filter, decay_rate, residue, skip_gain, norm_gain
):
    tokens, chans = residual.shape
    groups = chans // LANES
    count = MINOR * MIDDLE * MAJOR
    block = float(tokens)

    def shape(rows, kind=f32):
        return jax.ShapeDtypeStruct((rows, LANES), kind)

    def hold(rows):
        return pltpu.VMEM((rows, LANES), f32)

    smem = pl.BlockSpec(memory_space=pltpu.SMEM)
    vmem = pl.BlockSpec(memory_space=pltpu.VMEM)
    hbm = pl.BlockSpec(memory_space=pltpu.HBM)
    wide = pltpu.VMEM((tokens, chans), bf16)
    poled_rows = POLES * groups
    parcel_rows = (POLES + RAW) * groups + EXTRA * MINOR

    parcel = call(
        first_kernel,
        shape(parcel_rows, bf16),
        room=10.1,
        in_specs=[hbm] * 5,
        scratch=[
            wide,
            wide,
            pltpu.VMEM((8, chans), bf16),
            pltpu.VMEM(short_filter.shape, f32),
            pltpu.VMEM(decay_rate.shape, f32),
            hold(tokens * groups),
            hold(tokens * groups),
            hold(poled_rows),
            hold(poled_rows),
            hold(poled_rows),
            pltpu.SemaphoreType.DMA((3 + 2 * (groups // SUBLANES),)),
        ],
    )(query_in, key_in, value_in, short_filter, decay_rate)

    place = lax.axis_index("seq").astype(jnp.int32).reshape(1)
    lines = [[g * MINOR + j for j in range(MINOR)] for g in range(MIDDLE * MAJOR)]
    planes = [
        [(z * MIDDLE + y) * MINOR + j for y in range(MIDDLE)]
        for z in range(MAJOR)
        for j in range(MINOR)
    ]

    def exchange(x, members):
        return lax.all_to_all(x, "seq", 0, 0, axis_index_groups=members, tiled=True)

    tables_in = (short_filter, decay_rate)
    parcel, place = lax.optimization_barrier((parcel, place))
    arrived = exchange(parcel, lines)
    sums, prefix = call(
        functools.partial(minor_kernel, block),
        (shape(parcel_rows, bf16), shape(poled_rows)),
        in_specs=[smem, vmem, vmem, vmem],
    )(place, arrived, *tables_in)
    line = arrived
    arrived = exchange(sums, planes)
    ahead = call(
        functools.partial(ahead_kernel, block),
        shape(parcel_rows // MINOR, bf16),
        in_specs=[smem, vmem, vmem, vmem],
    )(place, arrived, *tables_in)
    skip = skip_gain.reshape(groups, LANES)

    def inner(upper, place):
        return call(
            functools.partial(inner_kernel, upper),
            (
                shape(tokens * groups),
                shape(tokens * groups),
                shape(poled_rows),
                shape(3 * HALO * groups),
            ),
            room=11.5,
            in_specs=[smem] + [hbm] * 5 + [vmem] * 3,
            out_specs=(hbm, hbm, vmem, vmem),
            scratch=[wide] * 4
            + [pltpu.VMEM(residue.shape, f32)]
            + [hold(tokens * groups)] * 5
            + [hold(poled_rows)] * 3
            + [pltpu.SemaphoreType.DMA((1 + 4 * (groups // SUBLANES),))]
            + [pltpu.SemaphoreType.DMA((8,))],
        )(place, query_in, key_in, value_in, residual, residue, *tables_in, skip)

    place, ahead = lax.optimization_barrier((place, ahead))
    low = inner(False, place)
    *low, ahead = lax.optimization_barrier((*low, ahead))
    ahead = lax.ppermute(ahead, "seq", [(i, i + count // 2) for i in range(count // 2)])
    high = inner(True, place)
    carries = call(
        functools.partial(middle_kernel, block),
        shape(poled_rows + RAW * groups, bf16),
        in_specs=[smem] + [vmem] * 6,
    )(place, line, arrived, ahead, prefix, *tables_in)
    carries = exchange(carries, lines)
    members = lax.axis_size("chan")
    summed, squares = call(
        outer_kernel,
        (
            jax.ShapeDtypeStruct((tokens, chans), bf16),
            jax.ShapeDtypeStruct((members, tokens), f32),
        ),
        room=11.5,
        in_specs=[smem] + [vmem] * 8 + [hbm] * 4,
        scratch=[
            hold(poled_rows),
            hold(RAW * groups),
            hold(poled_rows),
            hold(poled_rows),
            hold(tokens * groups),
            hold(tokens * groups),
            pltpu.SemaphoreType.DMA((8,)),
        ],
    )(
        place,
        carries,
        *tables_in,
        skip,
        low[2],
        low[3],
        high[2],
        high[3],
        low[0],
        low[1],
        high[0],
        high[1],
    )
    squares = lax.all_to_all(squares, "chan", 0, 0, tiled=True)
    whole = jax.ShapeDtypeStruct((tokens, chans), bf16)
    return call(
        norm_kernel,
        (whole, whole),
        in_specs=[vmem] * 3,
        out_specs=(hbm, hbm),
        scratch=[wide, pltpu.SemaphoreType.DMA((5,))],
    )(summed, squares, norm_gain.reshape(groups, LANES))


def solution(mesh):
    whole = P("seq", "chan")
    in_specs = (whole, whole, whole, whole, P(None, None, "chan"))
    in_specs += (P(None, "chan"), P(None, "chan"), P("chan"), P("chan"))
    return jax.shard_map(
        layer, mesh=mesh, in_specs=in_specs, out_specs=(whole, whole), check_vma=False
    )
```

time: 77.7 us -> 69.1 us (0.89)
  the two profiles are of different devices: /device:TPU:63 before, /device:TPU:1 now
where the time goes in v5:
time: 69.1 us; the launch traced here: 68.5 us
  blocking collectives  34.2 us (49%)
  Pallas kernels  17.2 us (25%)
  starting transfers between devices  9.88 us (14%)
  waiting for transfers between devices  5.67 us (8%)
  local copies, waits for them, and re-layouts  0.79 us (1%)
  between operations  0.72 us (1%)
    all_to_all x2, blocking collectives, exchange(): return lax.all_to_all(x, 'seq', 0, 0, axis_index_groups=members, tiled=True)  25.5 us
    all_to_all x1, blocking collectives, layer(): squares = lax.all_to_all(squares, 'chan', 0, 0, tiled=True)  8.78 us
    pallas_call x2, Pallas kernels, inner(): call(functools.partial(inner_kernel, upper), (shape(tokens * groups), sha...  7.5 us
    all_to_all x1, starting transfers between devices, exchange(): return lax.all_to_all(x, 'seq', 0, 0, axis_index_groups=members, tiled=True)  6.34 us
    all_to_all x1, waiting for transfers between devices, exchange(): return lax.all_to_all(x, 'seq', 0, 0, axis_index_groups=members, tiled=True)  4.84 us
    pallas_call x1, Pallas kernels, layer(): call(first_kernel, shape(parcel_rows, bf16), room=10.1, in_specs=[hbm] *...  4.66 us
    ppermute x1, starting transfers between devices, layer(): lax.ppermute(ahead, 'seq', [(i, i + count // 2) for i in range(count // 2)])  3.54 us
    pallas_call x1, Pallas kernels, layer(): call(outer_kernel, (jax.ShapeDtypeStruct((tokens, chans), bf16), jax.Shap...  2.95 us
  transfers between devices with their start and end apart: 2, of which 2 were waited for; matrix products, arithmetic and copies ran while one was open for 0% of the time, Pallas kernels for 0%

profile of v5, /device:TPU:1, one launch (start us, length us, event | category | flops | bytes accessed | tf_op | source)
XLA Modules:
  0.0 68.5 jit_solution(3806459640056283859)
XLA Ops:
  0.6 4.7 %shard_map.104 = bf16[448,128]{1,0:T(8,128)(2,1)} custom-call(bf16[128,2048]{1,0:T(8,128)(2,1)} %query_hbm.3, bf16[128,2048]{1,0:T(8,128)(2,1)} %key_hbm.3, bf16[128,2048]{1,0:T(8,128)(2,1)} %value_hbm.3, f32[3,3,2048]{2,1,0:T(4,128)} %filters.11, f32[16,2048]{1,0:T(8,128)} %decay.5), custom_call_target="tpu_custom_call" | custom-call | tf_op jit(solution)/shard_map/pallas_call | solution.py:539
  5.3 0.0 copy-start
  5.3 0.0 copy-start.1
  5.3 15.3 %all_to_all.44 = bf16[8,56,128]{2,1,0:T(8,128)(2,1)S(1)} all-to-all(bf16[8,56,128]{2,1,0:T(8,128)(2,1)} %bitcast.25), channel_id=1, replica_groups={{0,4,8,12,16,20,24,28},{32,36,40,44,48,52,56,60},{64,68,72,76,80,84,88,..., dimensions={0} | all-to-all | bytes 229376 | tf_op jit(solution)/shard_map/all_to_all | solution.py:568
  20.7 0.0 copy-start.2
  20.7 0.0 copy-done
  20.7 0.0 copy-done.1
  20.7 0.1 shard_map.105
  20.8 10.1 %all_to_all.45 = bf16[8,56,128]{2,1,0:T(8,128)(2,1)S(1)} all-to-all(bf16[8,56,128]{2,1,0:T(8,128)(2,1)S(1)} %bitcast.18), channel_id=1, replica_groups={{0,32,64,96,128,160,192,224},{4,36,68,100,132,164,196,228},{8,40,72,104..., dimensions={0} | all-to-all | bytes 229376 | tf_op jit(solution)/shard_map/all_to_all | solution.py:568
  30.9 0.0 copy-start.3
  30.9 0.0 copy-start.4
  30.9 0.1 shard_map.106
  31.1 0.0 copy-done.2
  31.1 0.8 %copy-done.3 = f32[16,2048]{1,0:T(8,128)S(1)} copy-done((f32[16,2048]{1,0:T(8,128)S(1)}, f32[16,2048]{1,0:T(8,128)}, u32[]{:S(2)}) %copy-start.3) | copy-done | bytes 131096
  31.8 0.0 copy-done.4
  31.8 7.3 %shard_map.107 = (f32[2048,128]{1,0:T(8,128)}, f32[2048,128]{1,0:T(8,128)}, f32[256,128]{1,0:T(8,128)S(1)}, f32[96,128]{1,0:T(8,128)S(1)}) custom-call(s32[1]{0:T(128)} %bitcast.place, bf16[128,2048]{1,0:T(8,128)(2,1)S(1)} %copy-done.2, bf16[128,2048]{1,0:T(8,128)(2,1)} %key_hbm.3, bf16[128,2048]{1,0:T(8,128)(2,1)} %value_hbm.3, ...), custom_call_target="tpu_custom_call" | custom-call | tf_op jit(solution)/shard_map/pallas_call | solution.py:588
  39.2 3.5 %collective-permute-start = (bf16[56,128]{1,0:T(8,128)(2,1)S(1)}, bf16[56,128]{1,0:T(8,128)(2,1)S(1)}, u32[]{:S(2)}, u32[]{:S(2)}) collective-permute-start(bf16[56,128]{1,0:T(8,128)(2,1)S(1)} %shard_map.106), channel_id=1, source_target_pairs={{0,256},{4,260},{8,264},{12,268},{16,272},{20,276},{24,280},{28,28... | collective-permute-start | bytes 43016 | tf_op jit(solution)/shard_map/ppermute | solution.py:610
  42.7 0.8 %collective-permute-done.ahead = bf16[56,128]{1,0:T(8,128)(2,1)S(1)} collective-permute-done((bf16[56,128]{1,0:T(8,128)(2,1)S(1)}, bf16[56,128]{1,0:T(8,128)(2,1)S(1)}, u32[]{:S(2)}, u32[]{:S(2)}) %collective-permute-start) | collective-permute-done | bytes 14368 | tf_op jit(solution)/shard_map/ppermute | solution.py:610
  43.6 0.8 %shard_map.108 = bf16[384,128]{1,0:T(8,128)(2,1)} custom-call(s32[1]{0:T(128)} %bitcast.place, bf16[448,128]{1,0:T(8,128)(2,1)S(1)} %bitcast.14, bf16[448,128]{1,0:T(8,128)(2,1)S(1)} %bitcast.16, bf16[56,128]{1,0:T(8,128)(2,1)S(1)} %collective-permute-done.ahead, f32[256,128]{1,0:T(8,128)S(1)} %get-tuple-element.33.prefix, f32[3,3,2048]{2,1,0:T(4,128)S(1)} %copy-done.1, ...), custom_call_target="tpu_custom_call" | custom-call | tf_op jit(solution)/shard_map/pallas_call | solution.py:612
  44.4 6.3 %all-to-all-start.2 = ((bf16[8,48,128]{2,1,0:T(8,128)(2,1)}), bf16[8,48,128]{2,1,0:T(8,128)(2,1)S(1)}, u32[]{:S(2)}, u32[]{:S(2)}) async-start(bf16[8,48,128]{2,1,0:T(8,128)(2,1)} %bitcast.6), calls=%async_computation.2 | async-start | bytes 196608 | tf_op jit(solution)/shard_map/all_to_all | solution.py:568
  50.7 0.2 shard_map.109
  50.9 4.8 %all-to-all-done.2 = bf16[8,48,128]{2,1,0:T(8,128)(2,1)S(1)} async-done(((bf16[8,48,128]{2,1,0:T(8,128)(2,1)}), bf16[8,48,128]{2,1,0:T(8,128)(2,1)S(1)}, u32[]{:S(2)}, u32[]{:S(2)}) %all-to-all-start.2) | async-done | bytes 98336 | tf_op jit(solution)/shard_map/all_to_all | solution.py:568
  55.7 2.9 %shard_map.110 = (bf16[128,2048]{1,0:T(8,128)(2,1)S(1)}, f32[4,128]{1,0:T(4,128)S(1)}) custom-call(s32[1]{0:T(128)} %bitcast.place, bf16[384,128]{1,0:T(8,128)(2,1)S(1)} %bitcast.17, f32[3,3,2048]{2,1,0:T(4,128)S(1)} %copy-done.1, f32[16,2048]{1,0:T(8,128)S(1)} %copy-done, f32[16,128]{1,0:T(8,128)S(1)} %bitcast.21, ...), custom_call_target="tpu_custom_call" | custom-call | tf_op jit(solution)/shard_map/pallas_call | solution.py:619
  58.7 0.0 copy-start.5
  58.7 8.8 %all_to_all.46 = f32[4,1,128]{2,1,0:T(1,128)S(1)} all-to-all(f32[4,1,128]{2,1,0:T(1,128)S(1)} %bitcast.24), channel_id=1, replica_groups=mesh['seq'=128,'chan'=4] {'chan'}, dimensions={0} | all-to-all | bytes 4096 | tf_op jit(solution)/shard_map/all_to_all | solution.py:650
  67.5 0.0 copy-done.5
  67.5 1.0 %shard_map.111 = (bf16[128,2048]{1,0:T(8,128)(2,1)}, bf16[128,2048]{1,0:T(8,128)(2,1)}) custom-call(bf16[128,2048]{1,0:T(8,128)(2,1)S(1)} %get-tuple-element.42.summed, f32[4,128]{1,0:T(4,128)S(1)} %bitcast.23, f32[16,128]{1,0:T(8,128)S(1)} %bitcast.22), custom_call_target="tpu_custom_call" | custom-call | tf_op jit(solution)/shard_map/pallas_call | solution.py:652
Async XLA Ops:
  5.3 15.4 %copy-start = (f32[16,2048]{1,0:T(8,128)S(1)}, f32[16,2048]{1,0:T(8,128)}, u32[]{:S(2)}) copy-start(f32[16,2048]{1,0:T(8,128)} %decay.5) | copy-start | bytes 393220
  5.3 15.4 %copy-start.1 = (f32[3,3,2048]{2,1,0:T(4,128)S(1)}, f32[3,3,2048]{2,1,0:T(4,128)}, u32[]{:S(2)}) copy-start(f32[3,3,2048]{2,1,0:T(4,128)} %filters.11) | copy-start | bytes 221188
  20.7 10.4 %copy-start.2 = (bf16[128,2048]{1,0:T(8,128)(2,1)S(1)}, bf16[128,2048]{1,0:T(8,128)(2,1)}, u32[]{:S(2)}) copy-start(bf16[128,2048]{1,0:T(8,128)(2,1)} %query_hbm.3) | copy-start | bytes 1572868
  30.9 0.9 %copy-start.3 = (f32[16,2048]{1,0:T(8,128)S(1)}, f32[16,2048]{1,0:T(8,128)}, u32[]{:S(2)}) copy-start(f32[16,2048]{1,0:T(8,128)} %residue_hbm.3) | copy-start | bytes 393220
  30.9 0.9 %copy-start.4 = (f32[2048]{0:T(1024)S(1)}, f32[2048]{0:T(1024)}, u32[]{:S(2)}) copy-start(f32[2048]{0:T(1024)} %param.16) | copy-start | bytes 24580
  39.2 4.4 %collective-permute-start = (bf16[56,128]{1,0:T(8,128)(2,1)S(1)}, bf16[56,128]{1,0:T(8,128)(2,1)S(1)}, u32[]{:S(2)}, u32[]{:S(2)}) collective-permute-start(bf16[56,128]{1,0:T(8,128)(2,1)S(1)} %shard_map.106), channel_id=1, source_target_pairs={{0,256},{4,260},{8,264},{12,268},{16,272},{20,276},{24,280},{28,28... | collective-permute-start | bytes 43016 | tf_op jit(solution)/shard_map/ppermute | solution.py:610
  44.4 11.3 %all-to-all-start.2 = ((bf16[8,48,128]{2,1,0:T(8,128)(2,1)}), bf16[8,48,128]{2,1,0:T(8,128)(2,1)S(1)}, u32[]{:S(2)}, u32[]{:S(2)}) async-start(bf16[8,48,128]{2,1,0:T(8,128)(2,1)} %bitcast.6), calls=%async_computation.2 | async-start | bytes 196608 | tf_op jit(solution)/shard_map/all_to_all | solution.py:568
  58.7 8.8 %copy-start.5 = (f32[2048]{0:T(1024)S(1)}, f32[2048]{0:T(1024)}, u32[]{:S(2)}) copy-start(f32[2048]{0:T(1024)} %param.17) | copy-start | bytes 24580

commit v6 on v5

--- a/solution.py
+++ b/solution.py
@@ -15,7 +15,8 @@
 MINOR = 8
 MIDDLE = 8
 MAJOR = 2
-STEP = 6
+STEP = 9
+LONG_STEP = 18
 HALO = 2
 RAW = 8
 EXTRA = 8
@@ -39,23 +40,25 @@
 
 def spread(source, target, first, columns, groups):
     items = source.shape[0]
+    every = target.shape[0] // groups
     for g in columns:
-        target[pl.ds(first * groups + g, items, stride=groups), :] = source[
+        start = (g // SUBLANES * every + first) * SUBLANES + g % SUBLANES
+        target[pl.ds(start, items, stride=SUBLANES), :] = source[
             :, g * LANES : (g + 1) * LANES
         ].astype(f32)
 
 
-def start_of(item, half, groups):
-    start = item * groups + half * SUBLANES
-    return start if isinstance(start, int) else pl.multiple_of(start, SUBLANES)
+def at_tile(ref, item, half, groups):
+    start = (half * (ref.shape[0] // groups) + item) * SUBLANES
+    return pl.ds(start if isinstance(start, int) else pl.multiple_of(start, SUBLANES), SUBLANES)
 
 
 def tile(ref, item, half, groups):
-    return ref[pl.ds(start_of(item, half, groups), SUBLANES), :]
+    return ref[at_tile(ref, item, half, groups), :]
 
 
 def put(ref, item, half, groups, value):
-    ref[pl.ds(start_of(item, half, groups), SUBLANES), :] = value
+    ref[at_tile(ref, item, half, groups), :] = value
 
 
 def poled(item, half, stride=POLES):
@@ -124,8 +127,8 @@
 
         def turn(i, carry):
             k1, k2, v1, v2, *state = carry
-            for u in range(STEP):
-                t = HALO + i * STEP + u
+            for u in range(LONG_STEP):
+                t = HALO + i * LONG_STEP + u
                 k0 = tile(keys, t, half, groups)
                 v0 = tile(values, t, half, groups)
                 m = fir(key_taps, k0, k1, k2) * fir(value_taps, v0, v1, v2)
@@ -135,7 +138,7 @@
 
         begin = tuple(tile(x, t, half, groups) for x in (keys, values) for t in (1, 0))
         begin += (jnp.zeros((SUBLANES, LANES), f32),) * POLES
-        end = lax.fori_loop(0, (tokens - HALO) // STEP, turn, begin)
+        end = lax.fori_loop(0, (tokens - HALO) // LONG_STEP, turn, begin)
         for n in range(POLES):
             states[poled(n, half), :] = end[4 + n]
     small[2].wait()
@@ -193,7 +196,8 @@
     return lax.broadcasted_iota(jnp.int32, shape, 0) < shape[0] - EXTRA
 
 
-def minor_kernel(block, place, arrived, filters, decay_rate, sums, prefix):
+def minor_kernel(block, place, arrived, filters, decay_rate, skip, sums, prefix):
+    del skip
     rate, tap = piece_of(place, filters, decay_rate)
     size = arrived.shape[0] // MINOR
     rows = rate.shape[0]
@@ -279,9 +283,8 @@
 
 
 def inner_kernel(
-    upper, place, query_hbm, key_hbm, value_hbm, residual_hbm, residue_hbm, filters, decay, skip,
-    base_hbm, feature_hbm, lead, heads,
-    query_in, key_in, value_in, residual, residue, queries, keys, values, streams, feature,
+    upper, place, query_hbm, key_hbm, value_hbm, residual_hbm, residue_hbm, skip_hbm, filters, decay,
+    base_hbm, feature_hbm, heads, skip, query_in, key_in, value_in, residual, residue, queries, keys, values, streams, feature,
     weights, rates, taps, sem, out_sem,
 ):
     tokens, chans = query_in.shape
@@ -294,25 +297,30 @@
         (value_hbm, value_in, values),
         (residual_hbm, residual, streams),
     )
-    parts = out_sem.shape[0] // 2
-    span = tokens * groups // parts
+    parts = out_sem.shape[0] // (2 * halves)
+    span = tokens * SUBLANES // parts
 
     @pl.when((place[0] >= MINOR * MIDDLE) == upper)
     def _():
-        small = pltpu.make_async_copy(residue_hbm, residue, sem.at[0])
-        small.start()
+        small = [
+            pltpu.make_async_copy(residue_hbm, residue, sem.at[0]),
+            pltpu.make_async_copy(skip_hbm, skip, sem.at[1]),
+        ]
+        for copy in small:
+            copy.start()
         copies = []
         for half in range(halves):
             columns = slice(half * width, (half + 1) * width)
             for i, (source, target, _) in enumerate(lanes):
                 copies.append(
                     pltpu.make_async_copy(
-                        source.at[:, columns], target.at[:, columns], sem.at[1 + 4 * half + i]
+                        source.at[:, columns], target.at[:, columns], sem.at[2 + 4 * half + i]
                     )
                 )
                 copies[-1].start()
         fill_tables(filters, decay, rates, taps)
-        small.wait()
+        for copy in small:
+            copy.wait()
         for g in range(groups):
             weights[g * POLES : (g + 1) * POLES, :] = residue[:, g * LANES : (g + 1) * LANES]
         outward = []
@@ -350,7 +358,6 @@
                 rate = rates[poled(n, half), :]
                 factor.append(jnp.exp(-rate))
                 weight.append(weights[poled(n, half), :] * jnp.sqrt(2.0 * rate))
-                put(lead, n, half, groups, weight[n])
             direct = tile(skip, 0, half, groups)
 
             def turn(i, state):
@@ -372,36 +379,36 @@
                 last = min(turns, -((HALO - (p + 1) * tokens // parts) // STEP))
                 state = lax.fori_loop(done, last, turn, state)
                 done = last
-                if half == halves - 1:
-                    rows = slice(span * p, span * (p + 1))
-                    for i, (source, target) in enumerate(
-                        ((streams, base_hbm), (feature, feature_hbm))
-                    ):
-                        outward.append(
-                            pltpu.make_async_copy(
-                                source.at[rows, :], target.at[rows, :], out_sem.at[2 * p + i]
-                            )
+                rows = slice(span * (parts * half + p), span * (parts * half + p + 1))
+                for i, (source, target) in enumerate(
+                    ((streams, base_hbm), (feature, feature_hbm))
+                ):
+                    slot = 2 * (parts * half + p) + i
+                    outward.append(
+                        pltpu.make_async_copy(
+                            source.at[rows, :], target.at[rows, :], out_sem.at[slot]
                         )
-                        outward[-1].start()
+                    )
+                    outward[-1].start()
         for copy in outward:
             copy.wait()
 
 
 def outer_kernel(
-    place, carries, filters, decay, skip, lead_low, heads_low, lead_high, heads_high,
+    place, carries, filters, decay, residue, skip, heads_low, heads_high,
     base_low, feature_low, base_high, feature_high, summed, squares,
-    carried, before, rates, taps, query, gated, sem,
+    carried, before, rates, taps, weights, query, gated, sem,
 ):
     tokens, chans = summed.shape
     groups = chans // LANES
     lower = place[0] < MINOR * MIDDLE
-    parts = sem.shape[0] // 2
+    parts = sem.shape[0] // (2 * (groups // SUBLANES))
     span = tokens // parts
 
     def copies_from(feature, base):
         copies = []
-        for p in range(parts):
-            part = slice(p * span * groups, (p + 1) * span * groups)
+        for p in range(sem.shape[0] // 2):
+            part = slice(p * span * SUBLANES, (p + 1) * span * SUBLANES)
             for i, (source, target) in enumerate(((feature, query), (base, gated))):
                 copies.append(
                     pltpu.make_async_copy(
@@ -423,6 +430,8 @@
             copy.start()
 
     fill_tables(filters, decay, rates, taps)
+    for g in range(groups):
+        weights[g * POLES : (g + 1) * POLES, :] = residue[:, g * LANES : (g + 1) * LANES]
     size = carries.shape[0] // MINOR
     rows = groups // MINOR * POLES
     for j in range(MINOR):
@@ -443,8 +452,9 @@
         mixed = [opening[1][t] * opening[2][t] for t in range(2)]
         factor, state, weight = [], [], []
         for n in range(POLES):
-            factor.append(jnp.exp(-rates[poled(n, half), :]))
-            weight.append(chosen(lead_low, lead_high, n, half))
+            rate = rates[poled(n, half), :]
+            factor.append(jnp.exp(-rate))
+            weight.append(weights[poled(n, half), :] * jnp.sqrt(2.0 * rate))
             state.append(weight[n] * (factor[n] * carried[poled(n, half), :] + mixed[0]))
         direct = tile(skip, 0, half, groups)
 
@@ -472,9 +482,8 @@
         turns = (tokens - HALO) // STEP
         done = 0
         for p in range(parts):
-            if half == 0:
-                copies[2 * p].wait()
-                copies[2 * p + 1].wait()
+            for copy in copies[2 * (parts * half + p) : 2 * (parts * half + p + 1)]:
+                copy.wait()
             if p == 0:
                 for t in range(HALO):
                     put(gated, t, half, groups, tile(gated, t, half, groups) + start[t])
@@ -483,7 +492,8 @@
             done = last
     total = jnp.zeros((tokens, LANES), f32)
     for g in range(groups):
-        value = gated[pl.ds(g, tokens, stride=groups), :].astype(bf16)
+        start = g // SUBLANES * tokens * SUBLANES + g % SUBLANES
+        value = gated[pl.ds(start, tokens, stride=SUBLANES), :].astype(bf16)
         summed[:, g * LANES : (g + 1) * LANES] = value
         value = value.astype(f32)
         total = total + value * value
@@ -568,13 +578,14 @@
         return lax.all_to_all(x, "seq", 0, 0, axis_index_groups=members, tiled=True)
 
     tables_in = (short_filter, decay_rate)
+    skip = skip_gain.reshape(groups, LANES)
     parcel, place = lax.optimization_barrier((parcel, place))
     arrived = exchange(parcel, lines)
     sums, prefix = call(
         functools.partial(minor_kernel, block),
         (shape(parcel_rows, bf16), shape(poled_rows)),
-        in_specs=[smem, vmem, vmem, vmem],
-    )(place, arrived, *tables_in)
+        in_specs=[smem, vmem, vmem, vmem, vmem],
+    )(place, arrived, *tables_in, skip)
     line = arrived
     arrived = exchange(sums, planes)
     ahead = call(
@@ -582,7 +593,6 @@
         shape(parcel_rows // MINOR, bf16),
         in_specs=[smem, vmem, vmem, vmem],
     )(place, arrived, *tables_in)
-    skip = skip_gain.reshape(groups, LANES)
 
     def inner(upper, place):
         return call(
@@ -590,19 +600,19 @@
             (
                 shape(tokens * groups),
                 shape(tokens * groups),
-                shape(poled_rows),
                 shape(3 * HALO * groups),
             ),
-            room=11.5,
-            in_specs=[smem] + [hbm] * 5 + [vmem] * 3,
-            out_specs=(hbm, hbm, vmem, vmem),
-            scratch=[wide] * 4
+            room=10.25,
+            in_specs=[smem] + [hbm] * 6 + [vmem] * 2,
+            out_specs=(hbm, hbm, vmem),
+            scratch=[hold(groups)]
+            + [wide] * 4
             + [pltpu.VMEM(residue.shape, f32)]
             + [hold(tokens * groups)] * 5
             + [hold(poled_rows)] * 3
-            + [pltpu.SemaphoreType.DMA((1 + 4 * (groups // SUBLANES),))]
-            + [pltpu.SemaphoreType.DMA((8,))],
-        )(place, query_in, key_in, value_in, residual, residue, *tables_in, skip)
+            + [pltpu.SemaphoreType.DMA((2 + 4 * (groups // SUBLANES),))]
+            + [pltpu.SemaphoreType.DMA((16,))],
+        )(place, query_in, key_in, value_in, residual, residue, skip, *tables_in)
 
     place, ahead = lax.optimization_barrier((place, ahead))
     low = inner(False, place)
@@ -623,25 +633,25 @@
             jax.ShapeDtypeStruct((members, tokens), f32),
         ),
         room=11.5,
-        in_specs=[smem] + [vmem] * 8 + [hbm] * 4,
+        in_specs=[smem] + [vmem] * 7 + [hbm] * 4,
         scratch=[
             hold(poled_rows),
             hold(RAW * groups),
             hold(poled_rows),
             hold(poled_rows),
+            hold(poled_rows),
             hold(tokens * groups),
             hold(tokens * groups),
-            pltpu.SemaphoreType.DMA((8,)),
+            pltpu.SemaphoreType.DMA((16,)),
         ],
     )(
         place,
         carries,
         *tables_in,
+        residue,
         skip,
         low[2],
-        low[3],
         high[2],
-        high[3],
         low[0],
         low[1],
         high[0],

time: 69.1 us -> 68.1 us (0.986)
  starting transfers between devices: 9.88 us -> 11.1 us
  waiting for transfers between devices: 5.67 us -> 4.62 us
  local copies, waits for them, and re-layouts: 0.79 us -> 0.04 us
    ppermute x1, starting transfers between devices: 3.54 us -> 4.71 us  [layer(): lax.ppermute(ahead, 'seq', [(i, i + count // 2) for i in range(count // 2)])]
    all_to_all x1, waiting for transfers between devices: 4.84 us -> 3.78 us  [exchange(): return lax.all_to_all(x, 'seq', 0, 0, axis_index_groups=members, tiled=True)]
    pallas_call x2, Pallas kernels: 7.5 us -> 8.43 us  [inner(): call(functools.partial(inner_kernel, upper), (shape(tokens * groups), sha...]
    unnamed x12 -> x14, local copies, waits for them, and re-layouts: 0.79 us -> 0.04 us
  transfers between devices with their start and end apart: 2 -> 2, of which waited for: 2 -> 2; matrix products, arithmetic and copies ran while one was open for 0% -> 0% of each run, Pallas kernels for 0% -> 2%
where the time goes in v6:
time: 68.1 us; the launch traced here: 67.6 us
  blocking collectives  33.8 us (50%)
  Pallas kernels  17.3 us (25%)
  starting transfers between devices  11.1 us (16%)
  waiting for transfers between devices  4.62 us (7%)
  between operations  0.73 us (1%)
    all_to_all x2, blocking collectives, exchange(): return lax.all_to_all(x, 'seq', 0, 0, axis_index_groups=members, tiled=True)  25.3 us
    all_to_all x1, blocking collectives, layer(): squares = lax.all_to_all(squares, 'chan', 0, 0, tiled=True)  8.51 us
    pallas_call x2, Pallas kernels, inner(): call(functools.partial(inner_kernel, upper), (shape(tokens * groups), sha...  8.43 us
    all_to_all x1, starting transfers between devices, exchange(): return lax.all_to_all(x, 'seq', 0, 0, axis_index_groups=members, tiled=True)  6.34 us
    ppermute x1, starting transfers between devices, layer(): lax.ppermute(ahead, 'seq', [(i, i + count // 2) for i in range(count // 2)])  4.71 us
    pallas_call x1, Pallas kernels, layer(): call(first_kernel, shape(parcel_rows, bf16), room=10.1, in_specs=[hbm] *...  3.98 us
    all_to_all x1, waiting for transfers between devices, exchange(): return lax.all_to_all(x, 'seq', 0, 0, axis_index_groups=members, tiled=True)  3.78 us
    pallas_call x1, Pallas kernels, layer(): call(outer_kernel, (jax.ShapeDtypeStruct((tokens, chans), bf16), jax.Shap...  2.78 us
  transfers between devices with their start and end apart: 2, of which 2 were waited for; matrix products, arithmetic and copies ran while one was open for 0% of the time, Pallas kernels for 2%

profile of v6, /device:TPU:1, one launch (start us, length us, event | category | flops | bytes accessed | tf_op | source)
XLA Modules:
  0.0 67.6 jit_solution(11135473303747302688)
XLA Ops:
  0.6 0.0 copy-start.5
  0.6 4.0 %shard_map.104 = bf16[448,128]{1,0:T(8,128)(2,1)} custom-call(bf16[128,2048]{1,0:T(8,128)(2,1)} %query_hbm.3, bf16[128,2048]{1,0:T(8,128)(2,1)} %key_hbm.3, bf16[128,2048]{1,0:T(8,128)(2,1)} %value_hbm.3, f32[3,3,2048]{2,1,0:T(4,128)} %filters.11, f32[16,2048]{1,0:T(8,128)} %decay.5), custom_call_target="tpu_custom_call" | custom-call | tf_op jit(solution)/shard_map/pallas_call | solution.py:549
  4.6 0.0 copy-start
  4.6 0.0 copy-start.3
  4.7 15.3 %all_to_all.44 = bf16[8,56,128]{2,1,0:T(8,128)(2,1)S(1)} all-to-all(bf16[8,56,128]{2,1,0:T(8,128)(2,1)} %bitcast.26), channel_id=1, replica_groups={{0,4,8,12,16,20,24,28},{32,36,40,44,48,52,56,60},{64,68,72,76,80,84,88,..., dimensions={0} | all-to-all | bytes 229376 | tf_op jit(solution)/shard_map/all_to_all | solution.py:578
  20.0 0.0 copy-done.5
  20.0 0.0 copy-done
  20.0 0.0 copy-done.3
  20.0 0.1 shard_map.105
  20.1 10.0 %all_to_all.45 = bf16[8,56,128]{2,1,0:T(8,128)(2,1)S(1)} all-to-all(bf16[8,56,128]{2,1,0:T(8,128)(2,1)S(1)} %bitcast.22), channel_id=1, replica_groups={{0,32,64,96,128,160,192,224},{4,36,68,100,132,164,196,228},{8,40,72,104..., dimensions={0} | all-to-all | bytes 229376 | tf_op jit(solution)/shard_map/all_to_all | solution.py:578
  30.1 0.1 shard_map.106
  30.3 0.0 copy-start.1
  30.3 7.2 %shard_map.107 = (f32[2048,128]{1,0:T(8,128)}, f32[2048,128]{1,0:T(8,128)}, f32[96,128]{1,0:T(8,128)S(1)}) custom-call(s32[1]{0:T(128)} %bitcast.place, bf16[128,2048]{1,0:T(8,128)(2,1)} %query_hbm.3, bf16[128,2048]{1,0:T(8,128)(2,1)} %key_hbm.3, bf16[128,2048]{1,0:T(8,128)(2,1)} %value_hbm.3, bf16[128,2048]{1,0:T(8,128)(2,1)} %residual_hbm.3, ...), custom_call_target="tpu_custom_call" | custom-call | tf_op jit(solution)/shard_map/pallas_call | solution.py:598
  37.5 4.7 %collective-permute-start = (bf16[56,128]{1,0:T(8,128)(2,1)S(1)}, bf16[56,128]{1,0:T(8,128)(2,1)S(1)}, u32[]{:S(2)}, u32[]{:S(2)}) collective-permute-start(bf16[56,128]{1,0:T(8,128)(2,1)S(1)} %shard_map.106), channel_id=1, source_target_pairs={{0,256},{4,260},{8,264},{12,268},{16,272},{20,276},{24,280},{28,28... | collective-permute-start | bytes 43016 | tf_op jit(solution)/shard_map/ppermute | solution.py:620
  42.2 0.8 %collective-permute-done.ahead = bf16[56,128]{1,0:T(8,128)(2,1)S(1)} collective-permute-done((bf16[56,128]{1,0:T(8,128)(2,1)S(1)}, bf16[56,128]{1,0:T(8,128)(2,1)S(1)}, u32[]{:S(2)}, u32[]{:S(2)}) %collective-permute-start) | collective-permute-done | bytes 14368 | tf_op jit(solution)/shard_map/ppermute | solution.py:620
  43.1 0.0 copy-done.1
  43.1 0.8 %shard_map.108 = bf16[384,128]{1,0:T(8,128)(2,1)} custom-call(s32[1]{0:T(128)} %bitcast.place, bf16[448,128]{1,0:T(8,128)(2,1)S(1)} %bitcast.14, bf16[448,128]{1,0:T(8,128)(2,1)S(1)} %bitcast.16, bf16[56,128]{1,0:T(8,128)(2,1)S(1)} %collective-permute-done.ahead, f32[256,128]{1,0:T(8,128)S(1)} %get-tuple-element.29.prefix, f32[3,3,2048]{2,1,0:T(4,128)S(1)} %copy-done.3, ...), custom_call_target="tpu_custom_call" | custom-call | tf_op jit(solution)/shard_map/pallas_call | solution.py:622
  43.9 6.3 %all-to-all-start.2 = ((bf16[8,48,128]{2,1,0:T(8,128)(2,1)}), bf16[8,48,128]{2,1,0:T(8,128)(2,1)S(1)}, u32[]{:S(2)}, u32[]{:S(2)}) async-start(bf16[8,48,128]{2,1,0:T(8,128)(2,1)} %bitcast.6), calls=%async_computation.2 | async-start | bytes 196608 | tf_op jit(solution)/shard_map/all_to_all | solution.py:578
  50.2 0.0 copy-start.2
  50.2 0.0 copy-start.4
  50.2 1.2 %shard_map.109 = (f32[2048,128]{1,0:T(8,128)}, f32[2048,128]{1,0:T(8,128)}, f32[96,128]{1,0:T(8,128)S(1)}) custom-call(s32[1]{0:T(128)} %bitcast.place, bf16[128,2048]{1,0:T(8,128)(2,1)} %query_hbm.3, bf16[128,2048]{1,0:T(8,128)(2,1)} %key_hbm.3, bf16[128,2048]{1,0:T(8,128)(2,1)} %value_hbm.3, bf16[128,2048]{1,0:T(8,128)(2,1)} %residual_hbm.3, ...), custom_call_target="tpu_custom_call" | custom-call | tf_op jit(solution)/shard_map/pallas_call | solution.py:598
  51.4 3.8 %all-to-all-done.2 = bf16[8,48,128]{2,1,0:T(8,128)(2,1)S(1)} async-done(((bf16[8,48,128]{2,1,0:T(8,128)(2,1)}), bf16[8,48,128]{2,1,0:T(8,128)(2,1)S(1)}, u32[]{:S(2)}, u32[]{:S(2)}) %all-to-all-start.2) | async-done | bytes 98336 | tf_op jit(solution)/shard_map/all_to_all | solution.py:578
  55.2 0.0 copy-done.2
  55.2 0.0 copy-done.4
  55.2 2.8 %shard_map.110 = (bf16[128,2048]{1,0:T(8,128)(2,1)S(1)}, f32[4,128]{1,0:T(4,128)S(1)}) custom-call(s32[1]{0:T(128)} %bitcast.place, bf16[384,128]{1,0:T(8,128)(2,1)S(1)} %bitcast.17, f32[3,3,2048]{2,1,0:T(4,128)S(1)} %copy-done.3, f32[16,2048]{1,0:T(8,128)S(1)} %copy-done.2, f32[16,2048]{1,0:T(8,128)S(1)} %copy-done.4, f32[16,128]{1,0:T(8,128)S(1)} %bitcast.21, ...), custom_call_target="tpu_custom_call" | custom-call | tf_op jit(solution)/shard_map/pallas_call | solution.py:629
  58.0 0.0 copy-start.6
  58.0 8.5 %all_to_all.46 = f32[4,1,128]{2,1,0:T(1,128)S(1)} all-to-all(f32[4,1,128]{2,1,0:T(1,128)S(1)} %bitcast.25), channel_id=1, replica_groups=mesh['seq'=128,'chan'=4] {'chan'}, dimensions={0} | all-to-all | bytes 4096 | tf_op jit(solution)/shard_map/all_to_all | solution.py:660
  66.5 0.0 copy-done.6
  66.5 1.0 %shard_map.111 = (bf16[128,2048]{1,0:T(8,128)(2,1)}, bf16[128,2048]{1,0:T(8,128)(2,1)}) custom-call(bf16[128,2048]{1,0:T(8,128)(2,1)S(1)} %get-tuple-element.36.summed, f32[4,128]{1,0:T(4,128)S(1)} %bitcast.24, f32[16,128]{1,0:T(8,128)S(1)} %bitcast.23), custom_call_target="tpu_custom_call" | custom-call | tf_op jit(solution)/shard_map/pallas_call | solution.py:662
Async XLA Ops:
  0.6 19.4 %copy-start.5 = (f32[2048]{0:T(1024)S(1)}, f32[2048]{0:T(1024)}, u32[]{:S(2)}) copy-start(f32[2048]{0:T(1024)} %param.16) | copy-start | bytes 24580
  4.6 15.4 %copy-start = (f32[16,2048]{1,0:T(8,128)S(1)}, f32[16,2048]{1,0:T(8,128)}, u32[]{:S(2)}) copy-start(f32[16,2048]{1,0:T(8,128)} %decay.5) | copy-start | bytes 393220
  4.6 15.4 %copy-start.3 = (f32[3,3,2048]{2,1,0:T(4,128)S(1)}, f32[3,3,2048]{2,1,0:T(4,128)}, u32[]{:S(2)}) copy-start(f32[3,3,2048]{2,1,0:T(4,128)} %filters.11) | copy-start | bytes 221188
  30.3 12.8 %copy-start.1 = (f32[16,2048]{1,0:T(8,128)S(1)}, f32[16,2048]{1,0:T(8,128)}, u32[]{:S(2)}) copy-start(f32[16,2048]{1,0:T(8,128)} %decay.5) | copy-start | bytes 393220
  37.5 5.6 %collective-permute-start = (bf16[56,128]{1,0:T(8,128)(2,1)S(1)}, bf16[56,128]{1,0:T(8,128)(2,1)S(1)}, u32[]{:S(2)}, u32[]{:S(2)}) collective-permute-start(bf16[56,128]{1,0:T(8,128)(2,1)S(1)} %shard_map.106), channel_id=1, source_target_pairs={{0,256},{4,260},{8,264},{12,268},{16,272},{20,276},{24,280},{28,28... | collective-permute-start | bytes 43016 | tf_op jit(solution)/shard_map/ppermute | solution.py:620
  43.9 11.3 %all-to-all-start.2 = ((bf16[8,48,128]{2,1,0:T(8,128)(2,1)}), bf16[8,48,128]{2,1,0:T(8,128)(2,1)S(1)}, u32[]{:S(2)}, u32[]{:S(2)}) async-start(bf16[8,48,128]{2,1,0:T(8,128)(2,1)} %bitcast.6), calls=%async_computation.2 | async-start | bytes 196608 | tf_op jit(solution)/shard_map/all_to_all | solution.py:578
  50.2 5.0 %copy-start.2 = (f32[16,2048]{1,0:T(8,128)S(1)}, f32[16,2048]{1,0:T(8,128)}, u32[]{:S(2)}) copy-start(f32[16,2048]{1,0:T(8,128)} %decay.5) | copy-start | bytes 393220
  50.2 5.0 %copy-start.4 = (f32[16,2048]{1,0:T(8,128)S(1)}, f32[16,2048]{1,0:T(8,128)}, u32[]{:S(2)}) copy-start(f32[16,2048]{1,0:T(8,128)} %residue.1) | copy-start | bytes 393220
  58.0 8.5 %copy-start.6 = (f32[2048]{0:T(1024)S(1)}, f32[2048]{0:T(1024)}, u32[]{:S(2)}) copy-start(f32[2048]{0:T(1024)} %param.17) | copy-start | bytes 24580

commit v7 on v6

--- a/solution.py
+++ b/solution.py
@@ -283,8 +283,8 @@
 
 
 def inner_kernel(
-    upper, place, query_hbm, key_hbm, value_hbm, residual_hbm, residue_hbm, skip_hbm, filters, decay,
-    base_hbm, feature_hbm, heads, skip, query_in, key_in, value_in, residual, residue, queries, keys, values, streams, feature,
+    upper, place, query_hbm, key_hbm, value_hbm, residual_hbm, residue_hbm, skip_hbm, filters_hbm,
+    decay_hbm, base_hbm, feature_hbm, heads, skip, filters, decay, query_in, key_in, value_in, residual, residue, queries, keys, values, streams, feature,
     weights, rates, taps, sem, out_sem,
 ):
     tokens, chans = query_in.shape
@@ -305,6 +305,8 @@
         small = [
             pltpu.make_async_copy(residue_hbm, residue, sem.at[0]),
             pltpu.make_async_copy(skip_hbm, skip, sem.at[1]),
+            pltpu.make_async_copy(filters_hbm, filters, sem.at[2]),
+            pltpu.make_async_copy(decay_hbm, decay, sem.at[3]),
         ]
         for copy in small:
             copy.start()
@@ -314,13 +316,13 @@
             for i, (source, target, _) in enumerate(lanes):
                 copies.append(
                     pltpu.make_async_copy(
-                        source.at[:, columns], target.at[:, columns], sem.at[2 + 4 * half + i]
+                        source.at[:, columns], target.at[:, columns], sem.at[4 + 4 * half + i]
                     )
                 )
                 copies[-1].start()
-        fill_tables(filters, decay, rates, taps)
         for copy in small:
             copy.wait()
+        fill_tables(filters, decay, rates, taps)
         for g in range(groups):
             weights[g * POLES : (g + 1) * POLES, :] = residue[:, g * LANES : (g + 1) * LANES]
         outward = []
@@ -603,14 +605,15 @@
                 shape(3 * HALO * groups),
             ),
             room=10.25,
-            in_specs=[smem] + [hbm] * 6 + [vmem] * 2,
+            in_specs=[smem] + [hbm] * 8,
             out_specs=(hbm, hbm, vmem),
             scratch=[hold(groups)]
+            + [pltpu.VMEM(short_filter.shape, f32), pltpu.VMEM(decay_rate.shape, f32)]
             + [wide] * 4
             + [pltpu.VMEM(residue.shape, f32)]
             + [hold(tokens * groups)] * 5
             + [hold(poled_rows)] * 3
-            + [pltpu.SemaphoreType.DMA((2 + 4 * (groups // SUBLANES),))]
+            + [pltpu.SemaphoreType.DMA((4 + 4 * (groups // SUBLANES),))]
             + [pltpu.SemaphoreType.DMA((16,))],
         )(place, query_in, key_in, value_in, residual, residue, skip, *tables_in)
 

time: 68.1 us -> 67.1 us (0.985)
  Pallas kernels: 17.3 us -> 15.5 us
  waiting for transfers between devices: 4.62 us -> 5.57 us
    pallas_call x2, Pallas kernels: 8.43 us -> 6.68 us  [inner(): call(functools.partial(inner_kernel, upper), (shape(tokens * groups), sha...]
    all_to_all x1, waiting for transfers between devices: 3.78 us -> 4.74 us  [exchange(): return lax.all_to_all(x, 'seq', 0, 0, axis_index_groups=members, tiled=True)]
  transfers between devices with their start and end apart: 2 -> 2, of which waited for: 2 -> 2; matrix products, arithmetic and copies ran while one was open for 0% -> 0% of each run, Pallas kernels for 2% -> 0%
where the time goes in v7:
time: 67.1 us; the launch traced here: 66.6 us
  blocking collectives  33.8 us (50%)
  Pallas kernels  15.5 us (23%)
  starting transfers between devices  10.9 us (16%)
  waiting for transfers between devices  5.57 us (8%)
  between operations  0.73 us (1%)
    all_to_all x2, blocking collectives, exchange(): return lax.all_to_all(x, 'seq', 0, 0, axis_index_groups=members, tiled=True)  25.3 us
    all_to_all x1, blocking collectives, layer(): squares = lax.all_to_all(squares, 'chan', 0, 0, tiled=True)  8.51 us
    pallas_call x2, Pallas kernels, inner(): call(functools.partial(inner_kernel, upper), (shape(tokens * groups), sha...  6.68 us
    all_to_all x1, starting transfers between devices, exchange(): return lax.all_to_all(x, 'seq', 0, 0, axis_index_groups=members, tiled=True)  6.34 us
    all_to_all x1, waiting for transfers between devices, exchange(): return lax.all_to_all(x, 'seq', 0, 0, axis_index_groups=members, tiled=True)  4.74 us
    ppermute x1, starting transfers between devices, layer(): lax.ppermute(ahead, 'seq', [(i, i + count // 2) for i in range(count // 2)])  4.57 us
    pallas_call x1, Pallas kernels, layer(): call(first_kernel, shape(parcel_rows, bf16), room=10.1, in_specs=[hbm] *...  3.98 us
    pallas_call x1, Pallas kernels, layer(): call(outer_kernel, (jax.ShapeDtypeStruct((tokens, chans), bf16), jax.Shap...  2.78 us
  transfers between devices with their start and end apart: 2, of which 2 were waited for; matrix products, arithmetic and copies ran while one was open for 0% of the time, Pallas kernels for 0%

profile of v7, /device:TPU:1, one launch (start us, length us, event | category | flops | bytes accessed | tf_op | source)
XLA Modules:
  0.0 66.6 jit_solution(2905450387230431973)
XLA Ops:
  0.6 0.0 copy-start.5
  0.6 4.0 %shard_map.104 = bf16[448,128]{1,0:T(8,128)(2,1)} custom-call(bf16[128,2048]{1,0:T(8,128)(2,1)} %query_hbm.3, bf16[128,2048]{1,0:T(8,128)(2,1)} %key_hbm.3, bf16[128,2048]{1,0:T(8,128)(2,1)} %value_hbm.3, f32[3,3,2048]{2,1,0:T(4,128)} %filters.7, f32[16,2048]{1,0:T(8,128)} %decay.1), custom_call_target="tpu_custom_call" | custom-call | tf_op jit(solution)/shard_map/pallas_call | solution.py:551
  4.6 0.0 copy-start
  4.6 0.0 copy-start.3
  4.7 15.3 %all_to_all.44 = bf16[8,56,128]{2,1,0:T(8,128)(2,1)S(1)} all-to-all(bf16[8,56,128]{2,1,0:T(8,128)(2,1)} %bitcast.26), channel_id=1, replica_groups={{0,4,8,12,16,20,24,28},{32,36,40,44,48,52,56,60},{64,68,72,76,80,84,88,..., dimensions={0} | all-to-all | bytes 229376 | tf_op jit(solution)/shard_map/all_to_all | solution.py:580
  20.0 0.0 copy-done.5
  20.0 0.0 copy-done
  20.0 0.0 copy-done.3
  20.0 0.1 shard_map.105
  20.1 10.0 %all_to_all.45 = bf16[8,56,128]{2,1,0:T(8,128)(2,1)S(1)} all-to-all(bf16[8,56,128]{2,1,0:T(8,128)(2,1)S(1)} %bitcast.22), channel_id=1, replica_groups={{0,32,64,96,128,160,192,224},{4,36,68,100,132,164,196,228},{8,40,72,104..., dimensions={0} | all-to-all | bytes 229376 | tf_op jit(solution)/shard_map/all_to_all | solution.py:580
  30.1 0.1 shard_map.106
  30.3 0.0 copy-start.1
  30.3 6.4 %shard_map.107 = (f32[2048,128]{1,0:T(8,128)}, f32[2048,128]{1,0:T(8,128)}, f32[96,128]{1,0:T(8,128)S(1)}) custom-call(s32[1]{0:T(128)} %bitcast.place, bf16[128,2048]{1,0:T(8,128)(2,1)} %query_hbm.3, bf16[128,2048]{1,0:T(8,128)(2,1)} %key_hbm.3, bf16[128,2048]{1,0:T(8,128)(2,1)} %value_hbm.3, bf16[128,2048]{1,0:T(8,128)(2,1)} %residual_hbm.3, ...), custom_call_target="tpu_custom_call" | custom-call | tf_op jit(solution)/shard_map/pallas_call | solution.py:600
  36.7 4.6 %collective-permute-start = (bf16[56,128]{1,0:T(8,128)(2,1)S(1)}, bf16[56,128]{1,0:T(8,128)(2,1)S(1)}, u32[]{:S(2)}, u32[]{:S(2)}) collective-permute-start(bf16[56,128]{1,0:T(8,128)(2,1)S(1)} %shard_map.106), channel_id=1, source_target_pairs={{0,256},{4,260},{8,264},{12,268},{16,272},{20,276},{24,280},{28,28... | collective-permute-start | bytes 43016 | tf_op jit(solution)/shard_map/ppermute | solution.py:623
  41.3 0.8 %collective-permute-done.ahead = bf16[56,128]{1,0:T(8,128)(2,1)S(1)} collective-permute-done((bf16[56,128]{1,0:T(8,128)(2,1)S(1)}, bf16[56,128]{1,0:T(8,128)(2,1)S(1)}, u32[]{:S(2)}, u32[]{:S(2)}) %collective-permute-start) | collective-permute-done | bytes 14368 | tf_op jit(solution)/shard_map/ppermute | solution.py:623
  42.1 0.0 copy-done.1
  42.1 0.8 %shard_map.108 = bf16[384,128]{1,0:T(8,128)(2,1)} custom-call(s32[1]{0:T(128)} %bitcast.place, bf16[448,128]{1,0:T(8,128)(2,1)S(1)} %bitcast.14, bf16[448,128]{1,0:T(8,128)(2,1)S(1)} %bitcast.16, bf16[56,128]{1,0:T(8,128)(2,1)S(1)} %collective-permute-done.ahead, f32[256,128]{1,0:T(8,128)S(1)} %get-tuple-element.29.prefix, f32[3,3,2048]{2,1,0:T(4,128)S(1)} %copy-done.3, ...), custom_call_target="tpu_custom_call" | custom-call | tf_op jit(solution)/shard_map/pallas_call | solution.py:625
  42.9 6.3 %all-to-all-start.2 = ((bf16[8,48,128]{2,1,0:T(8,128)(2,1)}), bf16[8,48,128]{2,1,0:T(8,128)(2,1)S(1)}, u32[]{:S(2)}, u32[]{:S(2)}) async-start(bf16[8,48,128]{2,1,0:T(8,128)(2,1)} %bitcast.6), calls=%async_computation.2 | async-start | bytes 196608 | tf_op jit(solution)/shard_map/all_to_all | solution.py:580
  49.3 0.0 copy-start.2
  49.3 0.0 copy-start.4
  49.3 0.3 shard_map.109
  49.5 4.7 %all-to-all-done.2 = bf16[8,48,128]{2,1,0:T(8,128)(2,1)S(1)} async-done(((bf16[8,48,128]{2,1,0:T(8,128)(2,1)}), bf16[8,48,128]{2,1,0:T(8,128)(2,1)S(1)}, u32[]{:S(2)}, u32[]{:S(2)}) %all-to-all-start.2) | async-done | bytes 98336 | tf_op jit(solution)/shard_map/all_to_all | solution.py:580
  54.3 0.0 copy-done.2
  54.3 0.0 copy-done.4
  54.3 2.8 %shard_map.110 = (bf16[128,2048]{1,0:T(8,128)(2,1)S(1)}, f32[4,128]{1,0:T(4,128)S(1)}) custom-call(s32[1]{0:T(128)} %bitcast.place, bf16[384,128]{1,0:T(8,128)(2,1)S(1)} %bitcast.17, f32[3,3,2048]{2,1,0:T(4,128)S(1)} %copy-done.3, f32[16,2048]{1,0:T(8,128)S(1)} %copy-done.2, f32[16,2048]{1,0:T(8,128)S(1)} %copy-done.4, f32[16,128]{1,0:T(8,128)S(1)} %bitcast.21, ...), custom_call_target="tpu_custom_call" | custom-call | tf_op jit(solution)/shard_map/pallas_call | solution.py:632
  57.1 0.0 copy-start.6
  57.1 8.5 %all_to_all.46 = f32[4,1,128]{2,1,0:T(1,128)S(1)} all-to-all(f32[4,1,128]{2,1,0:T(1,128)S(1)} %bitcast.25), channel_id=1, replica_groups=mesh['seq'=128,'chan'=4] {'chan'}, dimensions={0} | all-to-all | bytes 4096 | tf_op jit(solution)/shard_map/all_to_all | solution.py:663
  65.6 0.0 copy-done.6
  65.6 1.0 %shard_map.111 = (bf16[128,2048]{1,0:T(8,128)(2,1)}, bf16[128,2048]{1,0:T(8,128)(2,1)}) custom-call(bf16[128,2048]{1,0:T(8,128)(2,1)S(1)} %get-tuple-element.36.summed, f32[4,128]{1,0:T(4,128)S(1)} %bitcast.24, f32[16,128]{1,0:T(8,128)S(1)} %bitcast.23), custom_call_target="tpu_custom_call" | custom-call | tf_op jit(solution)/shard_map/pallas_call | solution.py:665
Async XLA Ops:
  0.6 19.4 %copy-start.5 = (f32[2048]{0:T(1024)S(1)}, f32[2048]{0:T(1024)}, u32[]{:S(2)}) copy-start(f32[2048]{0:T(1024)} %param.16) | copy-start | bytes 24580
  4.6 15.4 %copy-start = (f32[16,2048]{1,0:T(8,128)S(1)}, f32[16,2048]{1,0:T(8,128)}, u32[]{:S(2)}) copy-start(f32[16,2048]{1,0:T(8,128)} %decay.1) | copy-start | bytes 393220
  4.6 15.4 %copy-start.3 = (f32[3,3,2048]{2,1,0:T(4,128)S(1)}, f32[3,3,2048]{2,1,0:T(4,128)}, u32[]{:S(2)}) copy-start(f32[3,3,2048]{2,1,0:T(4,128)} %filters.7) | copy-start | bytes 221188
  30.3 11.9 %copy-start.1 = (f32[16,2048]{1,0:T(8,128)S(1)}, f32[16,2048]{1,0:T(8,128)}, u32[]{:S(2)}) copy-start(f32[16,2048]{1,0:T(8,128)} %decay.1) | copy-start | bytes 393220
  36.7 5.4 %collective-permute-start = (bf16[56,128]{1,0:T(8,128)(2,1)S(1)}, bf16[56,128]{1,0:T(8,128)(2,1)S(1)}, u32[]{:S(2)}, u32[]{:S(2)}) collective-permute-start(bf16[56,128]{1,0:T(8,128)(2,1)S(1)} %shard_map.106), channel_id=1, source_target_pairs={{0,256},{4,260},{8,264},{12,268},{16,272},{20,276},{24,280},{28,28... | collective-permute-start | bytes 43016 | tf_op jit(solution)/shard_map/ppermute | solution.py:623
  42.9 11.3 %all-to-all-start.2 = ((bf16[8,48,128]{2,1,0:T(8,128)(2,1)}), bf16[8,48,128]{2,1,0:T(8,128)(2,1)S(1)}, u32[]{:S(2)}, u32[]{:S(2)}) async-start(bf16[8,48,128]{2,1,0:T(8,128)(2,1)} %bitcast.6), calls=%async_computation.2 | async-start | bytes 196608 | tf_op jit(solution)/shard_map/all_to_all | solution.py:580
  49.3 5.0 %copy-start.2 = (f32[16,2048]{1,0:T(8,128)S(1)}, f32[16,2048]{1,0:T(8,128)}, u32[]{:S(2)}) copy-start(f32[16,2048]{1,0:T(8,128)} %decay.1) | copy-start | bytes 393220
  49.3 5.0 %copy-start.4 = (f32[16,2048]{1,0:T(8,128)S(1)}, f32[16,2048]{1,0:T(8,128)}, u32[]{:S(2)}) copy-start(f32[16,2048]{1,0:T(8,128)} %residue.1) | copy-start | bytes 393220
  57.1 8.5 %copy-start.6 = (f32[2048]{0:T(1024)S(1)}, f32[2048]{0:T(1024)}, u32[]{:S(2)}) copy-start(f32[2048]{0:T(1024)} %param.17) | copy-start | bytes 24580

commit v8 on v7

--- a/solution.py
+++ b/solution.py
@@ -108,10 +108,8 @@
     ]
     small[0].start()
     small[1].start()
-    for pair in large:
-        pair[0].start()
-        pair[1].start()
-    small[2].start()
+    for copy in large[0]:
+        copy.start()
     small[0].wait()
     small[1].wait()
     fill_tables(filters, decay, rates, taps)
@@ -121,6 +119,8 @@
         value_taps = taps_of(taps, 2, half)
         for copy in large[half]:
             copy.wait()
+        for copy in large[half + 1] if half + 1 < halves else small[2:]:
+            copy.start()
         columns = range(half * SUBLANES, (half + 1) * SUBLANES)
         spread(key, keys, 0, columns, groups)
         spread(value, values, 0, columns, groups)
@@ -420,17 +420,21 @@
         return copies
 
     copies = copies_from(feature_low, base_low)
-
-    @pl.when(lower)
-    def _():
-        for copy in copies:
-            copy.start()
-
-    @pl.when(jnp.logical_not(lower))
-    def _():
-        for copy in copies_from(feature_high, base_high):
-            copy.start()
-
+    others = copies_from(feature_high, base_high)
+
+    def begin(parts):
+        @pl.when(lower)
+        def _():
+            for copy in copies[parts]:
+                copy.start()
+
+        @pl.when(jnp.logical_not(lower))
+        def _():
+            for copy in others[parts]:
+                copy.start()
+
+    ahead = 4
+    begin(slice(0, ahead))
     fill_tables(filters, decay, rates, taps)
     for g in range(groups):
         weights[g * POLES : (g + 1) * POLES, :] = residue[:, g * LANES : (g + 1) * LANES]
@@ -484,8 +488,11 @@
         turns = (tokens - HALO) // STEP
         done = 0
         for p in range(parts):
-            for copy in copies[2 * (parts * half + p) : 2 * (parts * half + p + 1)]:
+            now = 2 * (parts * half + p)
+            for copy in copies[now : now + 2]:
                 copy.wait()
+            if now + ahead < len(copies):
+                begin(slice(now + ahead, now + ahead + 2))
             if p == 0:
                 for t in range(HALO):
                     put(gated, t, half, groups, tile(gated, t, half, groups) + start[t])

time: 67.1 us -> 69.1 us (1.030)
  Pallas kernels: 15.5 us -> 17.5 us
    pallas_call x1, Pallas kernels: 2.78 us -> 4.75 us  [layer(): call(outer_kernel, (jax.ShapeDtypeStruct((tokens, chans), bf16), jax.Shap...]
where the time goes in v8:
time: 69.1 us; the launch traced here: 68.6 us
  blocking collectives  33.8 us (49%)
  Pallas kernels  17.5 us (25%)
  starting transfers between devices  10.9 us (16%)
  waiting for transfers between devices  5.57 us (8%)
  between operations  0.73 us (1%)
    all_to_all x2, blocking collectives, exchange(): return lax.all_to_all(x, 'seq', 0, 0, axis_index_groups=members, tiled=True)  25.3 us
    all_to_all x1, blocking collectives, layer(): squares = lax.all_to_all(squares, 'chan', 0, 0, tiled=True)  8.51 us
    pallas_call x2, Pallas kernels, inner(): call(functools.partial(inner_kernel, upper), (shape(tokens * groups), sha...  6.68 us
    all_to_all x1, starting transfers between devices, exchange(): return lax.all_to_all(x, 'seq', 0, 0, axis_index_groups=members, tiled=True)  6.34 us
    pallas_call x1, Pallas kernels, layer(): call(outer_kernel, (jax.ShapeDtypeStruct((tokens, chans), bf16), jax.Shap...  4.75 us
    all_to_all x1, waiting for transfers between devices, exchange(): return lax.all_to_all(x, 'seq', 0, 0, axis_index_groups=members, tiled=True)  4.74 us
    ppermute x1, starting transfers between devices, layer(): lax.ppermute(ahead, 'seq', [(i, i + count // 2) for i in range(count // 2)])  4.57 us
    pallas_call x1, Pallas kernels, layer(): call(first_kernel, shape(parcel_rows, bf16), room=10.1, in_specs=[hbm] *...  3.98 us
  transfers between devices with their start and end apart: 2, of which 2 were waited for; matrix products, arithmetic and copies ran while one was open for 0% of the time, Pallas kernels for 0%

profile of v8, /device:TPU:1, one launch (start us, length us, event | category | flops | bytes accessed | tf_op | source)
XLA Modules:
  0.0 68.6 jit_solution(753926166664586483)
XLA Ops:
  0.6 0.0 copy-start.5
  0.6 4.0 %shard_map.104 = bf16[448,128]{1,0:T(8,128)(2,1)} custom-call(bf16[128,2048]{1,0:T(8,128)(2,1)} %query_hbm.3, bf16[128,2048]{1,0:T(8,128)(2,1)} %key_hbm.3, bf16[128,2048]{1,0:T(8,128)(2,1)} %value_hbm.3, f32[3,3,2048]{2,1,0:T(4,128)} %filters.7, f32[16,2048]{1,0:T(8,128)} %decay.1), custom_call_target="tpu_custom_call" | custom-call | tf_op jit(solution)/shard_map/pallas_call | solution.py:558
  4.6 0.0 copy-start
  4.6 0.0 copy-start.3
  4.7 15.3 %all_to_all.44 = bf16[8,56,128]{2,1,0:T(8,128)(2,1)S(1)} all-to-all(bf16[8,56,128]{2,1,0:T(8,128)(2,1)} %bitcast.26), channel_id=1, replica_groups={{0,4,8,12,16,20,24,28},{32,36,40,44,48,52,56,60},{64,68,72,76,80,84,88,..., dimensions={0} | all-to-all | bytes 229376 | tf_op jit(solution)/shard_map/all_to_all | solution.py:587
  20.0 0.0 copy-done.5
  20.0 0.0 copy-done
  20.0 0.0 copy-done.3
  20.0 0.1 shard_map.105
  20.1 10.0 %all_to_all.45 = bf16[8,56,128]{2,1,0:T(8,128)(2,1)S(1)} all-to-all(bf16[8,56,128]{2,1,0:T(8,128)(2,1)S(1)} %bitcast.22), channel_id=1, replica_groups={{0,32,64,96,128,160,192,224},{4,36,68,100,132,164,196,228},{8,40,72,104..., dimensions={0} | all-to-all | bytes 229376 | tf_op jit(solution)/shard_map/all_to_all | solution.py:587
  30.1 0.1 shard_map.106
  30.3 0.0 copy-start.1
  30.3 6.4 %shard_map.107 = (f32[2048,128]{1,0:T(8,128)}, f32[2048,128]{1,0:T(8,128)}, f32[96,128]{1,0:T(8,128)S(1)}) custom-call(s32[1]{0:T(128)} %bitcast.place, bf16[128,2048]{1,0:T(8,128)(2,1)} %query_hbm.3, bf16[128,2048]{1,0:T(8,128)(2,1)} %key_hbm.3, bf16[128,2048]{1,0:T(8,128)(2,1)} %value_hbm.3, bf16[128,2048]{1,0:T(8,128)(2,1)} %residual_hbm.3, ...), custom_call_target="tpu_custom_call" | custom-call | tf_op jit(solution)/shard_map/pallas_call | solution.py:607
  36.7 4.6 %collective-permute-start = (bf16[56,128]{1,0:T(8,128)(2,1)S(1)}, bf16[56,128]{1,0:T(8,128)(2,1)S(1)}, u32[]{:S(2)}, u32[]{:S(2)}) collective-permute-start(bf16[56,128]{1,0:T(8,128)(2,1)S(1)} %shard_map.106), channel_id=1, source_target_pairs={{0,256},{4,260},{8,264},{12,268},{16,272},{20,276},{24,280},{28,28... | collective-permute-start | bytes 43016 | tf_op jit(solution)/shard_map/ppermute | solution.py:630
  41.3 0.8 %collective-permute-done.ahead = bf16[56,128]{1,0:T(8,128)(2,1)S(1)} collective-permute-done((bf16[56,128]{1,0:T(8,128)(2,1)S(1)}, bf16[56,128]{1,0:T(8,128)(2,1)S(1)}, u32[]{:S(2)}, u32[]{:S(2)}) %collective-permute-start) | collective-permute-done | bytes 14368 | tf_op jit(solution)/shard_map/ppermute | solution.py:630
  42.1 0.0 copy-done.1
  42.1 0.8 %shard_map.108 = bf16[384,128]{1,0:T(8,128)(2,1)} custom-call(s32[1]{0:T(128)} %bitcast.place, bf16[448,128]{1,0:T(8,128)(2,1)S(1)} %bitcast.14, bf16[448,128]{1,0:T(8,128)(2,1)S(1)} %bitcast.16, bf16[56,128]{1,0:T(8,128)(2,1)S(1)} %collective-permute-done.ahead, f32[256,128]{1,0:T(8,128)S(1)} %get-tuple-element.29.prefix, f32[3,3,2048]{2,1,0:T(4,128)S(1)} %copy-done.3, ...), custom_call_target="tpu_custom_call" | custom-call | tf_op jit(solution)/shard_map/pallas_call | solution.py:632
  42.9 6.3 %all-to-all-start.2 = ((bf16[8,48,128]{2,1,0:T(8,128)(2,1)}), bf16[8,48,128]{2,1,0:T(8,128)(2,1)S(1)}, u32[]{:S(2)}, u32[]{:S(2)}) async-start(bf16[8,48,128]{2,1,0:T(8,128)(2,1)} %bitcast.6), calls=%async_computation.2 | async-start | bytes 196608 | tf_op jit(solution)/shard_map/all_to_all | solution.py:587
  49.3 0.0 copy-start.2
  49.3 0.0 copy-start.4
  49.3 0.3 shard_map.109
  49.5 4.7 %all-to-all-done.2 = bf16[8,48,128]{2,1,0:T(8,128)(2,1)S(1)} async-done(((bf16[8,48,128]{2,1,0:T(8,128)(2,1)}), bf16[8,48,128]{2,1,0:T(8,128)(2,1)S(1)}, u32[]{:S(2)}, u32[]{:S(2)}) %all-to-all-start.2) | async-done | bytes 98336 | tf_op jit(solution)/shard_map/all_to_all | solution.py:587
  54.3 0.0 copy-done.2
  54.3 0.0 copy-done.4
  54.3 4.8 %shard_map.110 = (bf16[128,2048]{1,0:T(8,128)(2,1)S(1)}, f32[4,128]{1,0:T(4,128)S(1)}) custom-call(s32[1]{0:T(128)} %bitcast.place, bf16[384,128]{1,0:T(8,128)(2,1)S(1)} %bitcast.17, f32[3,3,2048]{2,1,0:T(4,128)S(1)} %copy-done.3, f32[16,2048]{1,0:T(8,128)S(1)} %copy-done.2, f32[16,2048]{1,0:T(8,128)S(1)} %copy-done.4, f32[16,128]{1,0:T(8,128)S(1)} %bitcast.21, ...), custom_call_target="tpu_custom_call" | custom-call | tf_op jit(solution)/shard_map/pallas_call | solution.py:639
  59.0 0.0 copy-start.6
  59.1 8.5 %all_to_all.46 = f32[4,1,128]{2,1,0:T(1,128)S(1)} all-to-all(f32[4,1,128]{2,1,0:T(1,128)S(1)} %bitcast.25), channel_id=1, replica_groups=mesh['seq'=128,'chan'=4] {'chan'}, dimensions={0} | all-to-all | bytes 4096 | tf_op jit(solution)/shard_map/all_to_all | solution.py:670
  67.6 0.0 copy-done.6
  67.6 1.0 %shard_map.111 = (bf16[128,2048]{1,0:T(8,128)(2,1)}, bf16[128,2048]{1,0:T(8,128)(2,1)}) custom-call(bf16[128,2048]{1,0:T(8,128)(2,1)S(1)} %get-tuple-element.36.summed, f32[4,128]{1,0:T(4,128)S(1)} %bitcast.24, f32[16,128]{1,0:T(8,128)S(1)} %bitcast.23), custom_call_target="tpu_custom_call" | custom-call | tf_op jit(solution)/shard_map/pallas_call | solution.py:672
Async XLA Ops:
  0.6 19.4 %copy-start.5 = (f32[2048]{0:T(1024)S(1)}, f32[2048]{0:T(1024)}, u32[]{:S(2)}) copy-start(f32[2048]{0:T(1024)} %param.16) | copy-start | bytes 24580
  4.6 15.4 %copy-start = (f32[16,2048]{1,0:T(8,128)S(1)}, f32[16,2048]{1,0:T(8,128)}, u32[]{:S(2)}) copy-start(f32[16,2048]{1,0:T(8,128)} %decay.1) | copy-start | bytes 393220
  4.6 15.4 %copy-start.3 = (f32[3,3,2048]{2,1,0:T(4,128)S(1)}, f32[3,3,2048]{2,1,0:T(4,128)}, u32[]{:S(2)}) copy-start(f32[3,3,2048]{2,1,0:T(4,128)} %filters.7) | copy-start | bytes 221188
  30.3 11.9 %copy-start.1 = (f32[16,2048]{1,0:T(8,128)S(1)}, f32[16,2048]{1,0:T(8,128)}, u32[]{:S(2)}) copy-start(f32[16,2048]{1,0:T(8,128)} %decay.1) | copy-start | bytes 393220
  36.7 5.4 %collective-permute-start = (bf16[56,128]{1,0:T(8,128)(2,1)S(1)}, bf16[56,128]{1,0:T(8,128)(2,1)S(1)}, u32[]{:S(2)}, u32[]{:S(2)}) collective-permute-start(bf16[56,128]{1,0:T(8,128)(2,1)S(1)} %shard_map.106), channel_id=1, source_target_pairs={{0,256},{4,260},{8,264},{12,268},{16,272},{20,276},{24,280},{28,28... | collective-permute-start | bytes 43016 | tf_op jit(solution)/shard_map/ppermute | solution.py:630
  42.9 11.3 %all-to-all-start.2 = ((bf16[8,48,128]{2,1,0:T(8,128)(2,1)}), bf16[8,48,128]{2,1,0:T(8,128)(2,1)S(1)}, u32[]{:S(2)}, u32[]{:S(2)}) async-start(bf16[8,48,128]{2,1,0:T(8,128)(2,1)} %bitcast.6), calls=%async_computation.2 | async-start | bytes 196608 | tf_op jit(solution)/shard_map/all_to_all | solution.py:587
  49.3 5.0 %copy-start.2 = (f32[16,2048]{1,0:T(8,128)S(1)}, f32[16,2048]{1,0:T(8,128)}, u32[]{:S(2)}) copy-start(f32[16,2048]{1,0:T(8,128)} %decay.1) | copy-start | bytes 393220
  49.3 5.0 %copy-start.4 = (f32[16,2048]{1,0:T(8,128)S(1)}, f32[16,2048]{1,0:T(8,128)}, u32[]{:S(2)}) copy-start(f32[16,2048]{1,0:T(8,128)} %residue.1) | copy-start | bytes 393220
  59.0 8.5 %copy-start.6 = (f32[2048]{0:T(1024)S(1)}, f32[2048]{0:T(1024)}, u32[]{:S(2)}) copy-start(f32[2048]{0:T(1024)} %param.17) | copy-start | bytes 24580

commit v9 on v7

--- a/solution.py
+++ b/solution.py
@@ -93,9 +93,19 @@
     halves = groups // SUBLANES
     width = SUBLANES * LANES
 
+    pieces = 4
+    span = tokens // pieces
+
     def part(source, target, half, slot):
         columns = slice(half * width, (half + 1) * width)
-        return pltpu.make_async_copy(source.at[:, columns], target.at[:, columns], sem.at[slot])
+        return [
+            pltpu.make_async_copy(
+                source.at[p * span : (p + 1) * span, columns],
+                target.at[p * span : (p + 1) * span, columns],
+                sem.at[3 + slot * pieces + p],
+            )
+            for p in range(pieces)
+        ]
 
     small = [
         pltpu.make_async_copy(decay_in, decay, sem.at[0]),
@@ -103,14 +113,13 @@
         pltpu.make_async_copy(query_in.at[tokens - 8 : tokens, :], query, sem.at[2]),
     ]
     large = [
-        (part(key_in, key, h, 3 + 2 * h), part(value_in, value, h, 4 + 2 * h))
-        for h in range(halves)
+        part(key_in, key, h, 2 * h) + part(value_in, value, h, 2 * h + 1) for h in range(halves)
     ]
     small[0].start()
     small[1].start()
-    for pair in large:
-        pair[0].start()
-        pair[1].start()
+    for group in large:
+        for copy in group:
+            copy.start()
     small[2].start()
     small[0].wait()
     small[1].wait()
@@ -404,13 +413,16 @@
     tokens, chans = summed.shape
     groups = chans // LANES
     lower = place[0] < MINOR * MIDDLE
-    parts = sem.shape[0] // (2 * (groups // SUBLANES))
+    parts = 4
+    pieces = 4
+    every = 2 * pieces
     span = tokens // parts
 
     def copies_from(feature, base):
         copies = []
+        piece = span // pieces
         for p in range(sem.shape[0] // 2):
-            part = slice(p * span * SUBLANES, (p + 1) * span * SUBLANES)
+            part = slice(p * piece * SUBLANES, (p + 1) * piece * SUBLANES)
             for i, (source, target) in enumerate(((feature, query), (base, gated))):
                 copies.append(
                     pltpu.make_async_copy(
@@ -484,7 +496,7 @@
         turns = (tokens - HALO) // STEP
         done = 0
         for p in range(parts):
-            for copy in copies[2 * (parts * half + p) : 2 * (parts * half + p + 1)]:
+            for copy in copies[every * (parts * half + p) : every * (parts * half + p + 1)]:
                 copy.wait()
             if p == 0:
                 for t in range(HALO):
@@ -564,7 +576,7 @@
             hold(poled_rows),
             hold(poled_rows),
             hold(poled_rows),
-            pltpu.SemaphoreType.DMA((3 + 2 * (groups // SUBLANES),)),
+            pltpu.SemaphoreType.DMA((3 + 8 * (groups // SUBLANES),)),
         ],
     )(query_in, key_in, value_in, short_filter, decay_rate)
 
@@ -645,7 +657,7 @@
             hold(poled_rows),
             hold(tokens * groups),
             hold(tokens * groups),
-            pltpu.SemaphoreType.DMA((16,)),
+            pltpu.SemaphoreType.DMA((64,)),
         ],
     )(
         place,

time: 67.1 us -> 67.7 us (level)
  no operation moved by 1% of the time
where the time goes in v9:
time: 67.7 us; the launch traced here: 67.1 us
  blocking collectives  33.8 us (50%)
  Pallas kernels  16 us (24%)
  starting transfers between devices  10.9 us (16%)
  waiting for transfers between devices  5.57 us (8%)
  between operations  0.73 us (1%)
    all_to_all x2, blocking collectives, exchange(): return lax.all_to_all(x, 'seq', 0, 0, axis_index_groups=members, tiled=True)  25.3 us
    all_to_all x1, blocking collectives, layer(): squares = lax.all_to_all(squares, 'chan', 0, 0, tiled=True)  8.51 us
    pallas_call x2, Pallas kernels, inner(): call(functools.partial(inner_kernel, upper), (shape(tokens * groups), sha...  6.68 us
    all_to_all x1, starting transfers between devices, exchange(): return lax.all_to_all(x, 'seq', 0, 0, axis_index_groups=members, tiled=True)  6.34 us
    all_to_all x1, waiting for transfers between devices, exchange(): return lax.all_to_all(x, 'seq', 0, 0, axis_index_groups=members, tiled=True)  4.74 us
    ppermute x1, starting transfers between devices, layer(): lax.ppermute(ahead, 'seq', [(i, i + count // 2) for i in range(count // 2)])  4.57 us
    pallas_call x1, Pallas kernels, layer(): call(first_kernel, shape(parcel_rows, bf16), room=10.1, in_specs=[hbm] *...  4.1 us
    pallas_call x1, Pallas kernels, layer(): call(outer_kernel, (jax.ShapeDtypeStruct((tokens, chans), bf16), jax.Shap...  3.17 us
  transfers between devices with their start and end apart: 2, of which 2 were waited for; matrix products, arithmetic and copies ran while one was open for 0% of the time, Pallas kernels for 0%

profile of v9, /device:TPU:1, one launch (start us, length us, event | category | flops | bytes accessed | tf_op | source)
XLA Modules:
  0.0 67.1 jit_solution(1995602098221757981)
XLA Ops:
  0.6 0.0 copy-start.5
  0.6 4.1 %shard_map.104 = bf16[448,128]{1,0:T(8,128)(2,1)} custom-call(bf16[128,2048]{1,0:T(8,128)(2,1)} %query_hbm.3, bf16[128,2048]{1,0:T(8,128)(2,1)} %key_hbm.3, bf16[128,2048]{1,0:T(8,128)(2,1)} %value_hbm.3, f32[3,3,2048]{2,1,0:T(4,128)} %filters.7, f32[16,2048]{1,0:T(8,128)} %decay.1), custom_call_target="tpu_custom_call" | custom-call | tf_op jit(solution)/shard_map/pallas_call | solution.py:563
  4.7 0.0 copy-start
  4.8 0.0 copy-start.3
  4.8 15.3 %all_to_all.44 = bf16[8,56,128]{2,1,0:T(8,128)(2,1)S(1)} all-to-all(bf16[8,56,128]{2,1,0:T(8,128)(2,1)} %bitcast.26), channel_id=1, replica_groups={{0,4,8,12,16,20,24,28},{32,36,40,44,48,52,56,60},{64,68,72,76,80,84,88,..., dimensions={0} | all-to-all | bytes 229376 | tf_op jit(solution)/shard_map/all_to_all | solution.py:592
  20.1 0.0 copy-done.5
  20.1 0.0 copy-done
  20.1 0.0 copy-done.3
  20.1 0.1 shard_map.105
  20.2 10.0 %all_to_all.45 = bf16[8,56,128]{2,1,0:T(8,128)(2,1)S(1)} all-to-all(bf16[8,56,128]{2,1,0:T(8,128)(2,1)S(1)} %bitcast.22), channel_id=1, replica_groups={{0,32,64,96,128,160,192,224},{4,36,68,100,132,164,196,228},{8,40,72,104..., dimensions={0} | all-to-all | bytes 229376 | tf_op jit(solution)/shard_map/all_to_all | solution.py:592
  30.2 0.1 shard_map.106
  30.4 0.0 copy-start.1
  30.4 6.4 %shard_map.107 = (f32[2048,128]{1,0:T(8,128)}, f32[2048,128]{1,0:T(8,128)}, f32[96,128]{1,0:T(8,128)S(1)}) custom-call(s32[1]{0:T(128)} %bitcast.place, bf16[128,2048]{1,0:T(8,128)(2,1)} %query_hbm.3, bf16[128,2048]{1,0:T(8,128)(2,1)} %key_hbm.3, bf16[128,2048]{1,0:T(8,128)(2,1)} %value_hbm.3, bf16[128,2048]{1,0:T(8,128)(2,1)} %residual_hbm.3, ...), custom_call_target="tpu_custom_call" | custom-call | tf_op jit(solution)/shard_map/pallas_call | solution.py:612
  36.8 4.6 %collective-permute-start = (bf16[56,128]{1,0:T(8,128)(2,1)S(1)}, bf16[56,128]{1,0:T(8,128)(2,1)S(1)}, u32[]{:S(2)}, u32[]{:S(2)}) collective-permute-start(bf16[56,128]{1,0:T(8,128)(2,1)S(1)} %shard_map.106), channel_id=1, source_target_pairs={{0,256},{4,260},{8,264},{12,268},{16,272},{20,276},{24,280},{28,28... | collective-permute-start | bytes 43016 | tf_op jit(solution)/shard_map/ppermute | solution.py:635
  41.4 0.8 %collective-permute-done.ahead = bf16[56,128]{1,0:T(8,128)(2,1)S(1)} collective-permute-done((bf16[56,128]{1,0:T(8,128)(2,1)S(1)}, bf16[56,128]{1,0:T(8,128)(2,1)S(1)}, u32[]{:S(2)}, u32[]{:S(2)}) %collective-permute-start) | collective-permute-done | bytes 14368 | tf_op jit(solution)/shard_map/ppermute | solution.py:635
  42.2 0.0 copy-done.1
  42.2 0.8 %shard_map.108 = bf16[384,128]{1,0:T(8,128)(2,1)} custom-call(s32[1]{0:T(128)} %bitcast.place, bf16[448,128]{1,0:T(8,128)(2,1)S(1)} %bitcast.14, bf16[448,128]{1,0:T(8,128)(2,1)S(1)} %bitcast.16, bf16[56,128]{1,0:T(8,128)(2,1)S(1)} %collective-permute-done.ahead, f32[256,128]{1,0:T(8,128)S(1)} %get-tuple-element.29.prefix, f32[3,3,2048]{2,1,0:T(4,128)S(1)} %copy-done.3, ...), custom_call_target="tpu_custom_call" | custom-call | tf_op jit(solution)/shard_map/pallas_call | solution.py:637
  43.0 6.3 %all-to-all-start.2 = ((bf16[8,48,128]{2,1,0:T(8,128)(2,1)}), bf16[8,48,128]{2,1,0:T(8,128)(2,1)S(1)}, u32[]{:S(2)}, u32[]{:S(2)}) async-start(bf16[8,48,128]{2,1,0:T(8,128)(2,1)} %bitcast.6), calls=%async_computation.2 | async-start | bytes 196608 | tf_op jit(solution)/shard_map/all_to_all | solution.py:592
  49.4 0.0 copy-start.2
  49.4 0.0 copy-start.4
  49.4 0.3 shard_map.109
  49.6 4.7 %all-to-all-done.2 = bf16[8,48,128]{2,1,0:T(8,128)(2,1)S(1)} async-done(((bf16[8,48,128]{2,1,0:T(8,128)(2,1)}), bf16[8,48,128]{2,1,0:T(8,128)(2,1)S(1)}, u32[]{:S(2)}, u32[]{:S(2)}) %all-to-all-start.2) | async-done | bytes 98336 | tf_op jit(solution)/shard_map/all_to_all | solution.py:592
  54.4 0.0 copy-done.2
  54.4 0.0 copy-done.4
  54.4 3.2 %shard_map.110 = (bf16[128,2048]{1,0:T(8,128)(2,1)S(1)}, f32[4,128]{1,0:T(4,128)S(1)}) custom-call(s32[1]{0:T(128)} %bitcast.place, bf16[384,128]{1,0:T(8,128)(2,1)S(1)} %bitcast.17, f32[3,3,2048]{2,1,0:T(4,128)S(1)} %copy-done.3, f32[16,2048]{1,0:T(8,128)S(1)} %copy-done.2, f32[16,2048]{1,0:T(8,128)S(1)} %copy-done.4, f32[16,128]{1,0:T(8,128)S(1)} %bitcast.21, ...), custom_call_target="tpu_custom_call" | custom-call | tf_op jit(solution)/shard_map/pallas_call | solution.py:644
  57.6 0.0 copy-start.6
  57.6 8.5 %all_to_all.46 = f32[4,1,128]{2,1,0:T(1,128)S(1)} all-to-all(f32[4,1,128]{2,1,0:T(1,128)S(1)} %bitcast.25), channel_id=1, replica_groups=mesh['seq'=128,'chan'=4] {'chan'}, dimensions={0} | all-to-all | bytes 4096 | tf_op jit(solution)/shard_map/all_to_all | solution.py:675
  66.1 0.0 copy-done.6
  66.1 1.0 %shard_map.111 = (bf16[128,2048]{1,0:T(8,128)(2,1)}, bf16[128,2048]{1,0:T(8,128)(2,1)}) custom-call(bf16[128,2048]{1,0:T(8,128)(2,1)S(1)} %get-tuple-element.36.summed, f32[4,128]{1,0:T(4,128)S(1)} %bitcast.24, f32[16,128]{1,0:T(8,128)S(1)} %bitcast.23), custom_call_target="tpu_custom_call" | custom-call | tf_op jit(solution)/shard_map/pallas_call | solution.py:677
Async XLA Ops:
  0.6 19.5 %copy-start.5 = (f32[2048]{0:T(1024)S(1)}, f32[2048]{0:T(1024)}, u32[]{:S(2)}) copy-start(f32[2048]{0:T(1024)} %param.16) | copy-start | bytes 24580
  4.7 15.4 %copy-start = (f32[16,2048]{1,0:T(8,128)S(1)}, f32[16,2048]{1,0:T(8,128)}, u32[]{:S(2)}) copy-start(f32[16,2048]{1,0:T(8,128)} %decay.1) | copy-start | bytes 393220
  4.8 15.4 %copy-start.3 = (f32[3,3,2048]{2,1,0:T(4,128)S(1)}, f32[3,3,2048]{2,1,0:T(4,128)}, u32[]{:S(2)}) copy-start(f32[3,3,2048]{2,1,0:T(4,128)} %filters.7) | copy-start | bytes 221188
  30.4 11.9 %copy-start.1 = (f32[16,2048]{1,0:T(8,128)S(1)}, f32[16,2048]{1,0:T(8,128)}, u32[]{:S(2)}) copy-start(f32[16,2048]{1,0:T(8,128)} %decay.1) | copy-start | bytes 393220
  36.8 5.4 %collective-permute-start = (bf16[56,128]{1,0:T(8,128)(2,1)S(1)}, bf16[56,128]{1,0:T(8,128)(2,1)S(1)}, u32[]{:S(2)}, u32[]{:S(2)}) collective-permute-start(bf16[56,128]{1,0:T(8,128)(2,1)S(1)} %shard_map.106), channel_id=1, source_target_pairs={{0,256},{4,260},{8,264},{12,268},{16,272},{20,276},{24,280},{28,28... | collective-permute-start | bytes 43016 | tf_op jit(solution)/shard_map/ppermute | solution.py:635
  43.0 11.3 %all-to-all-start.2 = ((bf16[8,48,128]{2,1,0:T(8,128)(2,1)}), bf16[8,48,128]{2,1,0:T(8,128)(2,1)S(1)}, u32[]{:S(2)}, u32[]{:S(2)}) async-start(bf16[8,48,128]{2,1,0:T(8,128)(2,1)} %bitcast.6), calls=%async_computation.2 | async-start | bytes 196608 | tf_op jit(solution)/shard_map/all_to_all | solution.py:592
  49.4 5.0 %copy-start.2 = (f32[16,2048]{1,0:T(8,128)S(1)}, f32[16,2048]{1,0:T(8,128)}, u32[]{:S(2)}) copy-start(f32[16,2048]{1,0:T(8,128)} %decay.1) | copy-start | bytes 393220
  49.4 5.0 %copy-start.4 = (f32[16,2048]{1,0:T(8,128)S(1)}, f32[16,2048]{1,0:T(8,128)}, u32[]{:S(2)}) copy-start(f32[16,2048]{1,0:T(8,128)} %residue.1) | copy-start | bytes 393220
  57.6 8.5 %copy-start.6 = (f32[2048]{0:T(1024)S(1)}, f32[2048]{0:T(1024)}, u32[]{:S(2)}) copy-start(f32[2048]{0:T(1024)} %param.17) | copy-start | bytes 24580
